TPU v7x, 512 devices: a whole 4x8x8 slice. The times are simulated.
512 devices in a mesh: dp: 16 (over y, core), ctx: 32 (over z, x).
Axes of the slice: x: 4, y: 8, z: 8, core: 2. Of those that a mesh axis runs over, the one named last changes fastest.
Arguments:
- delta_query_rows: bfloat16 [16, 4096, 16, 128], P('dp', 'ctx'), may hold values from -6 to 6
- delta_key_rows: bfloat16 [16, 4096, 16, 128], P('dp', 'ctx'), may hold values from -6 to 6
- delta_value_rows: bfloat16 [16, 4096, 16, 128], P('dp', 'ctx'), may hold values from -6 to 6
- delta_write_strength: float32 [16, 4096, 16], P('dp', 'ctx'), may hold values from 0.2 to 1
- token_gate_scale: float32 [16, 4096, 16], P('dp', 'ctx'), may hold values from 0.5 to 2
- channel_decay_rate: float32 [16, 128], replicated, may hold values from 0.00390625 to 0.0625
- sudden_loss_mask: int32 [16, 4096], P('dp', 'ctx'), may hold values 0 or 1
- document_numbers: int32 [16, 4096], P('dp'), may hold values from 0 to 63, never falling along the last dimension, each value on 1 to 128 neighbouring positions
- delta_norm_gain: float32 [128], replicated, may hold values from 0.5 to 1.5
- delta_output_cotangent: bfloat16 [16, 4096, 16, 128], P('dp', 'ctx'), may hold values from -6 to 6
- latent_query_rows: bfloat16 [16, 4096, 16, 128], P('dp', 'ctx'), may hold values from -90 to 90
- compressed_latents: bfloat16 [16, 4096, 512], P('dp', 'ctx'), may hold values from -90 to 90
- query_to_latent_map: bfloat16 [16, 128, 512], P(None, 'ctx'), may hold values from -0.5 to 0.5
- latent_to_value_map: bfloat16 [16, 512, 128], P(None, 'ctx'), may hold values from -0.25 to 0.25
Outputs:
- kda_output: bfloat16 [16, 4096, 16, 128], P('dp', 'ctx')
- mla_output: bfloat16 [16, 4096, 16, 128], P('dp', 'ctx')
- gain_grad: float32 [128], replicated
Inputs may be any that keep to these rules, and one draw needn't show every extreme that they name: `document_numbers`: each row's document numbers never fall; every document has 1 to 128 tokens, and some document has exactly 128.
All inputs are finite; a program needn't handle non-finite values. No bound on the sum of `sudden_loss_mask` on one device may be relied on, other than what follows from the above.
Results may differ from a plain program's by a relative error of at most 0.0065.
The roundings to bfloat16 on the way count: a program that leaves them out, or rounds other values in their place, can miss the bound.
Values may be sent and summed in bfloat16 or wider, within the bound.
No kernel may reach another device: no remote copies, remote signals or barrier semaphores. Data moves between devices by JAX's collectives and lax.ppermute only.
A program may use at most 128 MiB of HBM per device.

v0:
```python
import math

import jax
import jax.numpy as jnp
from jax import lax
from jax.sharding import PartitionSpec as P

DOCBLK = 2
DN = 128


exact_mode = lax.Precision.HIGHEST


def from_behind(value, axis, steps):
    count = lax.axis_size(axis)
    leading, last = (max(0, -steps), min(count, count - steps))
    return lax.ppermute(value, axis, [(source, source + steps) for source in range(leading, last)])


def unit_norm(tensor):
    widened = tensor.astype(jnp.float32)
    return widened * lax.rsqrt(jnp.sum(widened * widened, axis=-1, keepdims=True) + 1e-06)


def block_maps(queries, keyset, values, writes, log_decay_values, docs, before):
    size = docs.shape[0]
    places = jnp.arange(size, dtype=jnp.int32)
    same_doc = docs[:, None] == docs[None, :]
    within = (same_doc & (places[:, None] >= places[None, :])).astype(jnp.float32)
    earlier = (same_doc & (places[:, None] > places[None, :])).astype(jnp.float32)
    cumlog = jnp.einsum("ts,shc->thc", within, log_decay_values, precision=exact_mode)
    key_decayed = keyset * jnp.exp(cumlog)
    key_grown = keyset * jnp.exp(-cumlog)
    query_decayed = queries * jnp.exp(cumlog)
    carried = (docs == before).astype(jnp.float32)
    pairwise = jnp.einsum("thc,shc->hts", key_decayed, key_grown, precision=exact_mode)
    triangle = pairwise * jnp.transpose(writes)[:, :, None] * earlier[None]
    targets = jnp.concatenate(
        [writes[:, :, None] * values, (writes * carried[:, None])[:, :, None] * key_decayed],
        axis=-1,
    )
    identity_mat = jnp.eye(size, dtype=jnp.float32)
    solved = jax.scipy.linalg.solve_triangular(
        identity_mat[None] + triangle,
        jnp.transpose(targets, (1, 0, 2)),
        lower=True,
        unit_diagonal=True,
    )
    value_width = values.shape[-1]
    from_values = solved[:, :, :value_width]
    from_state = solved[:, :, value_width:]
    weights_att = (
        jnp.einsum("thc,shc->hts", query_decayed, key_grown, precision=exact_mode) * within[None]
    )
    local_out = jnp.einsum("hts,hsv->thv", weights_att, from_values, precision=exact_mode)
    state_query = carried[:, None, None] * query_decayed - jnp.einsum(
        "hts,hsc->thc", weights_att, from_state, precision=exact_mode
    )
    closing = jnp.exp(cumlog[size - 1])
    tailing = (docs == docs[size - 1]).astype(jnp.float32)
    leaving = key_grown * closing[None] * tailing[:, None, None]
    key_width = keyset.shape[-1]
    transfer_map = (carried[size - 1] * closing)[:, :, None] * jnp.eye(
        key_width, dtype=jnp.float32
    )[None]
    transfer_map = transfer_map - jnp.einsum(
        "shc,hsd->hcd", leaving, from_state, precision=exact_mode
    )
    offset_map = jnp.einsum("shc,hsv->hcv", leaving, from_values, precision=exact_mode)
    return (local_out, state_query, transfer_map, offset_map)


def advance(transfer_map, offset_map, state):
    return jnp.einsum("shcd,shdv->shcv", transfer_map, state, precision=exact_mode) + offset_map


def shards(
    delta_query_rows,
    delta_key_rows,
    delta_value_rows,
    delta_write_strength,
    token_gate_scale,
    channel_decay_rate,
    sudden_loss_mask,
    document_numbers,
    delta_norm_gain,
    delta_output_cotangent,
    latent_query_rows,
    compressed_latents,
    query_to_latent_map,
    latent_to_value_map,
):
    ranks = lax.axis_size("ctx")
    place = lax.axis_index("ctx")
    seqs = delta_query_rows.shape[0]
    rows = delta_query_rows.shape[1]
    half = rows // 2
    heads = delta_query_rows.shape[2]
    key_width = delta_query_rows.shape[3]
    value_width = delta_value_rows.shape[3]
    second_block = 2 * ranks - 1 - place
    zero_index = jnp.zeros((), jnp.int32)

    def block_docs(block):
        start = block * half
        docs = lax.dynamic_slice_in_dim(document_numbers, start, half, 1)
        prior = lax.dynamic_slice_in_dim(document_numbers, jnp.maximum(start - 1, 0), 1, 1)[:, 0]
        return (docs, jnp.where(block > 0, prior, -1))

    docs_first, prior_first = block_docs(place)
    docs_second, prior_second = block_docs(second_block)
    docs_pair = jnp.stack([docs_first, docs_second], axis=1)
    prior_pair = jnp.stack([prior_first, prior_second], axis=1)

    def split_rows(tensor):
        return tensor.reshape((seqs, 2, half) + tensor.shape[2:])

    queries = split_rows(unit_norm(delta_query_rows))
    keyset = split_rows(unit_norm(delta_key_rows))
    values = split_rows(delta_value_rows.astype(jnp.float32))
    writes = split_rows(delta_write_strength)
    log_decay_values = split_rows(
        -channel_decay_rate[None, None] * token_gate_scale[..., None]
        + sudden_loss_mask.astype(jnp.float32)[:, :, None, None] * math.log(0.6)
    )
    local_out, state_query, transfer_map, offset_map = jax.vmap(jax.vmap(block_maps))(
        queries, keyset, values, writes, log_decay_values, docs_pair, prior_pair
    )
    zero_state = jnp.zeros((seqs, heads, key_width, value_width), jnp.float32)
    state_first = zero_state
    state_second = zero_state
    for repeat in range(DOCBLK):
        out_first = advance(transfer_map[:, 0], offset_map[:, 0], state_first)
        out_second = advance(transfer_map[:, 1], offset_map[:, 1], state_second)
        state_first = from_behind(out_first, "ctx", 1)
        from_above = from_behind(out_second, "ctx", -1)
        state_second = jnp.where(place == ranks - 1, out_first, from_above)
    states = jnp.stack([state_first, state_second], axis=1)
    kda_raw = local_out + jnp.einsum(
        "sbthc,sbhcv->sbthv", state_query, states, precision=exact_mode
    )
    kda_raw = kda_raw.reshape(seqs, rows, heads, value_width)
    meansq = jnp.mean(kda_raw * kda_raw, axis=-1, keepdims=True)
    normed = kda_raw * lax.rsqrt(meansq + 1e-06)
    kda_output = (normed * delta_norm_gain).astype(jnp.bfloat16)
    partial_grad = jnp.sum(normed * delta_output_cotangent.astype(jnp.float32), axis=(0, 1, 2))
    total_grad = lax.psum(partial_grad, ("dp", "ctx"))
    gain_grad = total_grad / math.sqrt(seqs * lax.axis_size("dp") * rows * ranks * heads)
    latent_width = compressed_latents.shape[2]
    neighbours = {0: compressed_latents}
    offsets = []
    for distance in range(1, DOCBLK + 1):
        offsets.append(distance)
        offsets.append(-distance)
    for offset in offsets:
        neighbours[offset] = from_behind(compressed_latents, "ctx", offset)
    stacked = jnp.stack([neighbours[offset] for offset in range(-DOCBLK, DOCBLK + 1)], axis=0)
    stacked = stacked.reshape(2 * DOCBLK + 1, seqs, 2, half, latent_width)
    lift_keys, lift_values = (
        lax.all_gather(query_to_latent_map, "ctx", axis=1, tiled=True),
        lax.all_gather(latent_to_value_map, "ctx", axis=1, tiled=True),
    )
    lifted = jnp.einsum(
        "sthn,hnl->sthl", latent_query_rows, lift_keys, preferred_element_type=jnp.float32
    ).astype(jnp.bfloat16)
    scale = 1.0 / math.sqrt(DN)
    halves_out = []
    for which in range(2):
        block = place if which == 0 else second_block
        key_parts = []
        doc_parts = []
        pos_parts = []
        for back in range(DOCBLK, -1, -1):
            source = block - back
            in_first = source < ranks
            owner = jnp.where(in_first, source, 2 * ranks - 1 - source)
            side = jnp.where(in_first, 0, 1).astype(jnp.int32)
            slot = jnp.clip(place - owner, -DOCBLK, DOCBLK) + DOCBLK
            piece = lax.dynamic_slice(
                stacked,
                (slot, zero_index, side, zero_index, zero_index),
                (1, seqs, 1, half, latent_width),
            )
            key_parts.append(piece.reshape(seqs, half, latent_width))
            source_docs = lax.dynamic_slice_in_dim(
                document_numbers, jnp.maximum(source, 0) * half, half, 1
            )
            doc_parts.append(jnp.where(source >= 0, source_docs, -1))
            pos_parts.append(source * half + jnp.arange(half, dtype=jnp.int32))
        key_rows = jnp.concatenate(key_parts, axis=1)
        key_docs = jnp.concatenate(doc_parts, axis=1)
        key_pos = jnp.concatenate(pos_parts, axis=0)
        query_docs = docs_pair[:, which]
        query_pos = block * half + jnp.arange(half, dtype=jnp.int32)
        block_query = lifted[:, which * half : (which + 1) * half]
        logits = (
            jnp.einsum("sthl,skl->shtk", block_query, key_rows, preferred_element_type=jnp.float32)
            * scale
        )
        allowed = (query_docs[:, None, :, None] == key_docs[:, None, None, :]) & (
            key_pos[None, None, None, :] <= query_pos[None, None, :, None]
        )
        logits = jnp.where(allowed, logits, -jnp.inf)
        peak = jnp.max(logits, axis=-1, keepdims=True)
        expo = jnp.exp(logits - peak)
        probs = (expo / jnp.sum(expo, axis=-1, keepdims=True)).astype(jnp.bfloat16)
        latent_mix = jnp.einsum(
            "shtk,skl->sthl", probs, key_rows, preferred_element_type=jnp.float32
        ).astype(jnp.bfloat16)
        halves_out.append(
            jnp.einsum(
                "sthl,hlv->sthv", latent_mix, lift_values, preferred_element_type=jnp.float32
            ).astype(jnp.bfloat16)
        )
    mla_output = jnp.concatenate(halves_out, axis=1)
    return (kda_output, mla_output, gain_grad)


def solution(mesh):
    placed = (
        P("dp", "ctx", None, None),
        P("dp", "ctx", None, None),
        P("dp", "ctx", None, None),
        P("dp", "ctx", None),
        P("dp", "ctx", None),
        P(),
        P("dp", "ctx"),
        P("dp", None),
        P(),
        P("dp", "ctx", None, None),
        P("dp", "ctx", None, None),
        P("dp", "ctx", None),
        P(None, "ctx", None),
        P(None, "ctx", None),
    )
    return jax.shard_map(
        shards,
        mesh=mesh,
        in_specs=placed,
        out_specs=(P("dp", "ctx", None, None), P("dp", "ctx", None, None), P()),
        check_vma=False,
    )
```

profile of v0, /device:TPU:1, one launch (start us, length us, event | category | flops | bytes accessed | tf_op | source)
XLA Modules:
  0.0 411.5 jit_solution(6213377689688391206)
XLA Ops:
  10.0 7.0 %collective-permute-start.7 = (bf16[1,128,512]{2,1,0:T(8,128)(2,1)}, bf16[1,128,512]{2,1,0:T(8,128)(2,1)S(1)}, u32[]{:S(2)}, u32[]{:S(2)}) collective-permute-start(bf16[1,128,512]{2,1,0:T(8,128)(2,1)} %param.25), channel_id=1, source_target_pairs={{0,2},{1,3},{2,4},{3,5},{4,6},{5,7},{6,8},{7,9},{8,10},{9,11},{10,... | collective-permute-start | bytes 393224 | tf_op jit(solution)/shard_map/ppermute | solution.py:18
  18.6 1.5 broadcast_select_fusion.5
  30.9 1.5 multiply_bitcast_fusion
  32.4 3.1 fusion.27
  35.4 158.9 %custom-call.4 = f32[1,2,16,1,64,64]{4,5,3,2,1,0:T(8,128)} custom-call(f32[1,2,16,1,64,64]{5,4,3,2,1,0:T(8,128)} %fusion.27), custom_call_target="InvertDiagBlocksLowerTriangular" | custom-call | tf_op jit(solution)/shard_map/vmap(vmap(jit(_solve_triangular)))/vmap()/triangular_solve | solution.py:44
  195.9 2.0 fusion.10
  198.0 3.6 convolution_bitcast_fusion
  201.6 4.0 subtract_bitcast_fusion
  205.6 2.0 fusion.20
  207.7 1.9 collective-permute-start.2
  209.6 2.0 fusion.22
  211.6 5.0 %collective-permute-start = (f32[1,16,128,128]{3,2,1,0:T(8,128)}, f32[1,16,128,128]{3,2,1,0:T(8,128)}, u32[]{:S(2)}, u32[]{:S(2)}) collective-permute-start(f32[1,16,128,128]{3,2,1,0:T(8,128)} %fusion.22), channel_id=1, source_target_pairs={{0,1},{1,2},{2,3},{3,4},{4,5},{5,6},{6,7},{7,8},{8,9},{9,10},{10,1... | collective-permute-start | bytes 3145736 | tf_op jit(solution)/shard_map/ppermute | solution.py:18
  217.6 2.1 convolution_multiply_fusion.2
  222.5 5.7 %collective-permute-done.2 = f32[1,16,128,128]{3,2,1,0:T(8,128)} collective-permute-done((f32[1,16,128,128]{3,2,1,0:T(8,128)}, f32[1,16,128,128]{3,2,1,0:T(8,128)}, u32[]{:S(2)}, u32[]{:S(2)}) %collective-permute-start.2) | collective-permute-done | bytes 1048608 | tf_op jit(solution)/shard_map/ppermute | solution.py:18
  228.2 3.5 fusion.19
  233.1 2.4 fusion.21
  235.5 5.8 %collective-permute-start.1 = (f32[1,16,128,128]{3,2,1,0:T(8,128)S(1)}, f32[1,16,128,128]{3,2,1,0:T(8,128)}, u32[]{:S(2)}, u32[]{:S(2)}) collective-permute-start(f32[1,16,128,128]{3,2,1,0:T(8,128)S(1)} %fusion.21), channel_id=1, source_target_pairs={{0,1},{1,2},{2,3},{3,4},{4,5},{5,6},{6,7},{7,8},{8,9},{9,10},{10,1... | collective-permute-start | bytes 3145736 | tf_op jit(solution)/shard_map/ppermute | solution.py:18
  242.0 5.8 %collective-permute-start.6 = (bf16[1,128,512]{2,1,0:T(8,128)(2,1)S(1)}, bf16[1,128,512]{2,1,0:T(8,128)(2,1)S(1)}, u32[]{:S(2)}, u32[]{:S(2)}) collective-permute-start(bf16[1,128,512]{2,1,0:T(8,128)(2,1)S(1)} %copy-done.12), channel_id=1, source_target_pairs={{0,1},{1,2},{2,3},{3,4},{4,5},{5,6},{6,7},{7,8},{8,9},{9,10},{10,1... | collective-permute-start | bytes 393224 | tf_op jit(solution)/shard_map/ppermute | solution.py:18
  248.8 11.5 %collective-permute-done.6 = bf16[1,128,512]{2,1,0:T(8,128)(2,1)S(1)} collective-permute-done((bf16[1,128,512]{2,1,0:T(8,128)(2,1)S(1)}, bf16[1,128,512]{2,1,0:T(8,128)(2,1)S(1)}, u32[]{:S(2)}, u32[]{:S(2)}) %collective-permute-start.6) | collective-permute-done | bytes 131104 | tf_op jit(solution)/shard_map/ppermute | solution.py:18
  261.8 3.3 multiply_reduce_fusion.1
  267.3 124.6 %psum.7 = f32[128]{0:T(128)S(1)} all-reduce(f32[128]{0:T(128)S(1)} %get-tuple-element.17), channel_id=1, replica_groups=mesh['dp'=16,'ctx'=32] {'dp','ctx'}, use_global_device_ids=true, to_apply=%region_8.9 | all-reduce | flops 128 | bytes 1024 | tf_op jit(solution)/shard_map/psum | solution.py:148
  392.4 4.2 %convert_bitcast_fusion = bf16[1,128,16,512]{3,1,2,0:T(8,128)(2,1)S(1)} fusion(bf16[16,128,512]{2,0,1:T(8,128)(2,1)} %all-gather.3.cloned.1.call-done, bf16[128,16,128]{2,1,0:T(8,128)(2,1)S(1)} %bitcast.248), kind=kOutput, calls=%fused_computation.10 | convolution fusion | flops 269484032 | bytes 4718592 | tf_op jit(solution)/shard_map/sthn,hnl->sthl/dot_general | solution.py:164
  398.5 2.4 fusion.34
  400.9 2.4 fusion.35
  (143 shorter events, 29.3 us)
Async XLA Ops:
  7.2 21.9 %copy-start.7 = (bf16[1,128,16,128]{3,2,1,0:T(8,128)(2,1)S(1)}, bf16[1,128,16,128]{3,2,1,0:T(8,128)(2,1)}, u32[]{:S(2)}) copy-start(bf16[1,128,16,128]{3,2,1,0:T(8,128)(2,1)} %param.15) | copy-start | bytes 1572868
  7.2 385.2 %all-gather.3.cloned.1.call-start = ((), (), s32[]{:S(2)}) async-start(), calls=%async_computation | async-start | bytes 2162688 | tf_op jit(solution)/shard_map/all_gather | solution.py:161
  7.2 241.6 %collective-permute-start.5 = (bf16[1,128,512]{2,1,0:T(8,128)(2,1)}, bf16[1,128,512]{2,1,0:T(8,128)(2,1)S(1)}, u32[]{:S(2)}, u32[]{:S(2)}) collective-permute-start(bf16[1,128,512]{2,1,0:T(8,128)(2,1)} %param.25), channel_id=1, source_target_pairs={{1,0},{2,1},{3,2},{4,3},{5,4},{6,5},{7,6},{8,7},{9,8},{10,9},{11,1... | collective-permute-start | bytes 393224 | tf_op jit(solution)/shard_map/ppermute | solution.py:18
  8.7 233.4 %collective-permute-start.4 = (bf16[1,128,512]{2,1,0:T(8,128)(2,1)}, bf16[1,128,512]{2,1,0:T(8,128)(2,1)}, u32[]{:S(2)}, u32[]{:S(2)}) collective-permute-start(bf16[1,128,512]{2,1,0:T(8,128)(2,1)} %param.25), channel_id=1, source_target_pairs={{2,0},{3,1},{4,2},{5,3},{6,4},{7,5},{8,6},{9,7},{10,8},{11,9},{12,... | collective-permute-start | bytes 393224 | tf_op jit(solution)/shard_map/ppermute | solution.py:18
  10.0 250.4 %collective-permute-start.7 = (bf16[1,128,512]{2,1,0:T(8,128)(2,1)}, bf16[1,128,512]{2,1,0:T(8,128)(2,1)S(1)}, u32[]{:S(2)}, u32[]{:S(2)}) collective-permute-start(bf16[1,128,512]{2,1,0:T(8,128)(2,1)} %param.25), channel_id=1, source_target_pairs={{0,2},{1,3},{2,4},{3,5},{4,6},{5,7},{6,8},{7,9},{8,10},{9,11},{10,... | collective-permute-start | bytes 393224 | tf_op jit(solution)/shard_map/ppermute | solution.py:18
  18.4 380.0 %all-gather.5.cloned.1.call-start = ((), (), s32[]{:S(2)}) async-start(), calls=%async_computation.1 | async-start | bytes 2162688 | tf_op jit(solution)/shard_map/all_gather | solution.py:162
  201.5 8.0 %copy-start.2 = (f32[1,2,16,128,128]{4,3,2,1,0:T(8,128)}, f32[1,2,16,128,128]{4,3,2,1,0:T(8,128)S(1)}, u32[]{:S(2)}) copy-start(f32[1,2,16,128,128]{4,3,2,1,0:T(8,128)S(1)} %convolution_bitcast_fusion) | copy-start | bytes 6291460
  207.6 9.0 %copy-start.8 = (bf16[1,128,16,128]{3,2,1,0:T(8,128)(2,1)S(1)}, bf16[1,128,16,128]{3,2,1,0:T(8,128)(2,1)}, u32[]{:S(2)}) copy-start(bf16[1,128,16,128]{3,2,1,0:T(8,128)(2,1)} %param.14) | copy-start | bytes 1572868
  207.6 9.8 %copy-start.22 = (s32[1,64]{1,0:T(1,128)S(1)}, s32[1,64]{1,0:T(1,128)}, u32[]{:S(2)}) copy-start(s32[1,64]{1,0:T(1,128)} %get-tuple-element.25) | copy-start | bytes 772
  207.6 9.8 %copy-start.23 = (s32[1,64]{1,0:T(1,128)S(1)}, s32[1,64]{1,0:T(1,128)}, u32[]{:S(2)}) copy-start(s32[1,64]{1,0:T(1,128)} %get-tuple-element.26) | copy-start | bytes 772
  207.6 9.8 %copy-start.24 = (s32[1,64]{1,0:T(1,128)S(1)}, s32[1,64]{1,0:T(1,128)}, u32[]{:S(2)}) copy-start(s32[1,64]{1,0:T(1,128)} %get-tuple-element.27) | copy-start | bytes 772
  207.6 9.8 %copy-start.25 = (s32[1,64]{1,0:T(1,128)S(1)}, s32[1,64]{1,0:T(1,128)}, u32[]{:S(2)}) copy-start(s32[1,64]{1,0:T(1,128)} %get-tuple-element.28) | copy-start | bytes 772
  207.6 9.8 %copy-start.26 = (s32[1,64]{1,0:T(1,128)S(1)}, s32[1,64]{1,0:T(1,128)}, u32[]{:S(2)}) copy-start(s32[1,64]{1,0:T(1,128)} %get-tuple-element.31) | copy-start | bytes 772
  207.7 9.8 %copy-start.27 = (s32[1,64]{1,0:T(1,128)S(1)}, s32[1,64]{1,0:T(1,128)}, u32[]{:S(2)}) copy-start(s32[1,64]{1,0:T(1,128)} %get-tuple-element.32) | copy-start | bytes 772
  207.7 20.5 %collective-permute-start.2 = (f32[1,16,128,128]{3,2,1,0:T(8,128)}, f32[1,16,128,128]{3,2,1,0:T(8,128)}, u32[]{:S(2)}, u32[]{:S(2)}) collective-permute-start(f32[1,16,128,128]{3,2,1,0:T(8,128)} %fusion.20), channel_id=1, source_target_pairs={{1,0},{2,1},{3,2},{4,3},{5,4},{6,5},{7,6},{8,7},{9,8},{10,9},{11,1... | collective-permute-start | bytes 3145736 | tf_op jit(solution)/shard_map/ppermute | solution.py:18
  211.6 21.5 %collective-permute-start = (f32[1,16,128,128]{3,2,1,0:T(8,128)}, f32[1,16,128,128]{3,2,1,0:T(8,128)}, u32[]{:S(2)}, u32[]{:S(2)}) collective-permute-start(f32[1,16,128,128]{3,2,1,0:T(8,128)} %fusion.22), channel_id=1, source_target_pairs={{0,1},{1,2},{2,3},{3,4},{4,5},{5,6},{6,7},{7,8},{8,9},{9,10},{10,1... | collective-permute-start | bytes 3145736 | tf_op jit(solution)/shard_map/ppermute | solution.py:18
  221.0 7.2 %copy-start.3 = (f32[1,2,16,128,128]{4,3,2,1,0:T(8,128)S(1)}, f32[1,2,16,128,128]{4,3,2,1,0:T(8,128)}, u32[]{:S(2)}) copy-start(f32[1,2,16,128,128]{4,3,2,1,0:T(8,128)} %copy-done.2) | copy-start | bytes 6291460
  231.7 9.7 %copy-start.16 = (s32[1,64]{1,0:T(1,128)S(1)}, s32[1,64]{1,0:T(1,128)}, u32[]{:S(2)}) copy-start(s32[1,64]{1,0:T(1,128)} %copy-done.15) | copy-start | bytes 772
  231.7 9.7 %copy-start.29 = (s32[64]{0:T(128)S(1)}, s32[64]{0:T(128)}, u32[]{:S(2)}) copy-start(s32[64]{0:T(128)} %copy-done.28) | copy-start | bytes 772
  231.7 10.4 %copy-start.12 = (bf16[1,128,512]{2,1,0:T(8,128)(2,1)S(1)}, bf16[1,128,512]{2,1,0:T(8,128)(2,1)}, u32[]{:S(2)}) copy-start(bf16[1,128,512]{2,1,0:T(8,128)(2,1)} %param.25) | copy-start | bytes 393220
  231.7 28.8 %collective-permute-start.3 = (f32[1,16,128,128]{3,2,1,0:T(8,128)}, f32[1,16,128,128]{3,2,1,0:T(8,128)}, u32[]{:S(2)}, u32[]{:S(2)}) collective-permute-start(f32[1,16,128,128]{3,2,1,0:T(8,128)} %fusion.19), channel_id=1, source_target_pairs={{1,0},{2,1},{3,2},{4,3},{5,4},{6,5},{7,6},{8,7},{9,8},{10,9},{11,1... | collective-permute-start | bytes 3145736 | tf_op jit(solution)/shard_map/ppermute | solution.py:18
  235.5 26.3 %collective-permute-start.1 = (f32[1,16,128,128]{3,2,1,0:T(8,128)S(1)}, f32[1,16,128,128]{3,2,1,0:T(8,128)}, u32[]{:S(2)}, u32[]{:S(2)}) collective-permute-start(f32[1,16,128,128]{3,2,1,0:T(8,128)S(1)} %fusion.21), channel_id=1, source_target_pairs={{0,1},{1,2},{2,3},{3,4},{4,5},{5,6},{6,7},{7,8},{8,9},{9,10},{10,1... | collective-permute-start | bytes 3145736 | tf_op jit(solution)/shard_map/ppermute | solution.py:18
  242.0 18.3 %collective-permute-start.6 = (bf16[1,128,512]{2,1,0:T(8,128)(2,1)S(1)}, bf16[1,128,512]{2,1,0:T(8,128)(2,1)S(1)}, u32[]{:S(2)}, u32[]{:S(2)}) collective-permute-start(bf16[1,128,512]{2,1,0:T(8,128)(2,1)S(1)} %copy-done.12), channel_id=1, source_target_pairs={{0,1},{1,2},{2,3},{3,4},{4,5},{5,6},{6,7},{7,8},{8,9},{9,10},{10,1... | collective-permute-start | bytes 393224 | tf_op jit(solution)/shard_map/ppermute | solution.py:18
  265.2 127.2 %copy-start.10 = (bf16[1,128,16,128]{3,2,1,0:T(8,128)(2,1)S(1)}, bf16[1,128,16,128]{3,2,1,0:T(8,128)(2,1)}, u32[]{:S(2)}) copy-start(bf16[1,128,16,128]{3,2,1,0:T(8,128)(2,1)} %param.24) | copy-start | bytes 1572868
  (18 other events, 58.5 us)
Sparse Core Ops, SparseCore 0:
  18.6 86.8 all-gather.2
  216.7 88.3 all-gather.4
where the time goes:
time: 417 us; the launch traced here: 411 us
  other arithmetic  174 us (42%)
  blocking collectives  125 us (30%)
  matrix products  41.3 us (10%)
  starting transfers between devices  29.7 us (7%)
  waiting for transfers between devices  17.3 us (4%)
  between operations  16.2 us (4%)
  local copies, waits for them, and re-layouts  8.72 us (2%)
    another operation x4, other arithmetic, block_maps(): jax.scipy.linalg.solve_triangular(identity_mat[None] + triangle, jnp.tran...  160 us
    psum x1, blocking collectives, shards(): total_grad = lax.psum(partial_grad, ('dp', 'ctx'))  125 us
    ppermute x8, starting transfers between devices, from_behind(): lax.ppermute(value, axis, [(source, source + steps) for source in range(l...  29.6 us
    ppermute x8, waiting for transfers between devices, from_behind(): lax.ppermute(value, axis, [(source, source + steps) for source in range(l...  17.3 us
    dot_general x4, matrix products, advance(): jnp.einsum('shcd,shdv->shcv', transfer_map, state, precision=exact_mode)  9.83 us
  transfers between devices with their start and end apart: 10, of which 2 were waited for; matrix products, arithmetic and copies ran while one was open for 53% of the time, Pallas kernels for 0%

commit v1 on v0

v1 whole, which is shorter than its diff:
```python
import functools
import math

import jax
import jax.numpy as jnp
from jax import lax
from jax.experimental import pallas as pl
from jax.experimental.pallas import tpu as pltpu
from jax.sharding import PartitionSpec as P

DN = 128
XS = 4
HALF = 64
F32 = jnp.float32
BF = jnp.bfloat16
LOSS = math.log(0.6)


def mm(a, b):
    return lax.dot_general(a, b, (((1,), (0,)), ((), ())), preferred_element_type=F32)


def mm_nt(a, b):
    return lax.dot_general(a, b, (((1,), (1,)), ((), ())), preferred_element_type=F32)


def mm_tn(a, b):
    return lax.dot_general(a, b, (((0,), (0,)), ((), ())), preferred_element_type=F32)


def iota2(shape, dim):
    return lax.broadcasted_iota(jnp.int32, shape, dim)


def docs_row(docs_ref, block):
    row = docs_ref[pl.ds(block // 2, 1), :].astype(F32)
    odd = jnp.full((1, HALF), block % 2, jnp.int32)
    return jnp.where(odd == 1, row[:, HALF:], row[:, :HALF])


def as_column(row):
    size = row.shape[1]
    eye = iota2((size, size), 0) == iota2((size, size), 1)
    return jnp.sum(jnp.where(eye, jnp.broadcast_to(row, (size, size)), 0.0), axis=1, keepdims=True)


def kda_pairs_kernel(
    place_ref, q_ref, k_ref, v_ref, w_ref, scale_ref, rate_ref, mask_ref, docs_ref,
    lmat, att, rhs, leaving, closing, carried_q,
    qn, kn, vn, acol, wcol, bcol, ccol, tcol, incl, excl,
):
    heads = rate_ref.shape[0]
    place = place_ref[0]
    ranks = docs_ref.shape[0]
    rows = HALF * heads

    def widen(c, _):
        at = pl.ds(pl.multiple_of(c * 256, 256), 256)
        for source, target in ((q_ref, qn), (k_ref, kn)):
            x = source[at, :].astype(F32)
            target[at, :] = x * lax.rsqrt(jnp.sum(x * x, axis=1, keepdims=True) + 1e-06)
        vn[at, :] = v_ref[at, :].astype(F32)
        return 0

    lax.fori_loop(0, 2 * rows // 256, widen, 0)
    ti, si = iota2((HALF, HALF), 0), iota2((HALF, HALF), 1)
    for i in range(2):
        block = place if i == 0 else 2 * ranks - 1 - place
        drow = docs_row(docs_ref, block)
        prior = docs_row(docs_ref, jnp.maximum(block - 1, 0))[:, HALF - 1 :]
        prior = jnp.where(jnp.full((1, 1), block, jnp.int32) > 0, prior, -1.0)
        dcol = as_column(drow)
        same = dcol == drow
        within = jnp.where(same & (ti >= si), 1.0, 0.0)
        incl[i] = within
        excl[i] = jnp.where(same & (ti > si), 1.0, 0.0)
        gates = lax.dot_general(
            within, scale_ref[i * HALF : (i + 1) * HALF, :], (((1,), (0,)), ((), ())),
            precision=lax.Precision.HIGHEST, preferred_element_type=F32,
        )
        lost = mask_ref[:, i * HALF : (i + 1) * HALF].astype(F32)
        bcol[i] = jnp.broadcast_to(jnp.sum(within * lost, axis=1, keepdims=True) * LOSS, (HALF, DN))
        ccol[i] = jnp.broadcast_to(jnp.where(dcol == prior, 1.0, 0.0), (HALF, DN))
        tcol[i] = jnp.broadcast_to(jnp.where(dcol == drow[:, HALF - 1 :], 1.0, 0.0), (HALF, DN))
        writes = w_ref[i * HALF : (i + 1) * HALF, :]
        for h in range(heads):
            acol[i * heads + h] = jnp.broadcast_to(gates[:, h : h + 1], (HALF, DN))
            wcol[i * heads + h] = jnp.broadcast_to(writes[:, h : h + 1], (HALF, DN))

    def pairs(g, _):
        for u in range(4):
            p = g * 4 + u
            i = p // heads
            h = p % heads
            at = pl.ds(i * rows + h, HALF, stride=heads)
            q, k, v = qn[at, :], kn[at, :], vn[at, :]
            w = wcol[p]
            carried = ccol[i]
            cumlog = bcol[i] - acol[p] * rate_ref[pl.ds(h, 1), :]
            grow = jnp.exp(cumlog)
            kd, qd = k * grow, q * grow
            kg = k * jnp.exp(-cumlog)
            both = jnp.concatenate([kd, qd], axis=0)
            both_hi, kg_hi = both.astype(BF), kg.astype(BF)
            both_lo = (both - both_hi.astype(F32)).astype(BF)
            kg_lo = (kg - kg_hi.astype(F32)).astype(BF)
            inner = mm_nt(both_hi, kg_hi) + mm_nt(both_hi, kg_lo) + mm_nt(both_lo, kg_hi)
            lmat[p] = inner[:HALF] * w[:, :HALF] * excl[i]
            att[p] = (inner[HALF:] * incl[i]).astype(BF)
            rhs[p, :, :DN] = (w * v).astype(BF)
            rhs[p, :, DN:] = (w * carried * kd).astype(BF)
            carried_q[p] = (carried * qd).astype(BF)
            last = grow[HALF - 1 :, :]
            leaving[p] = (kg * last * tcol[i]).astype(BF)
            closing[p] = jnp.broadcast_to(carried[HALF - 1 :, :] * last, (8, DN))
        return 0

    lax.fori_loop(0, 2 * heads // 4, pairs, 0)


def kda_pairs(place, q, k, v, w, scale, rate, mask, docs):
    heads = rate.shape[0]
    n = 2 * heads
    rows = q.shape[0]
    vm = lambda *s: pltpu.VMEM(s, F32)
    spec = pl.BlockSpec(memory_space=pltpu.VMEM)
    shapes = (
        jax.ShapeDtypeStruct((n, HALF, HALF), F32),
        jax.ShapeDtypeStruct((n, HALF, HALF), BF),
        jax.ShapeDtypeStruct((n, HALF, 2 * DN), BF),
        jax.ShapeDtypeStruct((n, HALF, DN), BF),
        jax.ShapeDtypeStruct((n, 8, DN), F32),
        jax.ShapeDtypeStruct((n, HALF, DN), BF),
    )
    return pl.pallas_call(
        kda_pairs_kernel,
        name="kda_pairs",
        out_shape=shapes,
        in_specs=[pl.BlockSpec(memory_space=pltpu.SMEM)] + [spec] * 8,
        out_specs=(spec,) * 6,
        scratch_shapes=[
            vm(rows, DN), vm(rows, DN), vm(rows, DN),
            vm(n, HALF, DN), vm(n, HALF, DN),
            vm(2, HALF, DN), vm(2, HALF, DN), vm(2, HALF, DN),
            vm(2, HALF, HALF), vm(2, HALF, HALF),
        ],
        compiler_params=pltpu.CompilerParams(vmem_limit_bytes=32 << 20),
        cost_estimate=pl.CostEstimate(flops=300_000_000, bytes_accessed=12_000_000, transcendentals=600_000),
    )(place, q, k, v, w, scale, rate, mask, docs)


def kda_invert_kernel(lmat, xmat):
    heads = lmat.shape[0] // 2
    ti, si = iota2((HALF, HALF), 0), iota2((HALF, HALF), 1)

    def base(g, _):
        for u in range(2):
            p = g * 2 + u
            lower = lmat[p]
            for b in range(HALF // 16):
                x = jnp.where(iota2((16, HALF), 0) + 16 * b == iota2((16, HALF), 1), 1.0, 0.0)
                part = lower[16 * b : 16 * b + 16, :]
                for j in range(15):
                    x = x - part[:, 16 * b + j : 16 * b + j + 1] * x[j : j + 1, :]
                xmat[p, 16 * b : 16 * b + 16, :] = x
        return 0

    lax.fori_loop(0, heads, base, 0)

    def merge(width, g, _):
        tb, sb = ti // width, si // width
        cross = ((tb % 2) == 1) & (sb == tb - 1)
        for u in range(8):
            p = g * 8 + u
            x = xmat[p]
            xb = x.astype(BF)
            y = mm(jnp.where(cross, lmat[p], 0.0).astype(BF), xb)
            xmat[p] = x - mm(xb, y.astype(BF))
        return 0

    lax.fori_loop(0, heads // 4, functools.partial(merge, 16), 0)
    lax.fori_loop(0, heads // 4, functools.partial(merge, 32), 0)


def kda_invert(lmat):
    spec = pl.BlockSpec(memory_space=pltpu.VMEM)
    return pl.pallas_call(
        kda_invert_kernel,
        name="kda_invert",
        out_shape=jax.ShapeDtypeStruct(lmat.shape, F32),
        in_specs=[spec],
        out_specs=spec,
        compiler_params=pltpu.CompilerParams(vmem_limit_bytes=16 << 20),
        cost_estimate=pl.CostEstimate(flops=300_000_000, bytes_accessed=12_000_000, transcendentals=0),
    )(lmat)


def kda_leave_kernel(xmat, rhs, leaving, closing, lat_ref, offs_first, offs_second, tmap, upd):
    heads = xmat.shape[0] // 2
    base_row = heads * DN
    for lb in range(4):
        part = lat_ref[:, lb * DN : (lb + 1) * DN]
        low = base_row + lb * HALF
        offs_first[low : low + HALF, :] = part[:HALF]
        offs_second[low : low + HALF, :] = part[:HALF]
        offs_second[low + 4 * HALF : low + 5 * HALF, :] = part[HALF:]

    def solve(g, _):
        for u in range(8):
            p = g * 8 + u
            upd[p] = mm(xmat[p].astype(BF), rhs[p]).astype(BF)
        return 0

    lax.fori_loop(0, heads // 4, solve, 0)

    eye = iota2((DN, DN), 0) == iota2((DN, DN), 1)
    for i, target in ((0, offs_first), (1, offs_second)):

        def leave(g, _, i=i, target=target):
            for u in range(4):
                h = g * 4 + u
                p = i * heads + h
                made = mm_tn(leaving[p], upd[p])
                target[pl.ds(pl.multiple_of(h * DN, DN), DN), :] = made[:, :DN].astype(BF)
                keep = jnp.where(eye, jnp.broadcast_to(closing[p][:1, :], (DN, DN)), 0.0)
                tmap[p] = (keep - made[:, DN:]).astype(BF)
            return 0

        lax.fori_loop(0, heads // 4, leave, 0)


def kda_leave(xmat, rhs, leaving, closing, latents):
    n = xmat.shape[0]
    spec = pl.BlockSpec(memory_space=pltpu.VMEM)
    shapes = (
        jax.ShapeDtypeStruct((n // 2 * DN + 4 * HALF, DN), BF),
        jax.ShapeDtypeStruct((n // 2 * DN + 8 * HALF, DN), BF),
        jax.ShapeDtypeStruct((n, DN, DN), BF),
        jax.ShapeDtypeStruct((n, HALF, 2 * DN), BF),
    )
    return pl.pallas_call(
        kda_leave_kernel,
        name="kda_leave",
        out_shape=shapes,
        in_specs=[spec] * 5,
        out_specs=(spec,) * 4,
        compiler_params=pltpu.CompilerParams(vmem_limit_bytes=24 << 20),
        cost_estimate=pl.CostEstimate(flops=300_000_000, bytes_accessed=8_000_000, transcendentals=0),
    )(xmat, rhs, leaving, closing, latents)


def kda_local_kernel(att, upd, carried_q, local, squery):
    n = att.shape[0]

    def body(g, _):
        for u in range(8):
            p = g * 8 + u
            made = mm(att[p], upd[p])
            local[p] = made[:, :DN]
            squery[p] = (carried_q[p].astype(F32) - made[:, DN:]).astype(BF)
        return 0

    lax.fori_loop(0, n // 8, body, 0)


def kda_local(att, upd, carried_q):
    n = att.shape[0]
    spec = pl.BlockSpec(memory_space=pltpu.VMEM)
    return pl.pallas_call(
        kda_local_kernel,
        name="kda_local",
        out_shape=(jax.ShapeDtypeStruct((n, HALF, DN), F32), jax.ShapeDtypeStruct((n, HALF, DN), BF)),
        in_specs=[spec] * 3,
        out_specs=(spec,) * 2,
        cost_estimate=pl.CostEstimate(flops=70_000_000, bytes_accessed=4_000_000, transcendentals=0),
    )(att, upd, carried_q)


def kda_carry_kernel(place_ref, tmap, offs_first, offs_second, in_first, in_second, out_first, out_second, *, ranks):
    heads = tmap.shape[0] // 2
    end = jnp.full((DN, DN), place_ref[0], jnp.int32) == ranks - 1
    low = heads * DN
    out_first[low:, :] = in_first[low:, :]
    out_second[low:, :] = in_second[low + 4 * HALF :, :]

    def body(g, _):
        for u in range(4):
            h = g * 4 + u
            at = pl.ds(pl.multiple_of(h * DN, DN), DN)
            own = offs_first[at, :].astype(F32)
            out_first[at, :] = (own + mm(tmap[h], in_first[at, :])).astype(BF)
            upper = jnp.where(end, own, in_second[at, :].astype(F32)).astype(BF)
            out_second[at, :] = (
                offs_second[at, :].astype(F32) + mm(tmap[heads + h], upper)
            ).astype(BF)
        return 0

    lax.fori_loop(0, heads // 4, body, 0)


def kda_carry(place, tmap, offs_first, offs_second, in_first, in_second, ranks):
    spec = pl.BlockSpec(memory_space=pltpu.VMEM)
    shape = jax.ShapeDtypeStruct(offs_first.shape, BF)
    return pl.pallas_call(
        functools.partial(kda_carry_kernel, ranks=ranks),
        name="kda_carry",
        out_shape=(shape, shape),
        in_specs=[pl.BlockSpec(memory_space=pltpu.SMEM)] + [spec] * 5,
        out_specs=(spec, spec),
        cost_estimate=pl.CostEstimate(flops=130_000_000, bytes_accessed=5_000_000, transcendentals=0),
    )(place, tmap, offs_first, offs_second, in_first, in_second)


def kda_close_kernel(place_ref, local, squery, own_first, in_first, in_second, gain, cot_ref, out_ref, grad_ref, cot, outs, *, ranks):
    heads = local.shape[0] // 2
    rows = HALF * heads
    end = jnp.full((DN, DN), place_ref[0], jnp.int32) == ranks - 1

    def widen(c, _):
        at = pl.ds(pl.multiple_of(c * 256, 256), 256)
        cot[at, :] = cot_ref[at, :].astype(F32)
        return 0

    lax.fori_loop(0, 2 * rows // 256, widen, 0)

    def body(g, grad):
        for u in range(4):
            h = g * 4 + u
            state_at = pl.ds(pl.multiple_of(h * DN, DN), DN)
            upper = jnp.where(
                end, own_first[state_at, :].astype(F32), in_second[state_at, :].astype(F32)
            ).astype(BF)
            for i, state in ((0, in_first[state_at, :]), (1, upper)):
                p = i * heads + h
                raw = local[p] + mm(squery[p], state)
                normed = raw * lax.rsqrt(jnp.mean(raw * raw, axis=1, keepdims=True) + 1e-06)
                at = pl.ds(i * rows + h, HALF, stride=heads)
                outs[at, :] = normed * gain[...]
                terms = normed * cot[at, :]
                grad = grad + jnp.sum(terms.reshape(HALF // 8, 8, DN), axis=0)
        return grad

    grad = lax.fori_loop(0, heads // 4, body, jnp.zeros((8, DN), F32))
    grad_ref[...] = jnp.broadcast_to(jnp.sum(grad, axis=0, keepdims=True), grad_ref.shape)

    def narrow(c, _):
        at = pl.ds(pl.multiple_of(c * 256, 256), 256)
        out_ref[at, :] = outs[at, :].astype(BF)
        return 0

    lax.fori_loop(0, 2 * rows // 256, narrow, 0)


def kda_close(place, local, squery, own_first, in_first, in_second, gain, cot, ranks):
    spec = pl.BlockSpec(memory_space=pltpu.VMEM)
    rows = cot.shape[0]
    return pl.pallas_call(
        functools.partial(kda_close_kernel, ranks=ranks),
        name="kda_close",
        out_shape=(jax.ShapeDtypeStruct((rows, DN), BF), jax.ShapeDtypeStruct((ranks, DN), F32)),
        in_specs=[pl.BlockSpec(memory_space=pltpu.SMEM)] + [spec] * 7,
        out_specs=(spec, spec),
        scratch_shapes=[pltpu.VMEM((rows, DN), F32), pltpu.VMEM((rows, DN), F32)],
        compiler_params=pltpu.CompilerParams(vmem_limit_bytes=32 << 20),
        cost_estimate=pl.CostEstimate(flops=70_000_000, bytes_accessed=5_000_000, transcendentals=4096),
    )(place, local, squery, own_first, in_first, in_second, gain, cot)


def onehot(shape, source):
    return jnp.where(iota2(shape, 0) == source(iota2(shape, 1)), 1.0, 0.0).astype(BF)


def mla_kernel(
    spot_ref, q_ref, lat_ref, back_one, ahead_one, back_two, ahead_two, docs_ref, own_w, other_w, out_ref,
    qp, keys, keysp, mask, lifted, mixed, outs, *, xs,
):
    ranks = docs_ref.shape[0]
    place, core = spot_ref[0], spot_ref[1]
    heads = q_ref.shape[0] // (2 * HALF)
    here_z, here_x = place // xs, place % xs
    width = keys.shape[1]

    def piece(ref, at, i, slot):
        for lb in range(4):
            keys[i, slot * HALF : (slot + 1) * HALF, lb * DN : (lb + 1) * DN] = ref[
                at + lb * HALF : at + (lb + 1) * HALF, :
            ]

    keys[0, 3 * HALF :, :] = jnp.zeros((width - 3 * HALF, 4 * DN), BF)
    keys[1, 3 * HALF :, :] = jnp.zeros((width - 3 * HALF, 4 * DN), BF)
    low = heads * DN
    piece(back_two, low, 0, 0)
    piece(back_one, low, 0, 1)
    keys[0, 2 * HALF : 3 * HALF, :] = lat_ref[:HALF, :]
    keys[1, 2 * HALF : 3 * HALF, :] = lat_ref[HALF:, :]

    @pl.when(place < ranks - 2)
    def _():
        piece(ahead_two, low, 1, 0)

    @pl.when(place == ranks - 2)
    def _():
        piece(ahead_one, low, 1, 0)

    @pl.when(place == ranks - 1)
    def _():
        piece(back_one, low, 1, 0)
        keys[1, HALF : 2 * HALF, :] = lat_ref[:HALF, :]

    @pl.when(place < ranks - 1)
    def _():
        piece(ahead_one, low + 4 * HALF, 1, 1)

    def source_n(k):
        off = ((k // 4) % 2) * 4 + ((k // 8) % 2) * 2 + (k // 16) % 2
        z = lax.bitwise_xor(off, jnp.full(k.shape, here_z, jnp.int32))
        return (z * xs + (k // 32 + here_x) % xs) * 4 + k % 4

    def source_l(k):
        off = ((k // 16) % 2) * 4 + ((k // 32) % 2) * 2 + (k // 64) % 2
        z = lax.bitwise_xor(off, jnp.full(k.shape, here_z, jnp.int32))
        return (z * xs + (k // 128 + here_x) % xs) * 16 + k % 16

    pick = onehot((DN, DN), source_n)
    rows = 256

    def place_q(c, _):
        at = pl.ds(pl.multiple_of(c * rows, rows), rows)
        qp[at, :] = mm(q_ref[at, :], pick)
        return 0

    lax.fori_loop(0, q_ref.shape[0] // rows, place_q, 0)
    spread = onehot((4 * DN, 4 * DN), source_l)
    ti, si = iota2((HALF, HALF), 0), iota2((HALF, HALF), 1)
    for i in range(2):
        keysp[i] = mm(keys[i], spread).astype(BF)
        block = place if i == 0 else 2 * ranks - 1 - place
        drow = docs_row(docs_ref, block)
        dcol = as_column(drow)
        for back in range(3):
            source = block - back
            krow = docs_row(docs_ref, jnp.maximum(source, 0))
            krow = jnp.where(jnp.full((1, HALF), source, jnp.int32) >= 0, krow, -1.0)
            allowed = dcol == krow
            if back == 0:
                allowed = allowed & (ti >= si)
            fill = jnp.where(allowed, 0.0, -1e30)
            for r in range(4):
                mask[i, r * HALF : (r + 1) * HALF, (2 - back) * HALF : (3 - back) * HALF] = fill
        mask[i, :, 3 * HALF :] = jnp.full((4 * HALF, width - 3 * HALF), -1e30, F32)

    span = heads // 2
    for side, weights in ((0, own_w), (1, other_w)):
        first = span * core if side == 0 else span * (1 - core)

        def lift(g, _, weights=weights, first=first):
            for u in range(2):
                hl = g * 2 + u
                h = first + hl
                q = qp[pl.ds(h, 2 * HALF, stride=heads), :].astype(BF)
                for lb in range(4):
                    at = pl.ds(pl.multiple_of((hl * 4 + lb) * 16, 16), 16)
                    w = jnp.concatenate(
                        [weights[xr, e, at, :] for xr in range(4) for e in range(2)], axis=0
                    )
                    made = mm(q, w).astype(BF)
                    for i in range(2):
                        dst = pl.ds(pl.multiple_of(h * HALF, HALF), HALF)
                        lifted[i, dst, lb * DN : (lb + 1) * DN] = made[i * HALF : (i + 1) * HALF]
            return 0

        lax.fori_loop(0, span // 2, lift, 0)

    scale = 1.0 / math.sqrt(DN)

    def attend(g, _):
        i = g // (heads // 4)
        at = pl.ds(pl.multiple_of((g % (heads // 4)) * rows, rows), rows)
        logits = mm_nt(lifted[i, at, :], keys[i]) * scale + mask[i]
        peak = jnp.max(logits, axis=1, keepdims=True)
        expo = jnp.exp(logits - peak)
        probs = (expo / jnp.sum(expo, axis=1, keepdims=True)).astype(BF)
        mixed[i, at, :] = mm(probs, keysp[i]).astype(BF)
        return 0

    lax.fori_loop(0, heads // 2, attend, 0)

    for side, weights in ((0, own_w), (1, other_w)):
        first = span * core if side == 0 else span * (1 - core)

        def lower(g, _, weights=weights, first=first):
            for u in range(2):
                hl = g * 2 + u
                h = first + hl
                w = jnp.concatenate(
                    [
                        weights[xr, e, pl.ds(pl.multiple_of(512 + (zr * span + hl) * 16, 16), 16), :]
                        for xr in range(4) for e in range(2) for zr in range(4)
                    ],
                    axis=0,
                )
                src = pl.ds(pl.multiple_of(h * HALF, HALF), HALF)
                both = jnp.concatenate([mixed[0, src, :], mixed[1, src, :]], axis=0)
                outs[pl.ds(h, 2 * HALF, stride=heads), :] = mm(both, w)
            return 0

        lax.fori_loop(0, span // 2, lower, 0)

    def narrow(c, _):
        at = pl.ds(pl.multiple_of(c * rows, rows), rows)
        out_ref[at, :] = outs[at, :].astype(BF)
        return 0

    lax.fori_loop(0, q_ref.shape[0] // rows, narrow, 0)


def mla(spot, q, latents, back_one, ahead_one, back_two, ahead_two, docs, own_w, other_w, xs):
    spec = pl.BlockSpec(memory_space=pltpu.VMEM)
    rows = q.shape[0]
    return pl.pallas_call(
        functools.partial(mla_kernel, xs=xs),
        name="mla",
        out_shape=jax.ShapeDtypeStruct((rows, DN), BF),
        in_specs=[pl.BlockSpec(memory_space=pltpu.SMEM)] + [spec] * 9,
        out_specs=spec,
        scratch_shapes=[
            pltpu.VMEM((rows, DN), F32),
            pltpu.VMEM((2, 256, 4 * DN), BF),
            pltpu.VMEM((2, 256, 4 * DN), BF),
            pltpu.VMEM((2, 256, 256), F32),
            pltpu.VMEM((2, rows // 2, 4 * DN), BF),
            pltpu.VMEM((2, rows // 2, 4 * DN), BF),
            pltpu.VMEM((rows, DN), F32),
        ],
        compiler_params=pltpu.CompilerParams(vmem_limit_bytes=40 << 20),
        cost_estimate=pl.CostEstimate(flops=1_500_000_000, bytes_accessed=7_000_000, transcendentals=600_000),
    )(spot, q, latents, back_one, ahead_one, back_two, ahead_two, docs, own_w, other_w)


def from_behind(value, axis, steps):
    count = lax.axis_size(axis)
    leading, last = (max(0, -steps), min(count, count - steps))
    return lax.ppermute(value, axis, [(source, source + steps) for source in range(leading, last)])


def shards(
    delta_query_rows,
    delta_key_rows,
    delta_value_rows,
    delta_write_strength,
    token_gate_scale,
    channel_decay_rate,
    sudden_loss_mask,
    document_numbers,
    delta_norm_gain,
    delta_output_cotangent,
    latent_query_rows,
    compressed_latents,
    query_to_latent_map,
    latent_to_value_map,
):
    ranks = lax.axis_size("ctx")
    place = lax.axis_index("ctx")
    seqs = delta_query_rows.shape[0]
    rows = delta_query_rows.shape[1]
    heads = delta_query_rows.shape[2]
    value_width = delta_value_rows.shape[3]
    here = place.astype(jnp.int32).reshape(1)
    docs = document_numbers.reshape(ranks, rows)
    latents = compressed_latents[0]
    flat = lambda tensor: tensor.reshape(rows * heads, tensor.shape[3])

    groups = lax.axis_size("dp")
    member = lax.axis_index("dp")
    core = member % 2
    span = heads // 2
    keep_lift = lax.dynamic_slice_in_dim(query_to_latent_map, core * span, span, 0)
    keep_lower = lax.dynamic_slice_in_dim(latent_to_value_map, core * span, span, 0)
    lift_rows = keep_lift.reshape(span, 4, 4, DN).transpose(0, 2, 1, 3).reshape(span * 16, DN)
    held = jnp.concatenate([lift_rows, keep_lower.reshape(span * 16, DN)], axis=0)

    def across(value, step):
        return lax.ppermute(value, "ctx", [(i, i ^ step) for i in range(ranks)])

    held = jnp.stack([held, across(held, 4 * XS)])
    held = jnp.stack([held, across(held, 2 * XS)])
    lift_tiles = held[:, :, : span * 16].reshape(2, 2, span, 4, 4, DN)
    lift_tiles = lift_tiles.transpose(2, 3, 0, 1, 4, 5).reshape(span * 64, DN)
    held = jnp.concatenate([lift_tiles, held[:, :, span * 16 :].reshape(span * 64, DN)], axis=0)
    held = jnp.stack([held, across(held, XS)])

    lmat, att, rhs, leaving, closing, carried_q = kda_pairs(
        here,
        flat(delta_query_rows),
        flat(delta_key_rows),
        flat(delta_value_rows),
        delta_write_strength[0],
        token_gate_scale[0],
        channel_decay_rate,
        sudden_loss_mask,
        docs,
    )
    xmat = kda_invert(lmat)
    offs_first, offs_second, tmap, upd = kda_leave(xmat, rhs, leaving, closing, latents)
    near_first = from_behind(offs_first, "ctx", 1)
    near_second = from_behind(offs_second, "ctx", -1)
    columns = [held]
    for step in range(1, XS):
        pairs = [(i - i % XS + (i + step) % XS, i) for i in range(ranks)]
        columns.append(lax.ppermute(held, "ctx", pairs))
    own_w = jnp.stack(columns)
    other_w = lax.ppermute(own_w, "dp", [(i, i ^ 1) for i in range(groups)])

    local, squery = kda_local(att, upd, carried_q)
    out_first, out_second = kda_carry(
        here, tmap, offs_first, offs_second, near_first, near_second, ranks
    )
    far_first = from_behind(out_first, "ctx", 1)
    far_second = from_behind(out_second, "ctx", -1)
    normed_rows, partial_grad = kda_close(
        here,
        local,
        squery,
        out_first,
        far_first,
        far_second,
        delta_norm_gain.reshape(1, value_width),
        flat(delta_output_cotangent),
        ranks,
    )
    kda_output = normed_rows.reshape(seqs, rows, heads, value_width)
    along = jnp.sum(lax.all_to_all(partial_grad, "ctx", 0, 0, tiled=True), axis=0)
    spread = jnp.broadcast_to(along, (groups, value_width))
    total_grad = jnp.sum(lax.all_to_all(spread, "dp", 0, 0, tiled=True), axis=0)
    gain_grad = total_grad / math.sqrt(seqs * groups * rows * ranks * heads)

    spot = jnp.stack([place, core]).astype(jnp.int32)
    mla_rows = mla(
        spot,
        flat(latent_query_rows),
        latents,
        near_first,
        near_second,
        far_first,
        far_second,
        docs,
        own_w,
        other_w,
        XS,
    )
    mla_output = mla_rows.reshape(seqs, rows, heads, DN)
    return (kda_output, mla_output, gain_grad)


def solution(mesh):
    placed = (
        P("dp", "ctx", None, None),
        P("dp", "ctx", None, None),
        P("dp", "ctx", None, None),
        P("dp", "ctx", None),
        P("dp", "ctx", None),
        P(),
        P("dp", "ctx"),
        P("dp", None),
        P(),
        P("dp", "ctx", None, None),
        P("dp", "ctx", None, None),
        P("dp", "ctx", None),
        P(None, "ctx", None),
        P(None, "ctx", None),
    )
    return jax.shard_map(
        shards,
        mesh=mesh,
        in_specs=placed,
        out_specs=(P("dp", "ctx", None, None), P("dp", "ctx", None, None), P()),
        check_vma=False,
    )
```

time: 417 us -> 206 us (0.49)
  other arithmetic: 174 us -> 4.6 us
  blocking collectives: 125 us -> 21.6 us
  waiting for transfers between devices: 17.3 us -> 63.9 us
  Pallas kernels: 0 us -> 43.4 us
  matrix products: 41.3 us -> 0 us
  starting transfers between devices: 29.7 us -> 55.5 us
  between operations: 16.2 us -> 0.98 us
  local copies, waits for them, and re-layouts: 8.72 us -> 14.6 us
    another operation x6 -> x7, other arithmetic: 161 us -> 0.97 us  [the longest x1 0.55 us: shards(): spot = jnp.stack([place, core]).astype(jnp.int32)]
    psum x1 -> x0, blocking collectives: 125 us -> none  [shards(): total_grad = lax.psum(partial_grad, ('dp', 'ctx'))]
    pallas_call x0 -> x7, Pallas kernels: none -> 43.4 us  [the longest x1 13.9 us: mla(): pl.pallas_call(functools.partial(mla_kernel, xs=xs), name='mla', out_shap...]
    dot_general x17 -> x0, matrix products: 39.3 us -> none  [the longest x4 9.83 us: advance(): jnp.einsum('shcd,shdv->shcv', transfer_map, state, precision=exact_mode)]
    ppermute x0 -> x7, starting transfers between devices: none -> 33.3 us  [the longest x3 18.8 us: across(): return lax.ppermute(value, 'ctx', [(i, i ^ step) for i in range(ranks)])]
    ppermute x0 -> x7, waiting for transfers between devices: none -> 33.2 us  [the longest x3 18.9 us: shards(): columns.append(lax.ppermute(held, 'ctx', pairs))]
    all_to_all x0 -> x1, blocking collectives: none -> 21.6 us  [shards(): lax.all_to_all(partial_grad, 'ctx', 0, 0, tiled=True)]
    ppermute x8 -> x4, starting transfers between devices: 29.6 us -> 11.2 us  [from_behind(): lax.ppermute(value, axis, [(source, source + steps) for source in range(l...]
  transfers between devices with their start and end apart: 10 -> 12, of which waited for: 2 -> 11; matrix products, arithmetic and copies ran while one was open for 53% -> 3% of each run, Pallas kernels for 0% -> 14%
where the time goes in v1:
time: 206 us; the launch traced here: 205 us
  waiting for transfers between devices  63.9 us (31%)
  starting transfers between devices  55.5 us (27%)
  Pallas kernels  43.4 us (21%)
  blocking collectives  21.6 us (10%)
  local copies, waits for them, and re-layouts  14.6 us (7%)
  other arithmetic  4.6 us (2%)
    ppermute x4, waiting for transfers between devices, from_behind(): lax.ppermute(value, axis, [(source, source + steps) for source in range(l...  24.3 us
    all_to_all x1, blocking collectives, shards(): lax.all_to_all(partial_grad, 'ctx', 0, 0, tiled=True)  21.6 us
    ppermute x3, waiting for transfers between devices, shards(): columns.append(lax.ppermute(held, 'ctx', pairs))  18.9 us
    ppermute x3, starting transfers between devices, across(): return lax.ppermute(value, 'ctx', [(i, i ^ step) for i in range(ranks)])  18.8 us
    ppermute x3, waiting for transfers between devices, across(): return lax.ppermute(value, 'ctx', [(i, i ^ step) for i in range(ranks)])  14.2 us
    pallas_call x1, Pallas kernels, mla(): pl.pallas_call(functools.partial(mla_kernel, xs=xs), name='mla', out_shap...  13.9 us
    unnamed x56, local copies, waits for them, and re-layouts  12.6 us
    ppermute x4, starting transfers between devices, from_behind(): lax.ppermute(value, axis, [(source, source + steps) for source in range(l...  11.2 us
  transfers between devices with their start and end apart: 12, of which 11 were waited for; matrix products, arithmetic and copies ran while one was open for 3% of the time, Pallas kernels for 14%

profile of v1, /device:TPU:1, one launch (start us, length us, event | category | flops | bytes accessed | tf_op | source)
XLA Modules:
  0.0 204.6 jit_solution(15594025004941873728)
XLA Ops:
  2.3 11.5 %collective-permute-start.4 = (bf16[256,128]{1,0:T(8,128)(2,1)S(1)}, bf16[256,128]{1,0:T(8,128)(2,1)S(1)}, u32[]{:S(2)}, u32[]{:S(2)}) collective-permute-start(bf16[256,128]{1,0:T(8,128)(2,1)S(1)} %get-tuple-element.44), channel_id=1, source_target_pairs={{0,16},{1,17},{2,18},{3,19},{4,20},{5,21},{6,22},{7,23},{8,24},{9,... | collective-permute-start | bytes 196616 | tf_op jit(solution)/shard_map/ppermute | solution.py:583
  15.5 5.4 %collective-permute-start.5 = (bf16[2,256,128]{2,1,0:T(8,128)(2,1)S(1)}, bf16[2,256,128]{2,1,0:T(8,128)(2,1)S(1)}, u32[]{:S(2)}, u32[]{:S(2)}) collective-permute-start(bf16[2,256,128]{2,1,0:T(8,128)(2,1)S(1)} %get-tuple-element.42), channel_id=1, source_target_pairs={{0,8},{1,9},{2,10},{3,11},{4,12},{5,13},{6,14},{7,15},{8,0},{9,1},... | collective-permute-start | bytes 393224 | tf_op jit(solution)/shard_map/ppermute | solution.py:583
  20.9 5.8 %collective-permute-done.5 = bf16[2,256,128]{2,1,0:T(8,128)(2,1)S(1)} collective-permute-done((bf16[2,256,128]{2,1,0:T(8,128)(2,1)S(1)}, bf16[2,256,128]{2,1,0:T(8,128)(2,1)S(1)}, u32[]{:S(2)}, u32[]{:S(2)}) %collective-permute-start.5) | collective-permute-done | bytes 131104 | tf_op jit(solution)/shard_map/ppermute | solution.py:583
  28.8 6.7 %collective-permute-done.6 = bf16[1024,128]{1,0:T(8,128)(2,1)S(1)} collective-permute-done((bf16[1024,128]{1,0:T(8,128)(2,1)S(1)}, bf16[1024,128]{1,0:T(8,128)(2,1)S(1)}, u32[]{:S(2)}, u32[]{:S(2)}) %collective-permute-start.6) | collective-permute-done | bytes 262176 | tf_op jit(solution)/shard_map/ppermute | solution.py:583
  35.6 3.5 %collective-permute-start.9 = (bf16[2,1024,128]{2,1,0:T(8,128)(2,1)S(1)}, bf16[2,1024,128]{2,1,0:T(8,128)(2,1)S(1)}, u32[]{:S(2)}, u32[]{:S(2)}) collective-permute-start(bf16[2,1024,128]{2,1,0:T(8,128)(2,1)S(1)} %get-tuple-element.36), channel_id=1, source_target_pairs={{3,0},{0,1},{1,2},{2,3},{7,4},{4,5},{5,6},{6,7},{11,8},{8,9},{9,10... | collective-permute-start | bytes 1572872 | tf_op jit(solution)/shard_map/ppermute | solution.py:610
  39.1 4.4 %collective-permute-start.8 = (bf16[2,1024,128]{2,1,0:T(8,128)(2,1)S(1)}, bf16[2,1024,128]{2,1,0:T(8,128)(2,1)S(1)}, u32[]{:S(2)}, u32[]{:S(2)}) collective-permute-start(bf16[2,1024,128]{2,1,0:T(8,128)(2,1)S(1)} %get-tuple-element.36), channel_id=1, source_target_pairs={{2,0},{3,1},{0,2},{1,3},{6,4},{7,5},{4,6},{5,7},{10,8},{11,9},{8,1... | collective-permute-start | bytes 1572872 | tf_op jit(solution)/shard_map/ppermute | solution.py:610
  43.5 3.1 %collective-permute-start.7 = (bf16[2,1024,128]{2,1,0:T(8,128)(2,1)S(1)}, bf16[2,1024,128]{2,1,0:T(8,128)(2,1)S(1)}, u32[]{:S(2)}, u32[]{:S(2)}) collective-permute-start(bf16[2,1024,128]{2,1,0:T(8,128)(2,1)S(1)} %get-tuple-element.36), channel_id=1, source_target_pairs={{1,0},{2,1},{3,2},{0,3},{5,4},{6,5},{7,6},{4,7},{9,8},{10,9},{11,1... | collective-permute-start | bytes 1572872 | tf_op jit(solution)/shard_map/ppermute | solution.py:610
  46.5 4.1 %collective-permute-done.9 = bf16[2,1024,128]{2,1,0:T(8,128)(2,1)S(1)} collective-permute-done((bf16[2,1024,128]{2,1,0:T(8,128)(2,1)S(1)}, bf16[2,1024,128]{2,1,0:T(8,128)(2,1)S(1)}, u32[]{:S(2)}, u32[]{:S(2)}) %collective-permute-start.9) | collective-permute-done | bytes 524320 | tf_op jit(solution)/shard_map/ppermute | solution.py:610
  50.6 12.4 %collective-permute-done.8 = bf16[2,1024,128]{2,1,0:T(8,128)(2,1)S(1)} collective-permute-done((bf16[2,1024,128]{2,1,0:T(8,128)(2,1)S(1)}, bf16[2,1024,128]{2,1,0:T(8,128)(2,1)S(1)}, u32[]{:S(2)}, u32[]{:S(2)}) %collective-permute-start.8) | collective-permute-done | bytes 524320 | tf_op jit(solution)/shard_map/ppermute | solution.py:610
  65.8 3.6 %collective-permute-start.10 = (bf16[4,2,1024,128]{3,2,1,0:T(8,128)(2,1)S(1)}, bf16[4,2,1024,128]{3,2,1,0:T(8,128)(2,1)}, u32[]{:S(2)}, u32[]{:S(2)}) collective-permute-start(bf16[4,2,1024,128]{3,2,1,0:T(8,128)(2,1)S(1)} %pad_maximum_fusion.own_w), channel_id=1, source_target_pairs={{0,32},{32,0},{64,96},{96,64},{128,160},{160,128},{192,224},{224,1... | collective-permute-start | bytes 6291464 | tf_op jit(solution)/shard_map/ppermute | solution.py:612
  70.7 5.4 %kda_pairs.1 = (f32[32,64,64]{2,1,0:T(8,128)S(1)}, bf16[32,64,64]{2,1,0:T(8,128)(2,1)S(1)}, bf16[32,64,256]{2,1,0:T(8,128)(2,1)S(1)}, bf16[32,64,128]{2,1,0:T(8,...) custom-call(s32[1]{0:T(128)} %bitcast.place_ref, bf16[2048,128]{1,0:T(8,128)(2,1)S(1)} %bitcast.45, ...), custom_call_target="tpu_custom_call" | custom-call | flops 300000000 | bytes 12000000 | tf_op jit(solution)/shard_map/kda_pairs/pallas_call | solution.py:135
  76.1 10.1 %kda_invert.1.xmat = f32[32,64,64]{2,1,0:T(8,128)S(1)} custom-call(f32[32,64,64]{2,1,0:T(8,128)S(1)} %get-tuple-element.20.lmat), custom_call_target="tpu_custom_call" | custom-call | flops 300000000 | bytes 12000000 | tf_op jit(solution)/shard_map/kda_invert/pallas_call | solution.py:187
  92.5 4.9 %collective-permute-start = (bf16[2304,128]{1,0:T(8,128)(2,1)S(1)}, bf16[2304,128]{1,0:T(8,128)(2,1)S(1)}, u32[]{:S(2)}, u32[]{:S(2)}) collective-permute-start(bf16[2304,128]{1,0:T(8,128)(2,1)S(1)} %get-tuple-element.29.offs_first), channel_id=1, source_target_pairs={{0,1},{1,2},{2,3},{3,4},{4,5},{5,6},{6,7},{7,8},{8,9},{9,10},{10,1... | collective-permute-start | bytes 1769480 | tf_op jit(solution)/shard_map/ppermute | solution.py:543
  97.3 12.6 %collective-permute-done.in_first.back_one = bf16[2304,128]{1,0:T(8,128)(2,1)S(1)} collective-permute-done((bf16[2304,128]{1,0:T(8,128)(2,1)S(1)}, bf16[2304,128]{1,0:T(8,128)(2,1)S(1)}, u32[]{:S(2)}, u32[]{:S(2)}) %collective-permute-start) | collective-permute-done | bytes 589856 | tf_op jit(solution)/shard_map/ppermute | solution.py:543
  111.3 3.9 %kda_carry.1 = (bf16[2304,128]{1,0:T(8,128)(2,1)}, bf16[2304,128]{1,0:T(8,128)(2,1)}) custom-call(s32[1]{0:T(128)} %bitcast.place_ref, bf16[32,128,128]{2,1,0:T(8,128)(2,1)} %copy-done.6, bf16[2304,128]{1,0:T(8,128)(2,1)} %copy-done.10, bf16[2560,128]{1,0:T(8,128)(2,1)} %copy-done.8, bf16[2304,128]{1,0:T(8,128)(2,1)} %copy-done.3, bf16[2560,128]{1,0:T(8,128)(2,1)} %copy-done.1), custom_call_target="tpu_custom_call" | custom-call | flops 130000000 | bytes 5000000 | tf_op jit(solution)/shard_map/kda_carry/pallas_call | solution.py:304
  115.2 3.8 %collective-permute-start.2 = (bf16[2304,128]{1,0:T(8,128)(2,1)}, bf16[2304,128]{1,0:T(8,128)(2,1)S(1)}, u32[]{:S(2)}, u32[]{:S(2)}) collective-permute-start(bf16[2304,128]{1,0:T(8,128)(2,1)} %get-tuple-element.31.own_first), channel_id=1, source_target_pairs={{0,1},{1,2},{2,3},{3,4},{4,5},{5,6},{6,7},{7,8},{8,9},{9,10},{10,1... | collective-permute-start | bytes 1769480 | tf_op jit(solution)/shard_map/ppermute | solution.py:543
  120.3 3.5 %kda_local.1 = (f32[32,64,128]{2,1,0:T(8,128)}, bf16[32,64,128]{2,1,0:T(8,128)(2,1)}) custom-call(bf16[32,64,64]{2,1,0:T(8,128)(2,1)} %copy-done.17, bf16[32,64,256]{2,1,0:T(8,128)(2,1)} %copy-done.5, bf16[32,64,128]{2,1,0:T(8,128)(2,1)} %copy-done.18), custom_call_target="tpu_custom_call" | custom-call | flops 70000000 | bytes 4000000 | tf_op jit(solution)/shard_map/kda_local/pallas_call | solution.py:269
  123.9 7.2 %collective-permute-done.2.in_first.back_two = bf16[2304,128]{1,0:T(8,128)(2,1)S(1)} collective-permute-done((bf16[2304,128]{1,0:T(8,128)(2,1)}, bf16[2304,128]{1,0:T(8,128)(2,1)S(1)}, u32[]{:S(2)}, u32[]{:S(2)}) %collective-permute-start.2) | collective-permute-done | bytes 589856 | tf_op jit(solution)/shard_map/ppermute | solution.py:543
  131.1 3.9 %collective-permute-done.3.in_second.ahead_two = bf16[2304,128]{1,0:T(8,128)(2,1)} collective-permute-done((bf16[2304,128]{1,0:T(8,128)(2,1)}, bf16[2304,128]{1,0:T(8,128)(2,1)}, u32[]{:S(2)}, u32[]{:S(2)}) %collective-permute-start.3) | collective-permute-done | bytes 589856 | tf_op jit(solution)/shard_map/ppermute | solution.py:543
  140.0 3.6 %kda_close.1 = (bf16[2048,128]{1,0:T(8,128)(2,1)}, f32[32,128]{1,0:T(8,128)S(1)}) custom-call(s32[1]{0:T(128)} %bitcast.place_ref, f32[32,64,128]{2,1,0:T(8,128)S(1)} %copy-done.7, bf16[32,64,128]{2,1,0:T(8,128)(2,1)S(1)} %copy-done.19, bf16[2304,128]{1,0:T(8,128)(2,1)S(1)} %copy-done.9, bf16[2304,128]{1,0:T(8,128)(2,1)S(1)} %collective-permute-done.2.in_first.back_two, ...), custom_call_target="tpu_custom_call" | custom-call | flops 70000000 | bytes 5000000 | tf_op jit(solution)/shard_map/kda_close/pallas_call | solution.py:357
  143.7 21.6 %all_to_all.15 = f32[32,1,128]{2,1,0:T(1,128)} all-to-all(f32[32,1,128]{2,1,0:T(1,128)S(1)} %bitcast.54), channel_id=1, replica_groups=mesh['dp'=16,'ctx'=32] {'ctx'}, dimensions={0} | all-to-all | bytes 32768 | tf_op jit(solution)/shard_map/all_to_all | solution.py:632
  167.7 10.9 %all-to-all-start.1 = ((f32[16,1,128]{2,1,0:T(1,128)}), f32[16,1,128]{2,1,0:T(1,128)}, u32[]{:S(2)}, u32[]{:S(2)}) async-start(f32[16,1,128]{2,1,0:T(1,128)} %broadcast_in_dim.3), calls=%async_computation.1 | async-start | bytes 16384 | tf_op jit(solution)/shard_map/all_to_all | solution.py:634
  179.1 6.5 %all-to-all-done.1 = f32[16,1,128]{2,1,0:T(1,128)} async-done(((f32[16,1,128]{2,1,0:T(1,128)}), f32[16,1,128]{2,1,0:T(1,128)}, u32[]{:S(2)}, u32[]{:S(2)}) %all-to-all-start.1) | async-done | bytes 8224 | tf_op jit(solution)/shard_map/all_to_all | solution.py:634
  190.7 13.9 %mla.1 = bf16[2048,128]{1,0:T(8,128)(2,1)} custom-call(s32[2]{0:T(128)S(1)} %copy-done.24, bf16[2048,128]{1,0:T(8,128)(2,1)S(1)} %bitcast.48, bf16[128,512]{1,0:T(8,128)(2,1)S(1)} %bitcast.44, bf16[2304,128]{1,0:T(8,128)(2,1)S(1)} %copy-done.4, bf16[2560,128]{1,0:T(8,128)(2,1)S(1)} %copy-done.2, ...), custom_call_target="tpu_custom_call" | custom-call | flops 1500000000 | bytes 7000000 | tf_op jit(solution)/shard_map/mla/pallas_call | solution.py:520
  (78 shorter events, 31.3 us)
Async XLA Ops:
  2.3 13.2 %collective-permute-start.4 = (bf16[256,128]{1,0:T(8,128)(2,1)S(1)}, bf16[256,128]{1,0:T(8,128)(2,1)S(1)}, u32[]{:S(2)}, u32[]{:S(2)}) collective-permute-start(bf16[256,128]{1,0:T(8,128)(2,1)S(1)} %get-tuple-element.44), channel_id=1, source_target_pairs={{0,16},{1,17},{2,18},{3,19},{4,20},{5,21},{6,22},{7,23},{8,24},{9,... | collective-permute-start | bytes 196616 | tf_op jit(solution)/shard_map/ppermute | solution.py:583
  15.5 11.3 %collective-permute-start.5 = (bf16[2,256,128]{2,1,0:T(8,128)(2,1)S(1)}, bf16[2,256,128]{2,1,0:T(8,128)(2,1)S(1)}, u32[]{:S(2)}, u32[]{:S(2)}) collective-permute-start(bf16[2,256,128]{2,1,0:T(8,128)(2,1)S(1)} %get-tuple-element.42), channel_id=1, source_target_pairs={{0,8},{1,9},{2,10},{3,11},{4,12},{5,13},{6,14},{7,15},{8,0},{9,1},... | collective-permute-start | bytes 393224 | tf_op jit(solution)/shard_map/ppermute | solution.py:583
  26.8 8.7 %collective-permute-start.6 = (bf16[1024,128]{1,0:T(8,128)(2,1)S(1)}, bf16[1024,128]{1,0:T(8,128)(2,1)S(1)}, u32[]{:S(2)}, u32[]{:S(2)}) collective-permute-start(bf16[1024,128]{1,0:T(8,128)(2,1)S(1)} %get-tuple-element.38), channel_id=1, source_target_pairs={{0,4},{1,5},{2,6},{3,7},{4,0},{5,1},{6,2},{7,3},{8,12},{9,13},{10,... | collective-permute-start | bytes 786440 | tf_op jit(solution)/shard_map/ppermute | solution.py:583
  35.6 15.0 %collective-permute-start.9 = (bf16[2,1024,128]{2,1,0:T(8,128)(2,1)S(1)}, bf16[2,1024,128]{2,1,0:T(8,128)(2,1)S(1)}, u32[]{:S(2)}, u32[]{:S(2)}) collective-permute-start(bf16[2,1024,128]{2,1,0:T(8,128)(2,1)S(1)} %get-tuple-element.36), channel_id=1, source_target_pairs={{3,0},{0,1},{1,2},{2,3},{7,4},{4,5},{5,6},{6,7},{11,8},{8,9},{9,10... | collective-permute-start | bytes 1572872 | tf_op jit(solution)/shard_map/ppermute | solution.py:610
  39.1 23.9 %collective-permute-start.8 = (bf16[2,1024,128]{2,1,0:T(8,128)(2,1)S(1)}, bf16[2,1024,128]{2,1,0:T(8,128)(2,1)S(1)}, u32[]{:S(2)}, u32[]{:S(2)}) collective-permute-start(bf16[2,1024,128]{2,1,0:T(8,128)(2,1)S(1)} %get-tuple-element.36), channel_id=1, source_target_pairs={{2,0},{3,1},{0,2},{1,3},{6,4},{7,5},{4,6},{5,7},{10,8},{11,9},{8,1... | collective-permute-start | bytes 1572872 | tf_op jit(solution)/shard_map/ppermute | solution.py:610
  43.5 22.0 %collective-permute-start.7 = (bf16[2,1024,128]{2,1,0:T(8,128)(2,1)S(1)}, bf16[2,1024,128]{2,1,0:T(8,128)(2,1)S(1)}, u32[]{:S(2)}, u32[]{:S(2)}) collective-permute-start(bf16[2,1024,128]{2,1,0:T(8,128)(2,1)S(1)} %get-tuple-element.36), channel_id=1, source_target_pairs={{1,0},{2,1},{3,2},{0,3},{5,4},{6,5},{7,6},{4,7},{9,8},{10,9},{11,1... | collective-permute-start | bytes 1572872 | tf_op jit(solution)/shard_map/ppermute | solution.py:610
  65.4 4.0 %copy-start.26 = (f32[1,128,16]{1,2,0:T(8,128)S(1)}, f32[1,128,16]{1,2,0:T(8,128)}, u32[]{:S(2)}) copy-start(f32[1,128,16]{1,2,0:T(8,128)} %param.18) | copy-start | bytes 24580
  65.4 4.2 %copy-start.12 = (bf16[1,128,16,128]{3,2,1,0:T(8,128)(2,1)S(1)}, bf16[1,128,16,128]{3,2,1,0:T(8,128)(2,1)}, u32[]{:S(2)}) copy-start(bf16[1,128,16,128]{3,2,1,0:T(8,128)(2,1)} %param.14) | copy-start | bytes 1572868
  65.4 4.2 %copy-start.13 = (bf16[1,128,16,128]{3,2,1,0:T(8,128)(2,1)S(1)}, bf16[1,128,16,128]{3,2,1,0:T(8,128)(2,1)}, u32[]{:S(2)}) copy-start(bf16[1,128,16,128]{3,2,1,0:T(8,128)(2,1)} %param.15) | copy-start | bytes 1572868
  65.5 4.2 %copy-start.20 = (s32[1,4096]{1,0:T(1,128)S(1)}, s32[1,4096]{1,0:T(1,128)}, u32[]{:S(2)}) copy-start(s32[1,4096]{1,0:T(1,128)} %param.21) | copy-start | bytes 49156
  65.5 4.2 %copy-start.21 = (f32[16,128]{1,0:T(8,128)S(1)}, f32[16,128]{1,0:T(8,128)}, u32[]{:S(2)}) copy-start(f32[16,128]{1,0:T(8,128)} %rate_ref.1) | copy-start | bytes 24580
  65.5 4.2 %copy-start.22 = (s32[1,128]{1,0:T(1,128)S(1)}, s32[1,128]{1,0:T(1,128)}, u32[]{:S(2)}) copy-start(s32[1,128]{1,0:T(1,128)} %mask_ref.1) | copy-start | bytes 1540
  65.8 20.5 %copy-start.11 = (bf16[1,128,512]{2,1,0:T(8,128)(2,1)S(1)}, bf16[1,128,512]{2,1,0:T(8,128)(2,1)}, u32[]{:S(2)}) copy-start(bf16[1,128,512]{2,1,0:T(8,128)(2,1)} %param.25) | copy-start | bytes 393220
  65.8 122.3 %collective-permute-start.10 = (bf16[4,2,1024,128]{3,2,1,0:T(8,128)(2,1)S(1)}, bf16[4,2,1024,128]{3,2,1,0:T(8,128)(2,1)}, u32[]{:S(2)}, u32[]{:S(2)}) collective-permute-start(bf16[4,2,1024,128]{3,2,1,0:T(8,128)(2,1)S(1)} %pad_maximum_fusion.own_w), channel_id=1, source_target_pairs={{0,32},{32,0},{64,96},{96,64},{128,160},{160,128},{192,224},{224,1... | collective-permute-start | bytes 6291464 | tf_op jit(solution)/shard_map/ppermute | solution.py:612
  76.1 13.1 %copy-start.17 = (bf16[32,64,64]{2,1,0:T(8,128)(2,1)}, bf16[32,64,64]{2,1,0:T(8,128)(2,1)S(1)}, u32[]{:S(2)}) copy-start(bf16[32,64,64]{2,1,0:T(8,128)(2,1)S(1)} %get-tuple-element.19.att) | copy-start | bytes 786436
  76.1 13.1 %copy-start.18 = (bf16[32,64,128]{2,1,0:T(8,128)(2,1)}, bf16[32,64,128]{2,1,0:T(8,128)(2,1)S(1)}, u32[]{:S(2)}) copy-start(bf16[32,64,128]{2,1,0:T(8,128)(2,1)S(1)} %get-tuple-element.25.carried_q) | copy-start | bytes 1572868
  91.2 19.3 %copy-start.8 = (bf16[2560,128]{1,0:T(8,128)(2,1)}, bf16[2560,128]{1,0:T(8,128)(2,1)S(1)}, u32[]{:S(2)}) copy-start(bf16[2560,128]{1,0:T(8,128)(2,1)S(1)} %get-tuple-element.30.offs_second) | copy-start | bytes 1966084
  91.2 19.3 %copy-start.10 = (bf16[2304,128]{1,0:T(8,128)(2,1)}, bf16[2304,128]{1,0:T(8,128)(2,1)S(1)}, u32[]{:S(2)}) copy-start(bf16[2304,128]{1,0:T(8,128)(2,1)S(1)} %get-tuple-element.29.offs_first) | copy-start | bytes 1769476
  91.2 19.3 %collective-permute-start.1 = (bf16[2560,128]{1,0:T(8,128)(2,1)S(1)}, bf16[2560,128]{1,0:T(8,128)(2,1)S(1)}, u32[]{:S(2)}, u32[]{:S(2)}) collective-permute-start(bf16[2560,128]{1,0:T(8,128)(2,1)S(1)} %get-tuple-element.30.offs_second), channel_id=1, source_target_pairs={{1,0},{2,1},{3,2},{4,3},{5,4},{6,5},{7,6},{8,7},{9,8},{10,9},{11,1... | collective-permute-start | bytes 1966088 | tf_op jit(solution)/shard_map/ppermute | solution.py:543
  92.5 17.5 %collective-permute-start = (bf16[2304,128]{1,0:T(8,128)(2,1)S(1)}, bf16[2304,128]{1,0:T(8,128)(2,1)S(1)}, u32[]{:S(2)}, u32[]{:S(2)}) collective-permute-start(bf16[2304,128]{1,0:T(8,128)(2,1)S(1)} %get-tuple-element.29.offs_first), channel_id=1, source_target_pairs={{0,1},{1,2},{2,3},{3,4},{4,5},{5,6},{6,7},{7,8},{8,9},{9,10},{10,1... | collective-permute-start | bytes 1769480 | tf_op jit(solution)/shard_map/ppermute | solution.py:543
  115.2 15.9 %collective-permute-start.2 = (bf16[2304,128]{1,0:T(8,128)(2,1)}, bf16[2304,128]{1,0:T(8,128)(2,1)S(1)}, u32[]{:S(2)}, u32[]{:S(2)}) collective-permute-start(bf16[2304,128]{1,0:T(8,128)(2,1)} %get-tuple-element.31.own_first), channel_id=1, source_target_pairs={{0,1},{1,2},{2,3},{3,4},{4,5},{5,6},{6,7},{7,8},{8,9},{9,10},{10,1... | collective-permute-start | bytes 1769480 | tf_op jit(solution)/shard_map/ppermute | solution.py:543
  119.0 16.0 %collective-permute-start.3 = (bf16[2304,128]{1,0:T(8,128)(2,1)}, bf16[2304,128]{1,0:T(8,128)(2,1)}, u32[]{:S(2)}, u32[]{:S(2)}) collective-permute-start(bf16[2304,128]{1,0:T(8,128)(2,1)} %get-tuple-element.32), channel_id=1, source_target_pairs={{1,0},{2,1},{3,2},{4,3},{5,4},{6,5},{7,6},{8,7},{9,8},{10,9},{11,1... | collective-permute-start | bytes 1769480 | tf_op jit(solution)/shard_map/ppermute | solution.py:543
  123.9 64.2 %copy-start.2 = (bf16[2560,128]{1,0:T(8,128)(2,1)S(1)}, bf16[2560,128]{1,0:T(8,128)(2,1)}, u32[]{:S(2)}) copy-start(bf16[2560,128]{1,0:T(8,128)(2,1)} %copy-done.1) | copy-start | bytes 1966084
  167.7 17.9 %all-to-all-start.1 = ((f32[16,1,128]{2,1,0:T(1,128)}), f32[16,1,128]{2,1,0:T(1,128)}, u32[]{:S(2)}, u32[]{:S(2)}) async-start(f32[16,1,128]{2,1,0:T(1,128)} %broadcast_in_dim.3), calls=%async_computation.1 | async-start | bytes 16384 | tf_op jit(solution)/shard_map/all_to_all | solution.py:634
  (15 other events, 17.2 us)

commit v2 on v1

--- a/solution.py
+++ b/solution.py
@@ -45,25 +45,25 @@
 
 
 def kda_pairs_kernel(
-    place_ref, q_ref, k_ref, v_ref, w_ref, scale_ref, rate_ref, mask_ref, docs_ref,
+    place_ref, q_hbm, k_hbm, v_hbm, w_ref, scale_ref, rate_ref, mask_ref, docs_ref,
     lmat, att, rhs, leaving, closing, carried_q,
-    qn, kn, vn, acol, wcol, bcol, ccol, tcol, incl, excl,
+    q_ref, k_ref, v_ref, sems, qn, kn, vn, acol, wcol, bcol, ccol, tcol, incl, excl,
 ):
     heads = rate_ref.shape[0]
     place = place_ref[0]
     ranks = docs_ref.shape[0]
     rows = HALF * heads
 
-    def widen(c, _):
-        at = pl.ds(pl.multiple_of(c * 256, 256), 256)
-        for source, target in ((q_ref, qn), (k_ref, kn)):
-            x = source[at, :].astype(F32)
-            target[at, :] = x * lax.rsqrt(jnp.sum(x * x, axis=1, keepdims=True) + 1e-06)
-        vn[at, :] = v_ref[at, :].astype(F32)
-        return 0
-
-    lax.fori_loop(0, 2 * rows // 256, widen, 0)
+    copies = [
+        pltpu.make_async_copy(source, target, sems.at[n])
+        for n, (source, target) in enumerate(((q_hbm, q_ref), (k_hbm, k_ref), (v_hbm, v_ref)))
+    ]
+    for copy in copies:
+        copy.start()
+
     ti, si = iota2((HALF, HALF), 0), iota2((HALF, HALF), 1)
+    scales = scale_ref[...].T
+    strengths = w_ref[...].T
     for i in range(2):
         block = place if i == 0 else 2 * ranks - 1 - place
         drow = docs_row(docs_ref, block)
@@ -75,17 +75,30 @@
         incl[i] = within
         excl[i] = jnp.where(same & (ti > si), 1.0, 0.0)
         gates = lax.dot_general(
-            within, scale_ref[i * HALF : (i + 1) * HALF, :], (((1,), (0,)), ((), ())),
+            within, scales[i * HALF : (i + 1) * HALF, :], (((1,), (0,)), ((), ())),
             precision=lax.Precision.HIGHEST, preferred_element_type=F32,
         )
         lost = mask_ref[:, i * HALF : (i + 1) * HALF].astype(F32)
         bcol[i] = jnp.broadcast_to(jnp.sum(within * lost, axis=1, keepdims=True) * LOSS, (HALF, DN))
         ccol[i] = jnp.broadcast_to(jnp.where(dcol == prior, 1.0, 0.0), (HALF, DN))
         tcol[i] = jnp.broadcast_to(jnp.where(dcol == drow[:, HALF - 1 :], 1.0, 0.0), (HALF, DN))
-        writes = w_ref[i * HALF : (i + 1) * HALF, :]
+        writes = strengths[i * HALF : (i + 1) * HALF, :]
         for h in range(heads):
             acol[i * heads + h] = jnp.broadcast_to(gates[:, h : h + 1], (HALF, DN))
             wcol[i * heads + h] = jnp.broadcast_to(writes[:, h : h + 1], (HALF, DN))
+
+    for copy in copies:
+        copy.wait()
+
+    def widen(c, _):
+        at = pl.ds(pl.multiple_of(c * 256, 256), 256)
+        for source, target in ((q_ref, qn), (k_ref, kn)):
+            x = source[at, :].astype(F32)
+            target[at, :] = x * lax.rsqrt(jnp.sum(x * x, axis=1, keepdims=True) + 1e-06)
+        vn[at, :] = v_ref[at, :].astype(F32)
+        return 0
+
+    lax.fori_loop(0, 2 * rows // 256, widen, 0)
 
     def pairs(g, _):
         for u in range(4):
@@ -136,9 +149,13 @@
         kda_pairs_kernel,
         name="kda_pairs",
         out_shape=shapes,
-        in_specs=[pl.BlockSpec(memory_space=pltpu.SMEM)] + [spec] * 8,
+        in_specs=[pl.BlockSpec(memory_space=pltpu.SMEM)]
+        + [pl.BlockSpec(memory_space=pltpu.HBM)] * 3
+        + [spec] * 5,
         out_specs=(spec,) * 6,
         scratch_shapes=[
+            pltpu.VMEM((rows, DN), BF), pltpu.VMEM((rows, DN), BF), pltpu.VMEM((rows, DN), BF),
+            pltpu.SemaphoreType.DMA((3,)),
             vm(rows, DN), vm(rows, DN), vm(rows, DN),
             vm(n, HALF, DN), vm(n, HALF, DN),
             vm(2, HALF, DN), vm(2, HALF, DN), vm(2, HALF, DN),
@@ -149,23 +166,46 @@
     )(place, q, k, v, w, scale, rate, mask, docs)
 
 
-def kda_invert_kernel(lmat, xmat):
+def kda_invert_kernel(lmat, xmat, pick, coef):
     heads = lmat.shape[0] // 2
     ti, si = iota2((HALF, HALF), 0), iota2((HALF, HALF), 1)
 
+    kk, lane = iota2((4 * HALF, DN), 0), iota2((4 * HALF, DN), 1)
+    side = (kk // DN) == (lane // HALF)
+    for j in range(15):
+        pick[:, j * DN : (j + 1) * DN] = jnp.where(side & (kk % 16 == j), 1.0, 0.0).astype(BF)
+    near = (ti // 16) == (si // 16)
+    rowi, coli = iota2((8, DN), 0), iota2((8, DN), 1) % HALF
+
     def base(g, _):
-        for u in range(2):
-            p = g * 2 + u
-            lower = lmat[p]
+        wide = []
+        for u in range(4):
+            parts = []
+            for v in range(2):
+                lower = jnp.where(near, lmat[g * 8 + 2 * u + v], 0.0)
+                high = lower.astype(BF).astype(F32)
+                parts += [high, lower - high]
+            wide.append(jnp.concatenate(parts, axis=1).astype(BF))
+        coef[...] = mm(jnp.concatenate(wide, axis=0), pick[...])
+        for u in range(4):
+            made = []
             for b in range(HALF // 16):
-                x = jnp.where(iota2((16, HALF), 0) + 16 * b == iota2((16, HALF), 1), 1.0, 0.0)
-                part = lower[16 * b : 16 * b + 16, :]
+                top = jnp.where(coli == rowi + 16 * b, 1.0, 0.0)
+                low = jnp.where(coli == rowi + 16 * b + 8, 1.0, 0.0)
+                at = u * HALF + 16 * b
                 for j in range(15):
-                    x = x - part[:, 16 * b + j : 16 * b + j + 1] * x[j : j + 1, :]
-                xmat[p, 16 * b : 16 * b + 16, :] = x
-        return 0
-
-    lax.fori_loop(0, heads, base, 0)
+                    lanes = slice(j * DN, (j + 1) * DN)
+                    row = top[j : j + 1, :] if j < 8 else low[j - 8 : j - 7, :]
+                    if j < 7:
+                        top = top - coef[at : at + 8, lanes] * row
+                    low = low - coef[at + 8 : at + 16, lanes] * row
+                made += [top, low]
+            x = jnp.concatenate(made, axis=0)
+            xmat[g * 8 + 2 * u] = x[:, :HALF]
+            xmat[g * 8 + 2 * u + 1] = x[:, HALF:]
+        return 0
+
+    lax.fori_loop(0, heads // 4, base, 0)
 
     def merge(width, g, _):
         tb, sb = ti // width, si // width
@@ -190,6 +230,7 @@
         out_shape=jax.ShapeDtypeStruct(lmat.shape, F32),
         in_specs=[spec],
         out_specs=spec,
+        scratch_shapes=[pltpu.VMEM((4 * HALF, 15 * DN), BF), pltpu.VMEM((4 * HALF, 15 * DN), F32)],
         compiler_params=pltpu.CompilerParams(vmem_limit_bytes=16 << 20),
         cost_estimate=pl.CostEstimate(flops=300_000_000, bytes_accessed=12_000_000, transcendentals=0),
     )(lmat)
@@ -311,10 +352,13 @@
     )(place, tmap, offs_first, offs_second, in_first, in_second)
 
 
-def kda_close_kernel(place_ref, local, squery, own_first, in_first, in_second, gain, cot_ref, out_ref, grad_ref, cot, outs, *, ranks):
+def kda_close_kernel(place_ref, local, squery, own_first, in_first, in_second, gain, cot_hbm, out_ref, grad_ref, cot_ref, sem, cot, outs, *, ranks):
     heads = local.shape[0] // 2
     rows = HALF * heads
     end = jnp.full((DN, DN), place_ref[0], jnp.int32) == ranks - 1
+    copy = pltpu.make_async_copy(cot_hbm, cot_ref, sem)
+    copy.start()
+    copy.wait()
 
     def widen(c, _):
         at = pl.ds(pl.multiple_of(c * 256, 256), 256)
@@ -358,9 +402,11 @@
         functools.partial(kda_close_kernel, ranks=ranks),
         name="kda_close",
         out_shape=(jax.ShapeDtypeStruct((rows, DN), BF), jax.ShapeDtypeStruct((ranks, DN), F32)),
-        in_specs=[pl.BlockSpec(memory_space=pltpu.SMEM)] + [spec] * 7,
+        in_specs=[pl.BlockSpec(memory_space=pltpu.SMEM)] + [spec] * 6 + [pl.BlockSpec(memory_space=pltpu.HBM)],
         out_specs=(spec, spec),
-        scratch_shapes=[pltpu.VMEM((rows, DN), F32), pltpu.VMEM((rows, DN), F32)],
+        scratch_shapes=[
+            pltpu.VMEM((rows, DN), BF), pltpu.SemaphoreType.DMA,
+            pltpu.VMEM((rows, DN), F32), pltpu.VMEM((rows, DN), F32)],
         compiler_params=pltpu.CompilerParams(vmem_limit_bytes=32 << 20),
         cost_estimate=pl.CostEstimate(flops=70_000_000, bytes_accessed=5_000_000, transcendentals=4096),
     )(place, local, squery, own_first, in_first, in_second, gain, cot)
@@ -371,12 +417,26 @@
 
 
 def mla_kernel(
-    spot_ref, q_ref, lat_ref, back_one, ahead_one, back_two, ahead_two, docs_ref, own_w, other_w, out_ref,
-    qp, keys, keysp, mask, lifted, mixed, outs, *, xs,
+    spot_ref, q_hbm, lat_ref, back_one_hbm, ahead_one_hbm, back_two_hbm, ahead_two_hbm, docs_ref, own_hbm, other_hbm, out_ref,
+    q_ref, back_one, ahead_one, back_two, ahead_two, own_w, other_w, sems, qp, keys, keysp, mask, lifted, mixed, outs, *, xs,
 ):
     ranks = docs_ref.shape[0]
     place, core = spot_ref[0], spot_ref[1]
     heads = q_ref.shape[0] // (2 * HALF)
+    low = heads * DN
+    quarter = pl.ds(low, 4 * HALF)
+    moves = (
+        (q_hbm, q_ref),
+        (back_two_hbm.at[quarter, :], back_two),
+        (back_one_hbm.at[quarter, :], back_one),
+        (ahead_two_hbm.at[quarter, :], ahead_two),
+        (ahead_one_hbm.at[pl.ds(low, 8 * HALF), :], ahead_one),
+        (own_hbm, own_w),
+        (other_hbm, other_w),
+    )
+    copies = [pltpu.make_async_copy(a, b, sems.at[n]) for n, (a, b) in enumerate(moves)]
+    for copy in copies:
+        copy.start()
     here_z, here_x = place // xs, place % xs
     width = keys.shape[1]
 
@@ -388,38 +448,39 @@
 
     keys[0, 3 * HALF :, :] = jnp.zeros((width - 3 * HALF, 4 * DN), BF)
     keys[1, 3 * HALF :, :] = jnp.zeros((width - 3 * HALF, 4 * DN), BF)
-    low = heads * DN
-    piece(back_two, low, 0, 0)
-    piece(back_one, low, 0, 1)
+    for copy in copies[:5]:
+        copy.wait()
+    piece(back_two, 0, 0, 0)
+    piece(back_one, 0, 0, 1)
     keys[0, 2 * HALF : 3 * HALF, :] = lat_ref[:HALF, :]
     keys[1, 2 * HALF : 3 * HALF, :] = lat_ref[HALF:, :]
 
     @pl.when(place < ranks - 2)
     def _():
-        piece(ahead_two, low, 1, 0)
+        piece(ahead_two, 0, 1, 0)
 
     @pl.when(place == ranks - 2)
     def _():
-        piece(ahead_one, low, 1, 0)
+        piece(ahead_one, 0, 1, 0)
 
     @pl.when(place == ranks - 1)
     def _():
-        piece(back_one, low, 1, 0)
+        piece(back_one, 0, 1, 0)
         keys[1, HALF : 2 * HALF, :] = lat_ref[:HALF, :]
 
     @pl.when(place < ranks - 1)
     def _():
-        piece(ahead_one, low + 4 * HALF, 1, 1)
+        piece(ahead_one, 4 * HALF, 1, 1)
 
     def source_n(k):
-        off = ((k // 4) % 2) * 4 + ((k // 8) % 2) * 2 + (k // 16) % 2
+        off = ((k // 4) % 2) * 4 + ((k // 32) % 2) * 2 + k // 64
         z = lax.bitwise_xor(off, jnp.full(k.shape, here_z, jnp.int32))
-        return (z * xs + (k // 32 + here_x) % xs) * 4 + k % 4
+        return (z * xs + ((k // 8) % xs + here_x) % xs) * 4 + k % 4
 
     def source_l(k):
-        off = ((k // 16) % 2) * 4 + ((k // 32) % 2) * 2 + (k // 64) % 2
+        off = ((k // 16) % 2) * 4 + ((k // 128) % 2) * 2 + k // 256
         z = lax.bitwise_xor(off, jnp.full(k.shape, here_z, jnp.int32))
-        return (z * xs + (k // 128 + here_x) % xs) * 16 + k % 16
+        return (z * xs + ((k // 32) % xs + here_x) % xs) * 16 + k % 16
 
     pick = onehot((DN, DN), source_n)
     rows = 256
@@ -452,6 +513,7 @@
     span = heads // 2
     for side, weights in ((0, own_w), (1, other_w)):
         first = span * core if side == 0 else span * (1 - core)
+        copies[5 + side].wait()
 
         def lift(g, _, weights=weights, first=first):
             for u in range(2):
@@ -459,9 +521,9 @@
                 h = first + hl
                 q = qp[pl.ds(h, 2 * HALF, stride=heads), :].astype(BF)
                 for lb in range(4):
-                    at = pl.ds(pl.multiple_of((hl * 4 + lb) * 16, 16), 16)
+                    at = pl.ds(pl.multiple_of((hl * 4 + lb) * 32, 32), 32)
                     w = jnp.concatenate(
-                        [weights[xr, e, at, :] for xr in range(4) for e in range(2)], axis=0
+                        [weights[e, b, at, :] for e in range(2) for b in range(2)], axis=0
                     )
                     made = mm(q, w).astype(BF)
                     for i in range(2):
@@ -494,8 +556,8 @@
                 h = first + hl
                 w = jnp.concatenate(
                     [
-                        weights[xr, e, pl.ds(pl.multiple_of(512 + (zr * span + hl) * 16, 16), 16), :]
-                        for xr in range(4) for e in range(2) for zr in range(4)
+                        weights[e, b, pl.ds(pl.multiple_of(1024 + (c * span + hl) * 16, 16), 16), :]
+                        for e in range(2) for b in range(2) for c in range(8)
                     ],
                     axis=0,
                 )
@@ -516,14 +578,23 @@
 
 def mla(spot, q, latents, back_one, ahead_one, back_two, ahead_two, docs, own_w, other_w, xs):
     spec = pl.BlockSpec(memory_space=pltpu.VMEM)
+    hbm = pl.BlockSpec(memory_space=pltpu.HBM)
     rows = q.shape[0]
     return pl.pallas_call(
         functools.partial(mla_kernel, xs=xs),
         name="mla",
         out_shape=jax.ShapeDtypeStruct((rows, DN), BF),
-        in_specs=[pl.BlockSpec(memory_space=pltpu.SMEM)] + [spec] * 9,
+        in_specs=[pl.BlockSpec(memory_space=pltpu.SMEM), hbm, spec, hbm, hbm, hbm, hbm, spec, hbm, hbm],
         out_specs=spec,
         scratch_shapes=[
+            pltpu.VMEM((rows, DN), BF),
+            pltpu.VMEM((4 * HALF, DN), BF),
+            pltpu.VMEM((8 * HALF, DN), BF),
+            pltpu.VMEM((4 * HALF, DN), BF),
+            pltpu.VMEM((4 * HALF, DN), BF),
+            pltpu.VMEM(own_w.shape, BF),
+            pltpu.VMEM(own_w.shape, BF),
+            pltpu.SemaphoreType.DMA((7,)),
             pltpu.VMEM((rows, DN), F32),
             pltpu.VMEM((2, 256, 4 * DN), BF),
             pltpu.VMEM((2, 256, 4 * DN), BF),
@@ -532,7 +603,7 @@
             pltpu.VMEM((2, rows // 2, 4 * DN), BF),
             pltpu.VMEM((rows, DN), F32),
         ],
-        compiler_params=pltpu.CompilerParams(vmem_limit_bytes=40 << 20),
+        compiler_params=pltpu.CompilerParams(vmem_limit_bytes=60 << 20),
         cost_estimate=pl.CostEstimate(flops=1_500_000_000, bytes_accessed=7_000_000, transcendentals=600_000),
     )(spot, q, latents, back_one, ahead_one, back_two, ahead_two, docs, own_w, other_w)
 
@@ -583,19 +654,25 @@
         return lax.ppermute(value, "ctx", [(i, i ^ step) for i in range(ranks)])
 
     held = jnp.stack([held, across(held, 4 * XS)])
+    columns = [held]
+    for step in range(1, XS):
+        pairs = [(i - i % XS + (i + step) % XS, i) for i in range(ranks)]
+        columns.append(lax.ppermute(held, "ctx", pairs))
+    held = jnp.stack(columns)
+    lift_tiles = held[:, :, : span * 16].reshape(XS, 2, span, 4, 4, DN)
+    lift_tiles = lift_tiles.transpose(2, 3, 0, 1, 4, 5).reshape(span * 128, DN)
+    held = jnp.concatenate([lift_tiles, held[:, :, span * 16 :].reshape(span * 128, DN)], axis=0)
     held = jnp.stack([held, across(held, 2 * XS)])
-    lift_tiles = held[:, :, : span * 16].reshape(2, 2, span, 4, 4, DN)
-    lift_tiles = lift_tiles.transpose(2, 3, 0, 1, 4, 5).reshape(span * 64, DN)
-    held = jnp.concatenate([lift_tiles, held[:, :, span * 16 :].reshape(span * 64, DN)], axis=0)
-    held = jnp.stack([held, across(held, XS)])
+    own_w = jnp.stack([held, across(held, XS)])
+    other_w = lax.ppermute(own_w, "dp", [(i, i ^ 1) for i in range(groups)])
 
     lmat, att, rhs, leaving, closing, carried_q = kda_pairs(
         here,
         flat(delta_query_rows),
         flat(delta_key_rows),
         flat(delta_value_rows),
-        delta_write_strength[0],
-        token_gate_scale[0],
+        delta_write_strength[0].T,
+        token_gate_scale[0].T,
         channel_decay_rate,
         sudden_loss_mask,
         docs,
@@ -604,13 +681,6 @@
     offs_first, offs_second, tmap, upd = kda_leave(xmat, rhs, leaving, closing, latents)
     near_first = from_behind(offs_first, "ctx", 1)
     near_second = from_behind(offs_second, "ctx", -1)
-    columns = [held]
-    for step in range(1, XS):
-        pairs = [(i - i % XS + (i + step) % XS, i) for i in range(ranks)]
-        columns.append(lax.ppermute(held, "ctx", pairs))
-    own_w = jnp.stack(columns)
-    other_w = lax.ppermute(own_w, "dp", [(i, i ^ 1) for i in range(groups)])
-
     local, squery = kda_local(att, upd, carried_q)
     out_first, out_second = kda_carry(
         here, tmap, offs_first, offs_second, near_first, near_second, ranks
@@ -629,9 +699,10 @@
         ranks,
     )
     kda_output = normed_rows.reshape(seqs, rows, heads, value_width)
-    along = jnp.sum(lax.all_to_all(partial_grad, "ctx", 0, 0, tiled=True), axis=0)
-    spread = jnp.broadcast_to(along, (groups, value_width))
-    total_grad = jnp.sum(lax.all_to_all(spread, "dp", 0, 0, tiled=True), axis=0)
+    terms = lax.all_to_all(partial_grad, "ctx", 0, 0, tiled=True)
+    spread = jnp.broadcast_to(jnp.sum(terms, axis=0), (groups, value_width))
+    terms = lax.all_to_all(spread, "dp", 0, 0, tiled=True)
+    total_grad = jnp.sum(terms, axis=0)
     gain_grad = total_grad / math.sqrt(seqs * groups * rows * ranks * heads)
 
     spot = jnp.stack([place, core]).astype(jnp.int32)

time: 206 us -> 211 us (1.024)
  waiting for transfers between devices: 63.9 us -> 81.7 us
  local copies, waits for them, and re-layouts: 14.6 us -> 8.08 us
  Pallas kernels: 43.4 us -> 38 us
  blocking collectives: 21.6 us -> 24 us
    ppermute x3, waiting for transfers between devices: 14.2 us -> 48.4 us  [across(): return lax.ppermute(value, 'ctx', [(i, i ^ step) for i in range(ranks)])]
    ppermute x3, waiting for transfers between devices: 18.9 us -> 3.35 us  [shards(): columns.append(lax.ppermute(held, 'ctx', pairs))]
    unnamed x56 -> x50, local copies, waits for them, and re-layouts: 12.6 us -> 6.57 us
    pallas_call x1, Pallas kernels: 10.1 us -> 5.03 us  [kda_invert(): pl.pallas_call(kda_invert_kernel, name='kda_invert', out_shape=jax.ShapeD...]
    all_to_all x1, blocking collectives: 21.6 us -> 24 us  [shards(): terms = lax.all_to_all(partial_grad, 'ctx', 0, 0, tiled=True)]
    reduce_sum x2, other arithmetic: 2.46 us -> 0.07 us  [the longest x1 0.05 us: shards(): spread = jnp.broadcast_to(jnp.sum(terms, axis=0), (groups, value_width))]
  transfers between devices with their start and end apart: 12 -> 12, of which waited for: 11 -> 10; matrix products, arithmetic and copies ran while one was open for 3% -> 1% of each run, Pallas kernels for 14% -> 11%
where the time goes in v2:
time: 211 us; the launch traced here: 210 us
  waiting for transfers between devices  81.7 us (39%)
  starting transfers between devices  54.5 us (26%)
  Pallas kernels  38 us (18%)
  blocking collectives  24 us (11%)
  local copies, waits for them, and re-layouts  8.08 us (4%)
  other arithmetic  2.99 us (1%)
    ppermute x3, waiting for transfers between devices, across(): return lax.ppermute(value, 'ctx', [(i, i ^ step) for i in range(ranks)])  48.4 us
    all_to_all x1, blocking collectives, shards(): terms = lax.all_to_all(partial_grad, 'ctx', 0, 0, tiled=True)  24 us
    ppermute x4, waiting for transfers between devices, from_behind(): lax.ppermute(value, axis, [(source, source + steps) for source in range(l...  23.5 us
    ppermute x3, starting transfers between devices, across(): return lax.ppermute(value, 'ctx', [(i, i ^ step) for i in range(ranks)])  18.8 us
    pallas_call x1, Pallas kernels, mla(): pl.pallas_call(functools.partial(mla_kernel, xs=xs), name='mla', out_shap...  14.2 us
    all_to_all x1, starting transfers between devices, shards(): terms = lax.all_to_all(spread, 'dp', 0, 0, tiled=True)  10.9 us
    ppermute x4, starting transfers between devices, from_behind(): lax.ppermute(value, axis, [(source, source + steps) for source in range(l...  10.9 us
    ppermute x3, starting transfers between devices, shards(): columns.append(lax.ppermute(held, 'ctx', pairs))  10.5 us
  transfers between devices with their start and end apart: 12, of which 10 were waited for; matrix products, arithmetic and copies ran while one was open for 1% of the time, Pallas kernels for 11%

profile of v2, /device:TPU:1, one launch (start us, length us, event | category | flops | bytes accessed | tf_op | source)
XLA Modules:
  0.0 210.3 jit_solution(3199457208262333321)
XLA Ops:
  2.3 11.5 %collective-permute-start.4 = (bf16[256,128]{1,0:T(8,128)(2,1)S(1)}, bf16[256,128]{1,0:T(8,128)(2,1)S(1)}, u32[]{:S(2)}, u32[]{:S(2)}) collective-permute-start(bf16[256,128]{1,0:T(8,128)(2,1)S(1)} %get-tuple-element.44), channel_id=1, source_target_pairs={{0,16},{1,17},{2,18},{3,19},{4,20},{5,21},{6,22},{7,23},{8,24},{9,... | collective-permute-start | bytes 196616 | tf_op jit(solution)/shard_map/ppermute | solution.py:654
  15.5 3.1 %collective-permute-start.7 = (bf16[2,256,128]{2,1,0:T(8,128)(2,1)S(1)}, bf16[2,256,128]{2,1,0:T(8,128)(2,1)S(1)}, u32[]{:S(2)}, u32[]{:S(2)}) collective-permute-start(bf16[2,256,128]{2,1,0:T(8,128)(2,1)S(1)} %get-tuple-element.42), channel_id=1, source_target_pairs={{3,0},{0,1},{1,2},{2,3},{7,4},{4,5},{5,6},{6,7},{11,8},{8,9},{9,10... | collective-permute-start | bytes 393224 | tf_op jit(solution)/shard_map/ppermute | solution.py:660
  18.6 4.4 %collective-permute-start.6 = (bf16[2,256,128]{2,1,0:T(8,128)(2,1)S(1)}, bf16[2,256,128]{2,1,0:T(8,128)(2,1)S(1)}, u32[]{:S(2)}, u32[]{:S(2)}) collective-permute-start(bf16[2,256,128]{2,1,0:T(8,128)(2,1)S(1)} %get-tuple-element.42), channel_id=1, source_target_pairs={{2,0},{3,1},{0,2},{1,3},{6,4},{7,5},{4,6},{5,7},{10,8},{11,9},{8,1... | collective-permute-start | bytes 393224 | tf_op jit(solution)/shard_map/ppermute | solution.py:660
  23.0 3.1 %collective-permute-start.5 = (bf16[2,256,128]{2,1,0:T(8,128)(2,1)S(1)}, bf16[2,256,128]{2,1,0:T(8,128)(2,1)S(1)}, u32[]{:S(2)}, u32[]{:S(2)}) collective-permute-start(bf16[2,256,128]{2,1,0:T(8,128)(2,1)S(1)} %get-tuple-element.42), channel_id=1, source_target_pairs={{1,0},{2,1},{3,2},{0,3},{5,4},{6,5},{7,6},{4,7},{9,8},{10,9},{11,1... | collective-permute-start | bytes 393224 | tf_op jit(solution)/shard_map/ppermute | solution.py:660
  26.9 2.5 %collective-permute-done.5 = bf16[2,256,128]{2,1,0:T(8,128)(2,1)S(1)} collective-permute-done((bf16[2,256,128]{2,1,0:T(8,128)(2,1)S(1)}, bf16[2,256,128]{2,1,0:T(8,128)(2,1)S(1)}, u32[]{:S(2)}, u32[]{:S(2)}) %collective-permute-start.5) | collective-permute-done | bytes 131104 | tf_op jit(solution)/shard_map/ppermute | solution.py:660
  29.7 5.4 %collective-permute-start.8 = (bf16[2048,128]{1,0:T(8,128)(2,1)S(1)}, bf16[2048,128]{1,0:T(8,128)(2,1)S(1)}, u32[]{:S(2)}, u32[]{:S(2)}) collective-permute-start(bf16[2048,128]{1,0:T(8,128)(2,1)S(1)} %get-tuple-element.38), channel_id=1, source_target_pairs={{0,8},{1,9},{2,10},{3,11},{4,12},{5,13},{6,14},{7,15},{8,0},{9,1},... | collective-permute-start | bytes 1572872 | tf_op jit(solution)/shard_map/ppermute | solution.py:654
  35.1 22.5 %collective-permute-done.8 = bf16[2048,128]{1,0:T(8,128)(2,1)S(1)} collective-permute-done((bf16[2048,128]{1,0:T(8,128)(2,1)S(1)}, bf16[2048,128]{1,0:T(8,128)(2,1)S(1)}, u32[]{:S(2)}, u32[]{:S(2)}) %collective-permute-start.8) | collective-permute-done | bytes 524320 | tf_op jit(solution)/shard_map/ppermute | solution.py:654
  59.8 24.2 %collective-permute-done.9 = bf16[2,2048,128]{2,1,0:T(8,128)(2,1)S(1)} collective-permute-done((bf16[2,2048,128]{2,1,0:T(8,128)(2,1)S(1)}, bf16[2,2048,128]{2,1,0:T(8,128)(2,1)S(1)}, u32[]{:S(2)}, u32[]{:S(2)}) %collective-permute-start.9) | collective-permute-done | bytes 1048608 | tf_op jit(solution)/shard_map/ppermute | solution.py:654
  85.6 3.4 %collective-permute-start.10 = (bf16[2,2,2048,128]{3,2,1,0:T(8,128)(2,1)}, bf16[2,2,2048,128]{3,2,1,0:T(8,128)(2,1)}, u32[]{:S(2)}, u32[]{:S(2)}) collective-permute-start(bf16[2,2,2048,128]{3,2,1,0:T(8,128)(2,1)} %pad_maximum_fusion.own_hbm), channel_id=1, source_target_pairs={{0,32},{32,0},{64,96},{96,64},{128,160},{160,128},{192,224},{224,1... | collective-permute-start | bytes 6291464 | tf_op jit(solution)/shard_map/ppermute | solution.py:667
  89.0 5.6 %kda_pairs.1 = (f32[32,64,64]{2,1,0:T(8,128)S(1)}, bf16[32,64,64]{2,1,0:T(8,128)(2,1)S(1)}, bf16[32,64,256]{2,1,0:T(8,128)(2,1)S(1)}, bf16[32,64,128]{2,1,0:T(8,...) custom-call(s32[1]{0:T(128)} %bitcast.place_ref, bf16[2048,128]{1,0:T(8,128)(2,1)S(1)} %bitcast.49, ...), custom_call_target="tpu_custom_call" | custom-call | flops 300000000 | bytes 12000000 | tf_op jit(solution)/shard_map/kda_pairs/pallas_call | solution.py:148
  94.7 5.0 %kda_invert.1.xmat = f32[32,64,64]{2,1,0:T(8,128)S(1)} custom-call(f32[32,64,64]{2,1,0:T(8,128)S(1)} %get-tuple-element.20.lmat), custom_call_target="tpu_custom_call" | custom-call | flops 300000000 | bytes 12000000 | tf_op jit(solution)/shard_map/kda_invert/pallas_call | solution.py:227
  99.7 2.9 %kda_leave.1 = (bf16[2304,128]{1,0:T(8,128)(2,1)S(1)}, bf16[2560,128]{1,0:T(8,128)(2,1)S(1)}, bf16[32,128,128]{2,1,0:T(8,128)(2,1)S(1)}, bf16[32,64,256]{2,1,0:T(8,128)(2,1)S(1)}) custom-call(f32[32,64,64]{2,1,0:T(8,128)S(1)} %kda_invert.1.xmat, bf16[32,64,256]{2,1,0:T(8,128)(2,1)S(1)} %get-tuple-element.21.rhs, ...), custom_call_target="tpu_custom_call" | custom-call | flops 300000000 | bytes 8000000 | tf_op jit(solution)/shard_map/kda_leave/pallas_call | solution.py:282
  106.0 4.0 %collective-permute-start = (bf16[2304,128]{1,0:T(8,128)(2,1)S(1)}, bf16[2304,128]{1,0:T(8,128)(2,1)S(1)}, u32[]{:S(2)}, u32[]{:S(2)}) collective-permute-start(bf16[2304,128]{1,0:T(8,128)(2,1)S(1)} %get-tuple-element.29.offs_first), channel_id=1, source_target_pairs={{0,1},{1,2},{2,3},{3,4},{4,5},{5,6},{6,7},{7,8},{8,9},{9,10},{10,1... | collective-permute-start | bytes 1769480 | tf_op jit(solution)/shard_map/ppermute | solution.py:614
  110.0 12.3 %collective-permute-done.in_first.back_one_hbm = bf16[2304,128]{1,0:T(8,128)(2,1)S(1)} collective-permute-done((bf16[2304,128]{1,0:T(8,128)(2,1)S(1)}, bf16[2304,128]{1,0:T(8,128)(2,1)S(1)}, u32[]{:S(2)}, u32[]{:S(2)}) %collective-permute-start) | collective-permute-done | bytes 589856 | tf_op jit(solution)/shard_map/ppermute | solution.py:614
  124.0 4.0 %kda_carry.1 = (bf16[2304,128]{1,0:T(8,128)(2,1)}, bf16[2304,128]{1,0:T(8,128)(2,1)}) custom-call(s32[1]{0:T(128)} %bitcast.place_ref, bf16[32,128,128]{2,1,0:T(8,128)(2,1)} %copy-done.4, bf16[2304,128]{1,0:T(8,128)(2,1)} %copy-done.8, bf16[2560,128]{1,0:T(8,128)(2,1)} %copy-done.6, bf16[2304,128]{1,0:T(8,128)(2,1)} %copy-done.24, bf16[2560,128]{1,0:T(8,128)(2,1)} %copy-done.23), custom_call_target="tpu_custom_call" | custom-call | flops 130000000 | bytes 5000000 | tf_op jit(solution)/shard_map/kda_carry/pallas_call | solution.py:345
  128.1 4.3 %collective-permute-start.2 = (bf16[2304,128]{1,0:T(8,128)(2,1)}, bf16[2304,128]{1,0:T(8,128)(2,1)S(1)}, u32[]{:S(2)}, u32[]{:S(2)}) collective-permute-start(bf16[2304,128]{1,0:T(8,128)(2,1)} %get-tuple-element.31.own_first), channel_id=1, source_target_pairs={{0,1},{1,2},{2,3},{3,4},{4,5},{5,6},{6,7},{7,8},{8,9},{9,10},{10,1... | collective-permute-start | bytes 1769480 | tf_op jit(solution)/shard_map/ppermute | solution.py:614
  133.6 3.5 %kda_local.1 = (f32[32,64,128]{2,1,0:T(8,128)}, bf16[32,64,128]{2,1,0:T(8,128)(2,1)}) custom-call(bf16[32,64,64]{2,1,0:T(8,128)(2,1)} %copy-done.14, bf16[32,64,256]{2,1,0:T(8,128)(2,1)} %copy-done.3, bf16[32,64,128]{2,1,0:T(8,128)(2,1)} %copy-done.15), custom_call_target="tpu_custom_call" | custom-call | flops 70000000 | bytes 4000000 | tf_op jit(solution)/shard_map/kda_local/pallas_call | solution.py:310
  137.2 7.0 %collective-permute-done.2.in_first.back_two_hbm = bf16[2304,128]{1,0:T(8,128)(2,1)S(1)} collective-permute-done((bf16[2304,128]{1,0:T(8,128)(2,1)}, bf16[2304,128]{1,0:T(8,128)(2,1)S(1)}, u32[]{:S(2)}, u32[]{:S(2)}) %collective-permute-start.2) | collective-permute-done | bytes 589856 | tf_op jit(solution)/shard_map/ppermute | solution.py:614
  144.1 3.8 %collective-permute-done.3.in_second.ahead_two_hbm = bf16[2304,128]{1,0:T(8,128)(2,1)S(1)} collective-permute-done((bf16[2304,128]{1,0:T(8,128)(2,1)}, bf16[2304,128]{1,0:T(8,128)(2,1)S(1)}, u32[]{:S(2)}, u32[]{:S(2)}) %collective-permute-start.3) | collective-permute-done | bytes 589856 | tf_op jit(solution)/shard_map/ppermute | solution.py:614
  150.4 2.6 %kda_close.1 = (bf16[2048,128]{1,0:T(8,128)(2,1)}, f32[32,128]{1,0:T(8,128)S(1)}) custom-call(s32[1]{0:T(128)} %bitcast.place_ref, f32[32,64,128]{2,1,0:T(8,128)S(1)} %copy-done.5, bf16[32,64,128]{2,1,0:T(8,128)(2,1)S(1)} %copy-done.16, bf16[2304,128]{1,0:T(8,128)(2,1)S(1)} %copy-done.7, bf16[2304,128]{1,0:T(8,128)(2,1)S(1)} %collective-permute-done.2.in_first.back_two_hbm, ...), custom_call_target="tpu_custom_call" | custom-call | flops 70000000 | bytes 5000000 | tf_op jit(solution)/shard_map/kda_close/pallas_call | solution.py:401
  153.0 24.0 %all_to_all.15 = f32[32,1,128]{2,1,0:T(1,128)S(1)} all-to-all(f32[32,1,128]{2,1,0:T(1,128)S(1)} %bitcast.55), channel_id=1, replica_groups=mesh['dp'=16,'ctx'=32] {'ctx'}, dimensions={0} | all-to-all | bytes 32768 | tf_op jit(solution)/shard_map/all_to_all | solution.py:702
  177.7 10.9 %all-to-all-start.1 = ((f32[16,1,128]{2,1,0:T(1,128)}), f32[16,1,128]{2,1,0:T(1,128)S(1)}, u32[]{:S(2)}, u32[]{:S(2)}) async-start(f32[16,1,128]{2,1,0:T(1,128)} %broadcast_in_dim.3), calls=%async_computation.1 | async-start | bytes 16384 | tf_op jit(solution)/shard_map/all_to_all | solution.py:704
  189.1 6.4 %all-to-all-done.1 = f32[16,1,128]{2,1,0:T(1,128)S(1)} async-done(((f32[16,1,128]{2,1,0:T(1,128)}), f32[16,1,128]{2,1,0:T(1,128)S(1)}, u32[]{:S(2)}, u32[]{:S(2)}) %all-to-all-start.1) | async-done | bytes 8224 | tf_op jit(solution)/shard_map/all_to_all | solution.py:704
  196.1 14.2 %mla.1 = bf16[2048,128]{1,0:T(8,128)(2,1)} custom-call(s32[2]{0:T(128)} %pad_add_fusion.spot_ref, bf16[2048,128]{1,0:T(8,128)(2,1)} %bitcast.63, bf16[128,512]{1,0:T(8,128)(2,1)} %bitcast.47, bf16[2304,128]{1,0:T(8,128)(2,1)} %copy-done.24, bf16[2560,128]{1,0:T(8,128)(2,1)} %copy-done.23, bf16[2304,128]{1,0:T(8,128)(2,1)} %copy-done.1, ...), custom_call_target="tpu_custom_call" | custom-call | flops 1500000000 | bytes 7000000 | tf_op jit(solution)/shard_map/mla/pallas_call | solution.py:583
  (73 shorter events, 18.6 us)
Async XLA Ops:
  2.3 13.2 %collective-permute-start.4 = (bf16[256,128]{1,0:T(8,128)(2,1)S(1)}, bf16[256,128]{1,0:T(8,128)(2,1)S(1)}, u32[]{:S(2)}, u32[]{:S(2)}) collective-permute-start(bf16[256,128]{1,0:T(8,128)(2,1)S(1)} %get-tuple-element.44), channel_id=1, source_target_pairs={{0,16},{1,17},{2,18},{3,19},{4,20},{5,21},{6,22},{7,23},{8,24},{9,... | collective-permute-start | bytes 196616 | tf_op jit(solution)/shard_map/ppermute | solution.py:654
  15.5 10.6 %collective-permute-start.7 = (bf16[2,256,128]{2,1,0:T(8,128)(2,1)S(1)}, bf16[2,256,128]{2,1,0:T(8,128)(2,1)S(1)}, u32[]{:S(2)}, u32[]{:S(2)}) collective-permute-start(bf16[2,256,128]{2,1,0:T(8,128)(2,1)S(1)} %get-tuple-element.42), channel_id=1, source_target_pairs={{3,0},{0,1},{1,2},{2,3},{7,4},{4,5},{5,6},{6,7},{11,8},{8,9},{9,10... | collective-permute-start | bytes 393224 | tf_op jit(solution)/shard_map/ppermute | solution.py:660
  18.6 8.3 %collective-permute-start.6 = (bf16[2,256,128]{2,1,0:T(8,128)(2,1)S(1)}, bf16[2,256,128]{2,1,0:T(8,128)(2,1)S(1)}, u32[]{:S(2)}, u32[]{:S(2)}) collective-permute-start(bf16[2,256,128]{2,1,0:T(8,128)(2,1)S(1)} %get-tuple-element.42), channel_id=1, source_target_pairs={{2,0},{3,1},{0,2},{1,3},{6,4},{7,5},{4,6},{5,7},{10,8},{11,9},{8,1... | collective-permute-start | bytes 393224 | tf_op jit(solution)/shard_map/ppermute | solution.py:660
  23.0 6.4 %collective-permute-start.5 = (bf16[2,256,128]{2,1,0:T(8,128)(2,1)S(1)}, bf16[2,256,128]{2,1,0:T(8,128)(2,1)S(1)}, u32[]{:S(2)}, u32[]{:S(2)}) collective-permute-start(bf16[2,256,128]{2,1,0:T(8,128)(2,1)S(1)} %get-tuple-element.42), channel_id=1, source_target_pairs={{1,0},{2,1},{3,2},{0,3},{5,4},{6,5},{7,6},{4,7},{9,8},{10,9},{11,1... | collective-permute-start | bytes 393224 | tf_op jit(solution)/shard_map/ppermute | solution.py:660
  29.7 28.0 %collective-permute-start.8 = (bf16[2048,128]{1,0:T(8,128)(2,1)S(1)}, bf16[2048,128]{1,0:T(8,128)(2,1)S(1)}, u32[]{:S(2)}, u32[]{:S(2)}) collective-permute-start(bf16[2048,128]{1,0:T(8,128)(2,1)S(1)} %get-tuple-element.38), channel_id=1, source_target_pairs={{0,8},{1,9},{2,10},{3,11},{4,12},{5,13},{6,14},{7,15},{8,0},{9,1},... | collective-permute-start | bytes 1572872 | tf_op jit(solution)/shard_map/ppermute | solution.py:654
  57.8 26.1 %collective-permute-start.9 = (bf16[2,2048,128]{2,1,0:T(8,128)(2,1)S(1)}, bf16[2,2048,128]{2,1,0:T(8,128)(2,1)S(1)}, u32[]{:S(2)}, u32[]{:S(2)}) collective-permute-start(bf16[2,2048,128]{2,1,0:T(8,128)(2,1)S(1)} %get-tuple-element.36), channel_id=1, source_target_pairs={{0,4},{1,5},{2,6},{3,7},{4,0},{5,1},{6,2},{7,3},{8,12},{9,13},{10,... | collective-permute-start | bytes 3145736 | tf_op jit(solution)/shard_map/ppermute | solution.py:654
  84.0 5.0 %copy-start.18 = (f32[1,128,16]{1,2,0:T(8,128)S(1)}, f32[1,128,16]{1,2,0:T(8,128)}, u32[]{:S(2)}) copy-start(f32[1,128,16]{1,2,0:T(8,128)} %param.17) | copy-start | bytes 24580
  84.0 5.0 %copy-start.19 = (f32[1,128,16]{1,2,0:T(8,128)S(1)}, f32[1,128,16]{1,2,0:T(8,128)}, u32[]{:S(2)}) copy-start(f32[1,128,16]{1,2,0:T(8,128)} %param.18) | copy-start | bytes 24580
  85.6 14.2 %copy-start.9 = (bf16[1,128,512]{2,1,0:T(8,128)(2,1)S(1)}, bf16[1,128,512]{2,1,0:T(8,128)(2,1)}, u32[]{:S(2)}) copy-start(bf16[1,128,512]{2,1,0:T(8,128)(2,1)} %param.25) | copy-start | bytes 393220
  85.6 110.5 %collective-permute-start.10 = (bf16[2,2,2048,128]{3,2,1,0:T(8,128)(2,1)}, bf16[2,2,2048,128]{3,2,1,0:T(8,128)(2,1)}, u32[]{:S(2)}, u32[]{:S(2)}) collective-permute-start(bf16[2,2,2048,128]{3,2,1,0:T(8,128)(2,1)} %pad_maximum_fusion.own_hbm), channel_id=1, source_target_pairs={{0,32},{32,0},{64,96},{96,64},{128,160},{160,128},{192,224},{224,1... | collective-permute-start | bytes 6291464 | tf_op jit(solution)/shard_map/ppermute | solution.py:667
  94.7 8.0 %copy-start.14 = (bf16[32,64,64]{2,1,0:T(8,128)(2,1)}, bf16[32,64,64]{2,1,0:T(8,128)(2,1)S(1)}, u32[]{:S(2)}) copy-start(bf16[32,64,64]{2,1,0:T(8,128)(2,1)S(1)} %get-tuple-element.19.att) | copy-start | bytes 786436
  94.7 8.0 %copy-start.15 = (bf16[32,64,128]{2,1,0:T(8,128)(2,1)}, bf16[32,64,128]{2,1,0:T(8,128)(2,1)S(1)}, u32[]{:S(2)}) copy-start(bf16[32,64,128]{2,1,0:T(8,128)(2,1)S(1)} %get-tuple-element.25.carried_q) | copy-start | bytes 1572868
  104.7 18.5 %copy-start.6 = (bf16[2560,128]{1,0:T(8,128)(2,1)}, bf16[2560,128]{1,0:T(8,128)(2,1)S(1)}, u32[]{:S(2)}) copy-start(bf16[2560,128]{1,0:T(8,128)(2,1)S(1)} %get-tuple-element.30.offs_second) | copy-start | bytes 1966084
  104.7 18.5 %copy-start.8 = (bf16[2304,128]{1,0:T(8,128)(2,1)}, bf16[2304,128]{1,0:T(8,128)(2,1)S(1)}, u32[]{:S(2)}) copy-start(bf16[2304,128]{1,0:T(8,128)(2,1)S(1)} %get-tuple-element.29.offs_first) | copy-start | bytes 1769476
  104.7 18.1 %collective-permute-start.1 = (bf16[2560,128]{1,0:T(8,128)(2,1)S(1)}, bf16[2560,128]{1,0:T(8,128)(2,1)S(1)}, u32[]{:S(2)}, u32[]{:S(2)}) collective-permute-start(bf16[2560,128]{1,0:T(8,128)(2,1)S(1)} %get-tuple-element.30.offs_second), channel_id=1, source_target_pairs={{1,0},{2,1},{3,2},{4,3},{5,4},{6,5},{7,6},{8,7},{9,8},{10,9},{11,1... | collective-permute-start | bytes 1966088 | tf_op jit(solution)/shard_map/ppermute | solution.py:614
  106.0 16.4 %collective-permute-start = (bf16[2304,128]{1,0:T(8,128)(2,1)S(1)}, bf16[2304,128]{1,0:T(8,128)(2,1)S(1)}, u32[]{:S(2)}, u32[]{:S(2)}) collective-permute-start(bf16[2304,128]{1,0:T(8,128)(2,1)S(1)} %get-tuple-element.29.offs_first), channel_id=1, source_target_pairs={{0,1},{1,2},{2,3},{3,4},{4,5},{5,6},{6,7},{7,8},{8,9},{9,10},{10,1... | collective-permute-start | bytes 1769480 | tf_op jit(solution)/shard_map/ppermute | solution.py:614
  124.0 23.8 %copy-start.13 = (bf16[1,128,16,128]{3,2,1,0:T(8,128)(2,1)S(1)}, bf16[1,128,16,128]{3,2,1,0:T(8,128)(2,1)}, u32[]{:S(2)}) copy-start(bf16[1,128,16,128]{3,2,1,0:T(8,128)(2,1)} %param.23) | copy-start | bytes 1572868
  124.0 23.8 %copy-start.22 = (f32[128]{0:T(128)S(1)}, f32[128]{0:T(128)}, u32[]{:S(2)}) copy-start(f32[128]{0:T(128)} %param.22) | copy-start | bytes 1540
  128.0 19.8 %copy-start.7 = (bf16[2304,128]{1,0:T(8,128)(2,1)S(1)}, bf16[2304,128]{1,0:T(8,128)(2,1)}, u32[]{:S(2)}) copy-start(bf16[2304,128]{1,0:T(8,128)(2,1)} %get-tuple-element.31.own_first) | copy-start | bytes 1769476
  128.1 16.1 %collective-permute-start.2 = (bf16[2304,128]{1,0:T(8,128)(2,1)}, bf16[2304,128]{1,0:T(8,128)(2,1)S(1)}, u32[]{:S(2)}, u32[]{:S(2)}) collective-permute-start(bf16[2304,128]{1,0:T(8,128)(2,1)} %get-tuple-element.31.own_first), channel_id=1, source_target_pairs={{0,1},{1,2},{2,3},{3,4},{4,5},{5,6},{6,7},{7,8},{8,9},{9,10},{10,1... | collective-permute-start | bytes 1769480 | tf_op jit(solution)/shard_map/ppermute | solution.py:614
  132.3 15.5 %collective-permute-start.3 = (bf16[2304,128]{1,0:T(8,128)(2,1)}, bf16[2304,128]{1,0:T(8,128)(2,1)S(1)}, u32[]{:S(2)}, u32[]{:S(2)}) collective-permute-start(bf16[2304,128]{1,0:T(8,128)(2,1)} %get-tuple-element.32), channel_id=1, source_target_pairs={{1,0},{2,1},{3,2},{4,3},{5,4},{6,5},{7,6},{8,7},{9,8},{10,9},{11,1... | collective-permute-start | bytes 1769480 | tf_op jit(solution)/shard_map/ppermute | solution.py:614
  144.1 52.0 %copy-start.1 = (bf16[2304,128]{1,0:T(8,128)(2,1)}, bf16[2304,128]{1,0:T(8,128)(2,1)S(1)}, u32[]{:S(2)}) copy-start(bf16[2304,128]{1,0:T(8,128)(2,1)S(1)} %collective-permute-done.2.in_first.back_two_hbm) | copy-start | bytes 1769476
  147.9 48.2 %copy-start.2 = (bf16[2304,128]{1,0:T(8,128)(2,1)}, bf16[2304,128]{1,0:T(8,128)(2,1)S(1)}, u32[]{:S(2)}) copy-start(bf16[2304,128]{1,0:T(8,128)(2,1)S(1)} %collective-permute-done.3.in_second.ahead_two_hbm) | copy-start | bytes 1769476
  177.7 17.9 %all-to-all-start.1 = ((f32[16,1,128]{2,1,0:T(1,128)}), f32[16,1,128]{2,1,0:T(1,128)S(1)}, u32[]{:S(2)}, u32[]{:S(2)}) async-start(f32[16,1,128]{2,1,0:T(1,128)} %broadcast_in_dim.3), calls=%async_computation.1 | async-start | bytes 16384 | tf_op jit(solution)/shard_map/all_to_all | solution.py:704
  (13 other events, 37.2 us)

commit v3 on v2

--- a/solution.py
+++ b/solution.py
@@ -161,7 +161,7 @@
             vm(2, HALF, DN), vm(2, HALF, DN), vm(2, HALF, DN),
             vm(2, HALF, HALF), vm(2, HALF, HALF),
         ],
-        compiler_params=pltpu.CompilerParams(vmem_limit_bytes=32 << 20),
+        compiler_params=pltpu.CompilerParams(vmem_limit_bytes=60 << 20),
         cost_estimate=pl.CostEstimate(flops=300_000_000, bytes_accessed=12_000_000, transcendentals=600_000),
     )(place, q, k, v, w, scale, rate, mask, docs)
 
@@ -236,15 +236,8 @@
     )(lmat)
 
 
-def kda_leave_kernel(xmat, rhs, leaving, closing, lat_ref, offs_first, offs_second, tmap, upd):
+def kda_leave_kernel(xmat, rhs, leaving, closing, offs_first, offs_second, tmap, upd):
     heads = xmat.shape[0] // 2
-    base_row = heads * DN
-    for lb in range(4):
-        part = lat_ref[:, lb * DN : (lb + 1) * DN]
-        low = base_row + lb * HALF
-        offs_first[low : low + HALF, :] = part[:HALF]
-        offs_second[low : low + HALF, :] = part[:HALF]
-        offs_second[low + 4 * HALF : low + 5 * HALF, :] = part[HALF:]
 
     def solve(g, _):
         for u in range(8):
@@ -270,12 +263,12 @@
         lax.fori_loop(0, heads // 4, leave, 0)
 
 
-def kda_leave(xmat, rhs, leaving, closing, latents):
+def kda_leave(xmat, rhs, leaving, closing):
     n = xmat.shape[0]
     spec = pl.BlockSpec(memory_space=pltpu.VMEM)
     shapes = (
-        jax.ShapeDtypeStruct((n // 2 * DN + 4 * HALF, DN), BF),
-        jax.ShapeDtypeStruct((n // 2 * DN + 8 * HALF, DN), BF),
+        jax.ShapeDtypeStruct((n // 2 * DN, DN), BF),
+        jax.ShapeDtypeStruct((n // 2 * DN, DN), BF),
         jax.ShapeDtypeStruct((n, DN, DN), BF),
         jax.ShapeDtypeStruct((n, HALF, 2 * DN), BF),
     )
@@ -283,11 +276,11 @@
         kda_leave_kernel,
         name="kda_leave",
         out_shape=shapes,
-        in_specs=[spec] * 5,
+        in_specs=[spec] * 4,
         out_specs=(spec,) * 4,
         compiler_params=pltpu.CompilerParams(vmem_limit_bytes=24 << 20),
         cost_estimate=pl.CostEstimate(flops=300_000_000, bytes_accessed=8_000_000, transcendentals=0),
-    )(xmat, rhs, leaving, closing, latents)
+    )(xmat, rhs, leaving, closing)
 
 
 def kda_local_kernel(att, upd, carried_q, local, squery):
@@ -320,9 +313,6 @@
 def kda_carry_kernel(place_ref, tmap, offs_first, offs_second, in_first, in_second, out_first, out_second, *, ranks):
     heads = tmap.shape[0] // 2
     end = jnp.full((DN, DN), place_ref[0], jnp.int32) == ranks - 1
-    low = heads * DN
-    out_first[low:, :] = in_first[low:, :]
-    out_second[low:, :] = in_second[low + 4 * HALF :, :]
 
     def body(g, _):
         for u in range(4):
@@ -423,21 +413,18 @@
     ranks = docs_ref.shape[0]
     place, core = spot_ref[0], spot_ref[1]
     heads = q_ref.shape[0] // (2 * HALF)
-    low = heads * DN
-    quarter = pl.ds(low, 4 * HALF)
     moves = (
         (q_hbm, q_ref),
-        (back_two_hbm.at[quarter, :], back_two),
-        (back_one_hbm.at[quarter, :], back_one),
-        (ahead_two_hbm.at[quarter, :], ahead_two),
-        (ahead_one_hbm.at[pl.ds(low, 8 * HALF), :], ahead_one),
+        (back_two_hbm.at[pl.ds(4 * HALF, 4 * HALF), :], back_two),
+        (back_one_hbm.at[pl.ds(8 * HALF, 4 * HALF), :], back_one),
+        (ahead_two_hbm.at[pl.ds(4 * HALF, 4 * HALF), :], ahead_two),
+        (ahead_one_hbm.at[pl.ds(8 * HALF, 8 * HALF), :], ahead_one),
         (own_hbm, own_w),
         (other_hbm, other_w),
     )
     copies = [pltpu.make_async_copy(a, b, sems.at[n]) for n, (a, b) in enumerate(moves)]
     for copy in copies:
         copy.start()
-    here_z, here_x = place // xs, place % xs
     width = keys.shape[1]
 
     def piece(ref, at, i, slot):
@@ -473,14 +460,14 @@
         piece(ahead_one, 4 * HALF, 1, 1)
 
     def source_n(k):
-        off = ((k // 4) % 2) * 4 + ((k // 32) % 2) * 2 + k // 64
-        z = lax.bitwise_xor(off, jnp.full(k.shape, here_z, jnp.int32))
-        return (z * xs + ((k // 8) % xs + here_x) % xs) * 4 + k % 4
+        turn, column = k // 64 + 2 * ((k // 32) % 2) + 4 * ((k // 4) % 2), (k // 8) % xs
+        shift = jnp.where(column == xs - 1, -1, column) + xs * turn
+        return ((shift + place + ranks) % ranks) * 4 + k % 4
 
     def source_l(k):
-        off = ((k // 16) % 2) * 4 + ((k // 128) % 2) * 2 + k // 256
-        z = lax.bitwise_xor(off, jnp.full(k.shape, here_z, jnp.int32))
-        return (z * xs + ((k // 32) % xs + here_x) % xs) * 16 + k % 16
+        turn, column = 7 * (k // 256) + 6 * ((k // 128) % 2) + 4 * ((k // 16) % 2), (k // 32) % xs
+        shift = jnp.where(column >= xs // 2, column - xs, column) + xs * turn
+        return ((shift + place + ranks) % ranks) * 16 + k % 16
 
     pick = onehot((DN, DN), source_n)
     rows = 256
@@ -523,7 +510,7 @@
                 for lb in range(4):
                     at = pl.ds(pl.multiple_of((hl * 4 + lb) * 32, 32), 32)
                     w = jnp.concatenate(
-                        [weights[e, b, at, :] for e in range(2) for b in range(2)], axis=0
+                        [weights[0, e, b, at, :] for e in range(2) for b in range(2)], axis=0
                     )
                     made = mm(q, w).astype(BF)
                     for i in range(2):
@@ -556,7 +543,7 @@
                 h = first + hl
                 w = jnp.concatenate(
                     [
-                        weights[e, b, pl.ds(pl.multiple_of(1024 + (c * span + hl) * 16, 16), 16), :]
+                        weights[1, e, b, pl.ds(pl.multiple_of((c * span + hl) * 16, 16), 16), :]
                         for e in range(2) for b in range(2) for c in range(8)
                     ],
                     axis=0,
@@ -647,23 +634,31 @@
     span = heads // 2
     keep_lift = lax.dynamic_slice_in_dim(query_to_latent_map, core * span, span, 0)
     keep_lower = lax.dynamic_slice_in_dim(latent_to_value_map, core * span, span, 0)
-    lift_rows = keep_lift.reshape(span, 4, 4, DN).transpose(0, 2, 1, 3).reshape(span * 16, DN)
-    held = jnp.concatenate([lift_rows, keep_lower.reshape(span * 16, DN)], axis=0)
-
-    def across(value, step):
-        return lax.ppermute(value, "ctx", [(i, i ^ step) for i in range(ranks)])
-
-    held = jnp.stack([held, across(held, 4 * XS)])
-    columns = [held]
-    for step in range(1, XS):
-        pairs = [(i - i % XS + (i + step) % XS, i) for i in range(ranks)]
-        columns.append(lax.ppermute(held, "ctx", pairs))
-    held = jnp.stack(columns)
-    lift_tiles = held[:, :, : span * 16].reshape(XS, 2, span, 4, 4, DN)
-    lift_tiles = lift_tiles.transpose(2, 3, 0, 1, 4, 5).reshape(span * 128, DN)
-    held = jnp.concatenate([lift_tiles, held[:, :, span * 16 :].reshape(span * 128, DN)], axis=0)
-    held = jnp.stack([held, across(held, 2 * XS)])
-    own_w = jnp.stack([held, across(held, XS)])
+    lift = keep_lift.reshape(span, 4, 4, DN).transpose(0, 2, 1, 3).reshape(span * 16, DN)
+    lower = keep_lower.reshape(span * 16, DN)
+
+    def shifted(value, step):
+        return lax.ppermute(value, "ctx", [((i + step) % ranks, i) for i in range(ranks)])
+
+    across = shifted(jnp.concatenate([lift, lower], axis=0), XS * ranks // (2 * XS))
+    lift = jnp.concatenate([lift, across[: span * 16]], axis=0)
+    lower = jnp.concatenate([lower, across[span * 16 :]], axis=0)
+    tiles = latents.reshape(2, HALF, 4, DN).transpose(0, 2, 1, 3).reshape(2, 4 * HALF, DN)
+    ahead_one = shifted(jnp.concatenate([lift, lower, tiles[0], tiles[1]], axis=0), 1)
+    back_one = shifted(jnp.concatenate([lift, lower, tiles[0]], axis=0), -1)
+    ahead_two = shifted(jnp.concatenate([lift, tiles[1]], axis=0), 2)
+    back_two = shifted(jnp.concatenate([lower, tiles[0]], axis=0), -2)
+    many = span * 32
+    lift = jnp.stack([lift, ahead_one[:many], ahead_two[:many], back_one[:many]])
+    lift = lift.reshape(XS, 2, span, 4, 4, DN).transpose(2, 3, 0, 1, 4, 5).reshape(XS * many, DN)
+    lower = jnp.concatenate(
+        [lower, ahead_one[many : 2 * many], back_two[:many], back_one[many : 2 * many]], axis=0
+    )
+    lift = jnp.stack([lift, shifted(lift, 2 * XS)])
+    lower = jnp.stack([lower, shifted(lower, -2 * XS)])
+    lift = jnp.stack([lift, shifted(lift, XS)])
+    lower = jnp.stack([lower, shifted(lower, -XS)])
+    own_w = jnp.stack([lift, lower])
     other_w = lax.ppermute(own_w, "dp", [(i, i ^ 1) for i in range(groups)])
 
     lmat, att, rhs, leaving, closing, carried_q = kda_pairs(
@@ -678,7 +673,7 @@
         docs,
     )
     xmat = kda_invert(lmat)
-    offs_first, offs_second, tmap, upd = kda_leave(xmat, rhs, leaving, closing, latents)
+    offs_first, offs_second, tmap, upd = kda_leave(xmat, rhs, leaving, closing)
     near_first = from_behind(offs_first, "ctx", 1)
     near_second = from_behind(offs_second, "ctx", -1)
     local, squery = kda_local(att, upd, carried_q)
@@ -710,10 +705,10 @@
         spot,
         flat(latent_query_rows),
         latents,
-        near_first,
-        near_second,
-        far_first,
-        far_second,
+        back_one,
+        ahead_one,
+        back_two,
+        ahead_two,
         docs,
         own_w,
         other_w,

time: 211 us -> 197 us (0.934)
  waiting for transfers between devices: 81.7 us -> 52.9 us
  starting transfers between devices: 54.5 us -> 66.9 us
  Pallas kernels: 38 us -> 40.9 us
  blocking collectives: 24 us -> 21.1 us
    ppermute x6 -> x9, waiting for transfers between devices: 51.8 us -> 22 us  [shifted(): lax.ppermute(value, 'ctx', [((i + step) % ranks, i) for i in range(ranks)])]
    ppermute x6 -> x9, starting transfers between devices: 29.4 us -> 47.8 us  [shifted(): lax.ppermute(value, 'ctx', [((i + step) % ranks, i) for i in range(ranks)])]
    ppermute x4, starting transfers between devices: 10.9 us -> 5.34 us  [from_behind(): lax.ppermute(value, axis, [(source, source + steps) for source in range(l...]
    pallas_call x1, Pallas kernels: 5.62 us -> 8.81 us  [kda_pairs(): pl.pallas_call(kda_pairs_kernel, name='kda_pairs', out_shape=shapes, in_s...]
    all_to_all x1, blocking collectives: 24 us -> 21.1 us  [shards(): terms = lax.all_to_all(partial_grad, 'ctx', 0, 0, tiled=True)]
    unnamed x50 -> x46, local copies, waits for them, and re-layouts: 6.57 us -> 7.31 us
  transfers between devices with their start and end apart: 12 -> 15, of which waited for: 10 -> 11; matrix products, arithmetic and copies ran while one was open for 1% -> 2% of each run, Pallas kernels for 11% -> 14%
where the time goes in v3:
time: 197 us; the launch traced here: 196 us
  starting transfers between devices  66.9 us (34%)
  waiting for transfers between devices  52.9 us (27%)
  Pallas kernels  40.9 us (21%)
  blocking collectives  21.1 us (11%)
  local copies, waits for them, and re-layouts  9.81 us (5%)
  other arithmetic  3.33 us (2%)
    ppermute x9, starting transfers between devices, shifted(): lax.ppermute(value, 'ctx', [((i + step) % ranks, i) for i in range(ranks)])  47.8 us
    ppermute x4, waiting for transfers between devices, from_behind(): lax.ppermute(value, axis, [(source, source + steps) for source in range(l...  24.6 us
    ppermute x9, waiting for transfers between devices, shifted(): lax.ppermute(value, 'ctx', [((i + step) % ranks, i) for i in range(ranks)])  22 us
    all_to_all x1, blocking collectives, shards(): terms = lax.all_to_all(partial_grad, 'ctx', 0, 0, tiled=True)  21.1 us
    pallas_call x1, Pallas kernels, mla(): pl.pallas_call(functools.partial(mla_kernel, xs=xs), name='mla', out_shap...  14.2 us
    all_to_all x1, starting transfers between devices, shards(): terms = lax.all_to_all(spread, 'dp', 0, 0, tiled=True)  10.5 us
    pallas_call x1, Pallas kernels, kda_pairs(): pl.pallas_call(kda_pairs_kernel, name='kda_pairs', out_shape=shapes, in_s...  8.81 us
    unnamed x46, local copies, waits for them, and re-layouts  7.31 us
  transfers between devices with their start and end apart: 15, of which 11 were waited for; matrix products, arithmetic and copies ran while one was open for 2% of the time, Pallas kernels for 14%

profile of v3, /device:TPU:1, one launch (start us, length us, event | category | flops | bytes accessed | tf_op | source)
XLA Modules:
  0.0 196.0 jit_solution(16532522786524705040)
XLA Ops:
  2.3 11.5 %collective-permute-start.4 = (bf16[256,128]{1,0:T(8,128)(2,1)S(1)}, bf16[256,128]{1,0:T(8,128)(2,1)S(1)}, u32[]{:S(2)}, u32[]{:S(2)}) collective-permute-start(bf16[256,128]{1,0:T(8,128)(2,1)S(1)} %pad_maximum_fusion.6), channel_id=1, source_target_pairs={{16,0},{17,1},{18,2},{19,3},{20,4},{21,5},{22,6},{23,7},{24,8},{25... | collective-permute-start | bytes 196616 | tf_op jit(solution)/shard_map/ppermute | solution.py:641
  15.6 9.4 %collective-permute-start.6 = (bf16[1024,128]{1,0:T(8,128)(2,1)S(1)}, bf16[1024,128]{1,0:T(8,128)(2,1)S(1)}, u32[]{:S(2)}, u32[]{:S(2)}) collective-permute-start(bf16[1024,128]{1,0:T(8,128)(2,1)S(1)} %constant_dynamic-update-slice_fusion.5), channel_id=1, source_target_pairs={{1,0},{2,1},{3,2},{4,3},{5,4},{6,5},{7,6},{8,7},{9,8},{10,9},{11,1... | collective-permute-start | bytes 786440 | tf_op jit(solution)/shard_map/ppermute | solution.py:641
  28.9 7.0 %collective-permute-start.8 = (bf16[512,128]{1,0:T(8,128)(2,1)S(1)}, bf16[512,128]{1,0:T(8,128)(2,1)S(1)}, u32[]{:S(2)}, u32[]{:S(2)}) collective-permute-start(bf16[512,128]{1,0:T(8,128)(2,1)S(1)} %pad_maximum_fusion.4), channel_id=1, source_target_pairs={{2,0},{3,1},{4,2},{5,3},{6,4},{7,5},{8,6},{9,7},{10,8},{11,9},{12,... | collective-permute-start | bytes 393224 | tf_op jit(solution)/shard_map/ppermute | solution.py:641
  39.0 2.9 %collective-permute-done.8.ahead_two_hbm = bf16[512,128]{1,0:T(8,128)(2,1)S(1)} collective-permute-done((bf16[512,128]{1,0:T(8,128)(2,1)S(1)}, bf16[512,128]{1,0:T(8,128)(2,1)S(1)}, u32[]{:S(2)}, u32[]{:S(2)}) %collective-permute-start.8) | collective-permute-done | bytes 131104 | tf_op jit(solution)/shard_map/ppermute | solution.py:641
  42.3 2.6 %collective-permute-start.9 = (bf16[1024,128]{1,0:T(8,128)(2,1)S(1)}, bf16[1024,128]{1,0:T(8,128)(2,1)S(1)}, u32[]{:S(2)}, u32[]{:S(2)}) collective-permute-start(bf16[1024,128]{1,0:T(8,128)(2,1)S(1)} %bitcast.57), channel_id=1, source_target_pairs={{8,0},{9,1},{10,2},{11,3},{12,4},{13,5},{14,6},{15,7},{16,8},{17,9... | collective-permute-start | bytes 786440 | tf_op jit(solution)/shard_map/ppermute | solution.py:641
  44.9 4.5 %collective-permute-done.11 = bf16[1024,128]{1,0:T(8,128)(2,1)S(1)} collective-permute-done((bf16[1024,128]{1,0:T(8,128)(2,1)S(1)}, bf16[1024,128]{1,0:T(8,128)(2,1)S(1)}, u32[]{:S(2)}, u32[]{:S(2)}) %collective-permute-start.11) | collective-permute-done | bytes 262176 | tf_op jit(solution)/shard_map/ppermute | solution.py:641
  51.4 2.2 %collective-permute-done.9 = bf16[1024,128]{1,0:T(8,128)(2,1)S(1)} collective-permute-done((bf16[1024,128]{1,0:T(8,128)(2,1)S(1)}, bf16[1024,128]{1,0:T(8,128)(2,1)S(1)}, u32[]{:S(2)}, u32[]{:S(2)}) %collective-permute-start.9) | collective-permute-done | bytes 262176 | tf_op jit(solution)/shard_map/ppermute | solution.py:641
  53.7 9.6 %collective-permute-start.10 = (bf16[2,1024,128]{2,1,0:T(8,128)(2,1)S(1)}, bf16[2,1024,128]{2,1,0:T(8,128)(2,1)S(1)}, u32[]{:S(2)}, u32[]{:S(2)}) collective-permute-start(bf16[2,1024,128]{2,1,0:T(8,128)(2,1)S(1)} %get-tuple-element.36), channel_id=1, source_target_pairs={{4,0},{5,1},{6,2},{7,3},{8,4},{9,5},{10,6},{11,7},{12,8},{13,9},{1... | collective-permute-start | bytes 1572872 | tf_op jit(solution)/shard_map/ppermute | solution.py:641
  63.4 10.6 %collective-permute-done.10 = bf16[2,1024,128]{2,1,0:T(8,128)(2,1)S(1)} collective-permute-done((bf16[2,1024,128]{2,1,0:T(8,128)(2,1)S(1)}, bf16[2,1024,128]{2,1,0:T(8,128)(2,1)S(1)}, u32[]{:S(2)}, u32[]{:S(2)}) %collective-permute-start.10) | collective-permute-done | bytes 524320 | tf_op jit(solution)/shard_map/ppermute | solution.py:641
  75.7 3.2 %collective-permute-start.13 = (bf16[2,2,2,1024,128]{4,3,2,1,0:T(8,128)(2,1)}, bf16[2,2,2,1024,128]{4,3,2,1,0:T(8,128)(2,1)}, u32[]{:S(2)}, u32[]{:S(2)}) collective-permute-start(bf16[2,2,2,1024,128]{4,3,2,1,0:T(8,128)(2,1)} %pad_maximum_fusion.own_hbm), channel_id=1, source_target_pairs={{0,32},{32,0},{64,96},{96,64},{128,160},{160,128},{192,224},{224,1... | collective-permute-start | bytes 6291464 | tf_op jit(solution)/shard_map/ppermute | solution.py:662
  79.0 8.8 %kda_pairs.1 = (f32[32,64,64]{2,1,0:T(8,128)}, bf16[32,64,64]{2,1,0:T(8,128)(2,1)}, bf16[32,64,256]{2,1,0:T(8,128)(2,1)}, bf16[32,64,128]{2,1,0:T(8,128)(2,1)}, ...) custom-call(s32[1]{0:T(128)} %bitcast.place_ref, bf16[2048,128]{1,0:T(8,128)(2,1)} %bitcast.71, ...), custom_call_target="tpu_custom_call" | custom-call | flops 300000000 | bytes 12000000 | tf_op jit(solution)/shard_map/kda_pairs/pallas_call | solution.py:148
  89.1 5.0 %kda_invert.1.xmat = f32[32,64,64]{2,1,0:T(8,128)S(1)} custom-call(f32[32,64,64]{2,1,0:T(8,128)S(1)} %copy-done.4), custom_call_target="tpu_custom_call" | custom-call | flops 300000000 | bytes 12000000 | tf_op jit(solution)/shard_map/kda_invert/pallas_call | solution.py:227
  94.2 2.9 %kda_leave.1 = (bf16[2048,128]{1,0:T(8,128)(2,1)S(1)}, bf16[2048,128]{1,0:T(8,128)(2,1)S(1)}, bf16[32,128,128]{2,1,0:T(8,128)(2,1)S(1)}, bf16[32,64,256]{2,1,0:T(8,128)(2,1)S(1)}) custom-call(f32[32,64,64]{2,1,0:T(8,128)S(1)} %kda_invert.1.xmat, bf16[32,64,256]{2,1,0:T(8,128)(2,1)S(1)} %copy-done.3, bf16[32,64,128]{2,1,0:T(8,128)(2,1)S(1)} %copy-done.11, ...), custom_call_target="tpu_custom_call" | custom-call | flops 300000000 | bytes 8000000 | tf_op jit(solution)/shard_map/kda_leave/pallas_call | solution.py:275
  101.7 10.2 %collective-permute-done.in_first = bf16[2048,128]{1,0:T(8,128)(2,1)S(1)} collective-permute-done((bf16[2048,128]{1,0:T(8,128)(2,1)S(1)}, bf16[2048,128]{1,0:T(8,128)(2,1)S(1)}, u32[]{:S(2)}, u32[]{:S(2)}) %collective-permute-start) | collective-permute-done | bytes 524320 | tf_op jit(solution)/shard_map/ppermute | solution.py:601
  111.9 3.9 %collective-permute-done.1.in_second = bf16[2048,128]{1,0:T(8,128)(2,1)S(1)} collective-permute-done((bf16[2048,128]{1,0:T(8,128)(2,1)S(1)}, bf16[2048,128]{1,0:T(8,128)(2,1)S(1)}, u32[]{:S(2)}, u32[]{:S(2)}) %collective-permute-start.1) | collective-permute-done | bytes 524320 | tf_op jit(solution)/shard_map/ppermute | solution.py:601
  116.6 3.8 %kda_carry.1 = (bf16[2048,128]{1,0:T(8,128)(2,1)}, bf16[2048,128]{1,0:T(8,128)(2,1)}) custom-call(s32[1]{0:T(128)} %bitcast.place_ref, bf16[32,128,128]{2,1,0:T(8,128)(2,1)} %copy-done.2, bf16[2048,128]{1,0:T(8,128)(2,1)} %copy-done.8, bf16[2048,128]{1,0:T(8,128)(2,1)} %copy-done.9, bf16[2048,128]{1,0:T(8,128)(2,1)} %copy-done.16, bf16[2048,128]{1,0:T(8,128)(2,1)} %copy-done.17), custom_call_target="tpu_custom_call" | custom-call | flops 130000000 | bytes 5000000 | tf_op jit(solution)/shard_map/kda_carry/pallas_call | solution.py:335
  123.1 3.5 %kda_local.1 = (f32[32,64,128]{2,1,0:T(8,128)}, bf16[32,64,128]{2,1,0:T(8,128)(2,1)}) custom-call(bf16[32,64,64]{2,1,0:T(8,128)(2,1)} %get-tuple-element.19.att, bf16[32,64,256]{2,1,0:T(8,128)(2,1)} %copy-done.1, bf16[32,64,128]{2,1,0:T(8,128)(2,1)} %get-tuple-element.25.carried_q), custom_call_target="tpu_custom_call" | custom-call | flops 70000000 | bytes 4000000 | tf_op jit(solution)/shard_map/kda_local/pallas_call | solution.py:303
  126.6 6.0 %collective-permute-done.2.in_first = bf16[2048,128]{1,0:T(8,128)(2,1)S(1)} collective-permute-done((bf16[2048,128]{1,0:T(8,128)(2,1)}, bf16[2048,128]{1,0:T(8,128)(2,1)S(1)}, u32[]{:S(2)}, u32[]{:S(2)}) %collective-permute-start.2) | collective-permute-done | bytes 524320 | tf_op jit(solution)/shard_map/ppermute | solution.py:601
  132.6 4.5 %collective-permute-done.3.in_second = bf16[2048,128]{1,0:T(8,128)(2,1)S(1)} collective-permute-done((bf16[2048,128]{1,0:T(8,128)(2,1)}, bf16[2048,128]{1,0:T(8,128)(2,1)S(1)}, u32[]{:S(2)}, u32[]{:S(2)}) %collective-permute-start.3) | collective-permute-done | bytes 524320 | tf_op jit(solution)/shard_map/ppermute | solution.py:601
  139.4 2.6 %kda_close.1 = (bf16[2048,128]{1,0:T(8,128)(2,1)}, f32[32,128]{1,0:T(8,128)S(1)}) custom-call(s32[1]{0:T(128)} %bitcast.place_ref, f32[32,64,128]{2,1,0:T(8,128)S(1)} %copy-done.5, bf16[32,64,128]{2,1,0:T(8,128)(2,1)S(1)} %copy-done.10, bf16[2048,128]{1,0:T(8,128)(2,1)S(1)} %copy-done.7, bf16[2048,128]{1,0:T(8,128)(2,1)S(1)} %collective-permute-done.2.in_first, ...), custom_call_target="tpu_custom_call" | custom-call | flops 70000000 | bytes 5000000 | tf_op jit(solution)/shard_map/kda_close/pallas_call | solution.py:391
  142.0 21.1 %all_to_all.15 = f32[32,1,128]{2,1,0:T(1,128)S(1)} all-to-all(f32[32,1,128]{2,1,0:T(1,128)S(1)} %bitcast.55), channel_id=1, replica_groups=mesh['dp'=16,'ctx'=32] {'ctx'}, dimensions={0} | all-to-all | bytes 32768 | tf_op jit(solution)/shard_map/all_to_all | solution.py:697
  163.8 10.5 %all-to-all-start.1 = ((f32[16,1,128]{2,1,0:T(1,128)}), f32[16,1,128]{2,1,0:T(1,128)S(1)}, u32[]{:S(2)}, u32[]{:S(2)}) async-start(f32[16,1,128]{2,1,0:T(1,128)} %broadcast_in_dim.3), calls=%async_computation.1 | async-start | bytes 16384 | tf_op jit(solution)/shard_map/all_to_all | solution.py:699
  174.9 6.4 %all-to-all-done.1 = f32[16,1,128]{2,1,0:T(1,128)S(1)} async-done(((f32[16,1,128]{2,1,0:T(1,128)}), f32[16,1,128]{2,1,0:T(1,128)S(1)}, u32[]{:S(2)}, u32[]{:S(2)}) %all-to-all-start.1) | async-done | bytes 8224 | tf_op jit(solution)/shard_map/all_to_all | solution.py:699
  181.8 14.2 %mla.1 = bf16[2048,128]{1,0:T(8,128)(2,1)} custom-call(s32[2]{0:T(128)} %pad_add_fusion.spot_ref, bf16[2048,128]{1,0:T(8,128)(2,1)} %bitcast.67, bf16[128,512]{1,0:T(8,128)(2,1)} %bitcast.69, bf16[768,128]{1,0:T(8,128)(2,1)} %copy-done.15, bf16[1024,128]{1,0:T(8,128)(2,1)} %copy-done.14, bf16[512,128]{1,0:T(8,128)(2,1)} %copy-done.18, ...), custom_call_target="tpu_custom_call" | custom-call | flops 1500000000 | bytes 7000000 | tf_op jit(solution)/shard_map/mla/pallas_call | solution.py:570
  (85 shorter events, 27.9 us)
Async XLA Ops:
  2.3 13.2 %collective-permute-start.4 = (bf16[256,128]{1,0:T(8,128)(2,1)S(1)}, bf16[256,128]{1,0:T(8,128)(2,1)S(1)}, u32[]{:S(2)}, u32[]{:S(2)}) collective-permute-start(bf16[256,128]{1,0:T(8,128)(2,1)S(1)} %pad_maximum_fusion.6), channel_id=1, source_target_pairs={{16,0},{17,1},{18,2},{19,3},{20,4},{21,5},{22,6},{23,7},{24,8},{25... | collective-permute-start | bytes 196616 | tf_op jit(solution)/shard_map/ppermute | solution.py:641
  15.6 20.3 %collective-permute-start.6 = (bf16[1024,128]{1,0:T(8,128)(2,1)S(1)}, bf16[1024,128]{1,0:T(8,128)(2,1)S(1)}, u32[]{:S(2)}, u32[]{:S(2)}) collective-permute-start(bf16[1024,128]{1,0:T(8,128)(2,1)S(1)} %constant_dynamic-update-slice_fusion.5), channel_id=1, source_target_pairs={{1,0},{2,1},{3,2},{4,3},{5,4},{6,5},{7,6},{8,7},{9,8},{10,9},{11,1... | collective-permute-start | bytes 786440 | tf_op jit(solution)/shard_map/ppermute | solution.py:641
  25.0 12.0 %collective-permute-start.5 = (bf16[768,128]{1,0:T(8,128)(2,1)S(1)}, bf16[768,128]{1,0:T(8,128)(2,1)S(1)}, u32[]{:S(2)}, u32[]{:S(2)}) collective-permute-start(bf16[768,128]{1,0:T(8,128)(2,1)S(1)} %get-tuple-element.51), channel_id=1, source_target_pairs={{31,0},{0,1},{1,2},{2,3},{3,4},{4,5},{5,6},{6,7},{7,8},{8,9},{9,10... | collective-permute-start | bytes 589832 | tf_op jit(solution)/shard_map/ppermute | solution.py:641
  27.0 10.0 %collective-permute-start.7 = (bf16[512,128]{1,0:T(8,128)(2,1)S(1)}, bf16[512,128]{1,0:T(8,128)(2,1)S(1)}, u32[]{:S(2)}, u32[]{:S(2)}) collective-permute-start(bf16[512,128]{1,0:T(8,128)(2,1)S(1)} %pad_maximum_fusion.3), channel_id=1, source_target_pairs={{30,0},{31,1},{0,2},{1,3},{2,4},{3,5},{4,6},{5,7},{6,8},{7,9},{8,1... | collective-permute-start | bytes 393224 | tf_op jit(solution)/shard_map/ppermute | solution.py:641
  28.9 13.0 %collective-permute-start.8 = (bf16[512,128]{1,0:T(8,128)(2,1)S(1)}, bf16[512,128]{1,0:T(8,128)(2,1)S(1)}, u32[]{:S(2)}, u32[]{:S(2)}) collective-permute-start(bf16[512,128]{1,0:T(8,128)(2,1)S(1)} %pad_maximum_fusion.4), channel_id=1, source_target_pairs={{2,0},{3,1},{4,2},{5,3},{6,4},{7,5},{8,6},{9,7},{10,8},{11,9},{12,... | collective-permute-start | bytes 393224 | tf_op jit(solution)/shard_map/ppermute | solution.py:641
  35.9 17.7 %copy-start.14 = (bf16[1024,128]{1,0:T(8,128)(2,1)}, bf16[1024,128]{1,0:T(8,128)(2,1)S(1)}, u32[]{:S(2)}) copy-start(bf16[1024,128]{1,0:T(8,128)(2,1)S(1)} %collective-permute-done.6.ahead_one_hbm) | copy-start | bytes 786436
  37.0 16.6 %copy-start.18 = (bf16[512,128]{1,0:T(8,128)(2,1)}, bf16[512,128]{1,0:T(8,128)(2,1)S(1)}, u32[]{:S(2)}) copy-start(bf16[512,128]{1,0:T(8,128)(2,1)S(1)} %collective-permute-done.7.back_two_hbm) | copy-start | bytes 393220
  37.0 16.6 %copy-start.15 = (bf16[768,128]{1,0:T(8,128)(2,1)}, bf16[768,128]{1,0:T(8,128)(2,1)S(1)}, u32[]{:S(2)}) copy-start(bf16[768,128]{1,0:T(8,128)(2,1)S(1)} %collective-permute-done.5.back_one_hbm) | copy-start | bytes 589828
  37.1 12.3 %collective-permute-start.11 = (bf16[1024,128]{1,0:T(8,128)(2,1)S(1)}, bf16[1024,128]{1,0:T(8,128)(2,1)S(1)}, u32[]{:S(2)}, u32[]{:S(2)}) collective-permute-start(bf16[1024,128]{1,0:T(8,128)(2,1)S(1)} %get-tuple-element.42), channel_id=1, source_target_pairs={{24,0},{25,1},{26,2},{27,3},{28,4},{29,5},{30,6},{31,7},{0,8},{1,9... | collective-permute-start | bytes 786440 | tf_op jit(solution)/shard_map/ppermute | solution.py:641
  41.9 11.8 %copy-start.19 = (bf16[512,128]{1,0:T(8,128)(2,1)}, bf16[512,128]{1,0:T(8,128)(2,1)S(1)}, u32[]{:S(2)}) copy-start(bf16[512,128]{1,0:T(8,128)(2,1)S(1)} %collective-permute-done.8.ahead_two_hbm) | copy-start | bytes 393220
  42.3 11.3 %collective-permute-start.9 = (bf16[1024,128]{1,0:T(8,128)(2,1)S(1)}, bf16[1024,128]{1,0:T(8,128)(2,1)S(1)}, u32[]{:S(2)}, u32[]{:S(2)}) collective-permute-start(bf16[1024,128]{1,0:T(8,128)(2,1)S(1)} %bitcast.57), channel_id=1, source_target_pairs={{8,0},{9,1},{10,2},{11,3},{12,4},{13,5},{14,6},{15,7},{16,8},{17,9... | collective-permute-start | bytes 786440 | tf_op jit(solution)/shard_map/ppermute | solution.py:641
  49.4 13.9 %collective-permute-start.12 = (bf16[2,1024,128]{2,1,0:T(8,128)(2,1)S(1)}, bf16[2,1024,128]{2,1,0:T(8,128)(2,1)S(1)}, u32[]{:S(2)}, u32[]{:S(2)}) collective-permute-start(bf16[2,1024,128]{2,1,0:T(8,128)(2,1)S(1)} %get-tuple-element.38), channel_id=1, source_target_pairs={{28,0},{29,1},{30,2},{31,3},{0,4},{1,5},{2,6},{3,7},{4,8},{5,9},{6... | collective-permute-start | bytes 1572872 | tf_op jit(solution)/shard_map/ppermute | solution.py:641
  53.7 20.4 %collective-permute-start.10 = (bf16[2,1024,128]{2,1,0:T(8,128)(2,1)S(1)}, bf16[2,1024,128]{2,1,0:T(8,128)(2,1)S(1)}, u32[]{:S(2)}, u32[]{:S(2)}) collective-permute-start(bf16[2,1024,128]{2,1,0:T(8,128)(2,1)S(1)} %get-tuple-element.36), channel_id=1, source_target_pairs={{4,0},{5,1},{6,2},{7,3},{8,4},{9,5},{10,6},{11,7},{12,8},{13,9},{1... | collective-permute-start | bytes 1572872 | tf_op jit(solution)/shard_map/ppermute | solution.py:641
  75.7 106.1 %collective-permute-start.13 = (bf16[2,2,2,1024,128]{4,3,2,1,0:T(8,128)(2,1)}, bf16[2,2,2,1024,128]{4,3,2,1,0:T(8,128)(2,1)}, u32[]{:S(2)}, u32[]{:S(2)}) collective-permute-start(bf16[2,2,2,1024,128]{4,3,2,1,0:T(8,128)(2,1)} %pad_maximum_fusion.own_hbm), channel_id=1, source_target_pairs={{0,32},{32,0},{64,96},{96,64},{128,160},{160,128},{192,224},{224,1... | collective-permute-start | bytes 6291464 | tf_op jit(solution)/shard_map/ppermute | solution.py:662
  99.1 16.7 %copy-start.8 = (bf16[2048,128]{1,0:T(8,128)(2,1)}, bf16[2048,128]{1,0:T(8,128)(2,1)S(1)}, u32[]{:S(2)}) copy-start(bf16[2048,128]{1,0:T(8,128)(2,1)S(1)} %get-tuple-element.29.offs_first) | copy-start | bytes 1572868
  99.1 16.7 %copy-start.9 = (bf16[2048,128]{1,0:T(8,128)(2,1)}, bf16[2048,128]{1,0:T(8,128)(2,1)S(1)}, u32[]{:S(2)}) copy-start(bf16[2048,128]{1,0:T(8,128)(2,1)S(1)} %get-tuple-element.30.offs_second) | copy-start | bytes 1572868
  99.1 12.8 %collective-permute-start = (bf16[2048,128]{1,0:T(8,128)(2,1)S(1)}, bf16[2048,128]{1,0:T(8,128)(2,1)S(1)}, u32[]{:S(2)}, u32[]{:S(2)}) collective-permute-start(bf16[2048,128]{1,0:T(8,128)(2,1)S(1)} %get-tuple-element.29.offs_first), channel_id=1, source_target_pairs={{0,1},{1,2},{2,3},{3,4},{4,5},{5,6},{6,7},{7,8},{8,9},{9,10},{10,1... | collective-permute-start | bytes 1572872 | tf_op jit(solution)/shard_map/ppermute | solution.py:601
  100.4 15.4 %collective-permute-start.1 = (bf16[2048,128]{1,0:T(8,128)(2,1)S(1)}, bf16[2048,128]{1,0:T(8,128)(2,1)S(1)}, u32[]{:S(2)}, u32[]{:S(2)}) collective-permute-start(bf16[2048,128]{1,0:T(8,128)(2,1)S(1)} %get-tuple-element.30.offs_second), channel_id=1, source_target_pairs={{1,0},{2,1},{3,2},{4,3},{5,4},{6,5},{7,6},{8,7},{9,8},{10,9},{11,1... | collective-permute-start | bytes 1572872 | tf_op jit(solution)/shard_map/ppermute | solution.py:601
  116.6 20.6 %copy-start.6 = (bf16[1,128,16,128]{3,2,1,0:T(8,128)(2,1)S(1)}, bf16[1,128,16,128]{3,2,1,0:T(8,128)(2,1)}, u32[]{:S(2)}) copy-start(bf16[1,128,16,128]{3,2,1,0:T(8,128)(2,1)} %param.23) | copy-start | bytes 1572868
  116.6 20.6 %copy-start.13 = (f32[128]{0:T(128)S(1)}, f32[128]{0:T(128)}, u32[]{:S(2)}) copy-start(f32[128]{0:T(128)} %param.22) | copy-start | bytes 1540
  120.4 16.8 %copy-start.7 = (bf16[2048,128]{1,0:T(8,128)(2,1)S(1)}, bf16[2048,128]{1,0:T(8,128)(2,1)}, u32[]{:S(2)}) copy-start(bf16[2048,128]{1,0:T(8,128)(2,1)} %get-tuple-element.31.own_first) | copy-start | bytes 1572868
  120.4 12.2 %collective-permute-start.2 = (bf16[2048,128]{1,0:T(8,128)(2,1)}, bf16[2048,128]{1,0:T(8,128)(2,1)S(1)}, u32[]{:S(2)}, u32[]{:S(2)}) collective-permute-start(bf16[2048,128]{1,0:T(8,128)(2,1)} %get-tuple-element.31.own_first), channel_id=1, source_target_pairs={{0,1},{1,2},{2,3},{3,4},{4,5},{5,6},{6,7},{7,8},{8,9},{9,10},{10,1... | collective-permute-start | bytes 1572872 | tf_op jit(solution)/shard_map/ppermute | solution.py:601
  121.8 15.3 %collective-permute-start.3 = (bf16[2048,128]{1,0:T(8,128)(2,1)}, bf16[2048,128]{1,0:T(8,128)(2,1)S(1)}, u32[]{:S(2)}, u32[]{:S(2)}) collective-permute-start(bf16[2048,128]{1,0:T(8,128)(2,1)} %get-tuple-element.32), channel_id=1, source_target_pairs={{1,0},{2,1},{3,2},{4,3},{5,4},{6,5},{7,6},{8,7},{9,8},{10,9},{11,1... | collective-permute-start | bytes 1572872 | tf_op jit(solution)/shard_map/ppermute | solution.py:601
  163.8 17.5 %all-to-all-start.1 = ((f32[16,1,128]{2,1,0:T(1,128)}), f32[16,1,128]{2,1,0:T(1,128)S(1)}, u32[]{:S(2)}, u32[]{:S(2)}) async-start(f32[16,1,128]{2,1,0:T(1,128)} %broadcast_in_dim.3), calls=%async_computation.1 | async-start | bytes 16384 | tf_op jit(solution)/shard_map/all_to_all | solution.py:699
  (11 other events, 27.6 us)

commit v4 on v3

--- a/solution.py
+++ b/solution.py
@@ -236,8 +236,10 @@
     )(lmat)
 
 
-def kda_leave_kernel(xmat, rhs, leaving, closing, offs_first, offs_second, tmap, upd):
+def kda_leave_kernel(xmat, rhs, leaving, closing, behind, offs_first, offs_second, tmap, upd):
     heads = xmat.shape[0] // 2
+
+    offs_first[heads * DN :, :] = behind[8 * HALF :, :]
 
     def solve(g, _):
         for u in range(8):
@@ -263,11 +265,11 @@
         lax.fori_loop(0, heads // 4, leave, 0)
 
 
-def kda_leave(xmat, rhs, leaving, closing):
+def kda_leave(xmat, rhs, leaving, closing, behind):
     n = xmat.shape[0]
     spec = pl.BlockSpec(memory_space=pltpu.VMEM)
     shapes = (
-        jax.ShapeDtypeStruct((n // 2 * DN, DN), BF),
+        jax.ShapeDtypeStruct((n // 2 * DN + 4 * HALF, DN), BF),
         jax.ShapeDtypeStruct((n // 2 * DN, DN), BF),
         jax.ShapeDtypeStruct((n, DN, DN), BF),
         jax.ShapeDtypeStruct((n, HALF, 2 * DN), BF),
@@ -276,11 +278,11 @@
         kda_leave_kernel,
         name="kda_leave",
         out_shape=shapes,
-        in_specs=[spec] * 4,
+        in_specs=[spec] * 5,
         out_specs=(spec,) * 4,
         compiler_params=pltpu.CompilerParams(vmem_limit_bytes=24 << 20),
         cost_estimate=pl.CostEstimate(flops=300_000_000, bytes_accessed=8_000_000, transcendentals=0),
-    )(xmat, rhs, leaving, closing)
+    )(xmat, rhs, leaving, closing, behind)
 
 
 def kda_local_kernel(att, upd, carried_q, local, squery):
@@ -331,7 +333,7 @@
 
 def kda_carry(place, tmap, offs_first, offs_second, in_first, in_second, ranks):
     spec = pl.BlockSpec(memory_space=pltpu.VMEM)
-    shape = jax.ShapeDtypeStruct(offs_first.shape, BF)
+    shape = jax.ShapeDtypeStruct(offs_second.shape, BF)
     return pl.pallas_call(
         functools.partial(kda_carry_kernel, ranks=ranks),
         name="kda_carry",
@@ -406,21 +408,90 @@
     return jnp.where(iota2(shape, 0) == source(iota2(shape, 1)), 1.0, 0.0).astype(BF)
 
 
-def mla_kernel(
-    spot_ref, q_hbm, lat_ref, back_one_hbm, ahead_one_hbm, back_two_hbm, ahead_two_hbm, docs_ref, own_hbm, other_hbm, out_ref,
-    q_ref, back_one, ahead_one, back_two, ahead_two, own_w, other_w, sems, qp, keys, keysp, mask, lifted, mixed, outs, *, xs,
+def mla_lift_kernel(spot_ref, q_hbm, own_hbm, other_hbm, lifted, q_ref, own_w, other_w, sems, qp, *, xs, ranks):
+    place, core = spot_ref[0], spot_ref[1]
+    heads = q_ref.shape[0] // (2 * HALF)
+    moves = ((q_hbm, q_ref), (own_hbm.at[0], own_w), (other_hbm.at[0], other_w))
+    copies = [pltpu.make_async_copy(a, b, sems.at[n]) for n, (a, b) in enumerate(moves)]
+    for copy in copies:
+        copy.start()
+
+    def source_n(k):
+        turn, column = k // 64 + 2 * ((k // 32) % 2) + 4 * ((k // 4) % 2), (k // 8) % xs
+        shift = jnp.where(column == xs - 1, -1, column) + xs * turn
+        return ((shift + place + ranks) % ranks) * 4 + k % 4
+
+    pick = onehot((DN, DN), source_n)
+    rows = 256
+    copies[0].wait()
+
+    def place_q(c, _):
+        at = pl.ds(pl.multiple_of(c * rows, rows), rows)
+        qp[at, :] = mm(q_ref[at, :], pick)
+        return 0
+
+    lax.fori_loop(0, q_ref.shape[0] // rows, place_q, 0)
+    span = heads // 2
+    for side, weights in ((0, own_w), (1, other_w)):
+        first = span * core if side == 0 else span * (1 - core)
+        copies[1 + side].wait()
+
+        def lift(g, _, weights=weights, first=first):
+            for u in range(2):
+                hl = g * 2 + u
+                h = first + hl
+                q = qp[pl.ds(h, 2 * HALF, stride=heads), :].astype(BF)
+                for lb in range(4):
+                    at = pl.ds(pl.multiple_of((hl * 4 + lb) * 32, 32), 32)
+                    w = jnp.concatenate(
+                        [weights[e, b, at, :] for e in range(2) for b in range(2)], axis=0
+                    )
+                    made = mm(q, w).astype(BF)
+                    for i in range(2):
+                        dst = pl.ds(pl.multiple_of(h * HALF, HALF), HALF)
+                        lifted[i, dst, lb * DN : (lb + 1) * DN] = made[i * HALF : (i + 1) * HALF]
+            return 0
+
+        lax.fori_loop(0, span // 2, lift, 0)
+
+
+def mla_lift(spot, q, own_w, other_w, xs, ranks):
+    hbm = pl.BlockSpec(memory_space=pltpu.HBM)
+    rows = q.shape[0]
+    return pl.pallas_call(
+        functools.partial(mla_lift_kernel, xs=xs, ranks=ranks),
+        name="mla_lift",
+        out_shape=jax.ShapeDtypeStruct((2, rows // 2, 4 * DN), BF),
+        in_specs=[pl.BlockSpec(memory_space=pltpu.SMEM), hbm, hbm, hbm],
+        out_specs=pl.BlockSpec(memory_space=pltpu.VMEM),
+        scratch_shapes=[
+            pltpu.VMEM((rows, DN), BF),
+            pltpu.VMEM(own_w.shape[1:], BF),
+            pltpu.VMEM(own_w.shape[1:], BF),
+            pltpu.SemaphoreType.DMA((3,)),
+            pltpu.VMEM((rows, DN), F32),
+        ],
+        compiler_params=pltpu.CompilerParams(vmem_limit_bytes=60 << 20),
+        cost_estimate=pl.CostEstimate(flops=400_000_000, bytes_accessed=5_000_000, transcendentals=0),
+    )(spot, q, own_w, other_w)
+
+
+def mla_mix_kernel(
+    spot_ref, lifted, lat_ref, back_one_hbm, ahead_one_hbm, back_two_hbm, ahead_two_hbm, docs_ref, own_hbm, other_hbm, out_ref,
+    back_one, ahead_one, back_two, ahead_two, own_w, other_w, sems, keys, keysp, mask, mixed, outs, *, xs,
 ):
     ranks = docs_ref.shape[0]
     place, core = spot_ref[0], spot_ref[1]
-    heads = q_ref.shape[0] // (2 * HALF)
+    heads = out_ref.shape[0] // (2 * HALF)
+    rows = 256
+    quarter = pl.ds(8 * HALF, 4 * HALF)
     moves = (
-        (q_hbm, q_ref),
-        (back_two_hbm.at[pl.ds(4 * HALF, 4 * HALF), :], back_two),
-        (back_one_hbm.at[pl.ds(8 * HALF, 4 * HALF), :], back_one),
-        (ahead_two_hbm.at[pl.ds(4 * HALF, 4 * HALF), :], ahead_two),
+        (back_two_hbm.at[pl.ds(heads * DN, 4 * HALF), :], back_two),
+        (back_one_hbm.at[quarter, :], back_one),
+        (ahead_two_hbm.at[quarter, :], ahead_two),
         (ahead_one_hbm.at[pl.ds(8 * HALF, 8 * HALF), :], ahead_one),
-        (own_hbm, own_w),
-        (other_hbm, other_w),
+        (own_hbm.at[1], own_w),
+        (other_hbm.at[1], other_w),
     )
     copies = [pltpu.make_async_copy(a, b, sems.at[n]) for n, (a, b) in enumerate(moves)]
     for copy in copies:
@@ -435,7 +506,7 @@
 
     keys[0, 3 * HALF :, :] = jnp.zeros((width - 3 * HALF, 4 * DN), BF)
     keys[1, 3 * HALF :, :] = jnp.zeros((width - 3 * HALF, 4 * DN), BF)
-    for copy in copies[:5]:
+    for copy in copies[:4]:
         copy.wait()
     piece(back_two, 0, 0, 0)
     piece(back_one, 0, 0, 1)
@@ -459,25 +530,11 @@
     def _():
         piece(ahead_one, 4 * HALF, 1, 1)
 
-    def source_n(k):
-        turn, column = k // 64 + 2 * ((k // 32) % 2) + 4 * ((k // 4) % 2), (k // 8) % xs
+    def source_l(k):
+        turn, column = 7 * (k // 256) + 2 * ((k // 128) % 2) + 4 * ((k // 16) % 2), (k // 32) % xs
         shift = jnp.where(column == xs - 1, -1, column) + xs * turn
-        return ((shift + place + ranks) % ranks) * 4 + k % 4
-
-    def source_l(k):
-        turn, column = 7 * (k // 256) + 6 * ((k // 128) % 2) + 4 * ((k // 16) % 2), (k // 32) % xs
-        shift = jnp.where(column >= xs // 2, column - xs, column) + xs * turn
         return ((shift + place + ranks) % ranks) * 16 + k % 16
 
-    pick = onehot((DN, DN), source_n)
-    rows = 256
-
-    def place_q(c, _):
-        at = pl.ds(pl.multiple_of(c * rows, rows), rows)
-        qp[at, :] = mm(q_ref[at, :], pick)
-        return 0
-
-    lax.fori_loop(0, q_ref.shape[0] // rows, place_q, 0)
     spread = onehot((4 * DN, 4 * DN), source_l)
     ti, si = iota2((HALF, HALF), 0), iota2((HALF, HALF), 1)
     for i in range(2):
@@ -497,29 +554,6 @@
                 mask[i, r * HALF : (r + 1) * HALF, (2 - back) * HALF : (3 - back) * HALF] = fill
         mask[i, :, 3 * HALF :] = jnp.full((4 * HALF, width - 3 * HALF), -1e30, F32)
 
-    span = heads // 2
-    for side, weights in ((0, own_w), (1, other_w)):
-        first = span * core if side == 0 else span * (1 - core)
-        copies[5 + side].wait()
-
-        def lift(g, _, weights=weights, first=first):
-            for u in range(2):
-                hl = g * 2 + u
-                h = first + hl
-                q = qp[pl.ds(h, 2 * HALF, stride=heads), :].astype(BF)
-                for lb in range(4):
-                    at = pl.ds(pl.multiple_of((hl * 4 + lb) * 32, 32), 32)
-                    w = jnp.concatenate(
-                        [weights[0, e, b, at, :] for e in range(2) for b in range(2)], axis=0
-                    )
-                    made = mm(q, w).astype(BF)
-                    for i in range(2):
-                        dst = pl.ds(pl.multiple_of(h * HALF, HALF), HALF)
-                        lifted[i, dst, lb * DN : (lb + 1) * DN] = made[i * HALF : (i + 1) * HALF]
-            return 0
-
-        lax.fori_loop(0, span // 2, lift, 0)
-
     scale = 1.0 / math.sqrt(DN)
 
     def attend(g, _):
@@ -534,8 +568,11 @@
 
     lax.fori_loop(0, heads // 2, attend, 0)
 
+    span = heads // 2
     for side, weights in ((0, own_w), (1, other_w)):
         first = span * core if side == 0 else span * (1 - core)
+
+        copies[4 + side].wait()
 
         def lower(g, _, weights=weights, first=first):
             for u in range(2):
@@ -543,7 +580,7 @@
                 h = first + hl
                 w = jnp.concatenate(
                     [
-                        weights[1, e, b, pl.ds(pl.multiple_of((c * span + hl) * 16, 16), 16), :]
+                        weights[e, b, pl.ds(pl.multiple_of((c * span + hl) * 16, 16), 16), :]
                         for e in range(2) for b in range(2) for c in range(8)
                     ],
                     axis=0,
@@ -560,39 +597,36 @@
         out_ref[at, :] = outs[at, :].astype(BF)
         return 0
 
-    lax.fori_loop(0, q_ref.shape[0] // rows, narrow, 0)
-
-
-def mla(spot, q, latents, back_one, ahead_one, back_two, ahead_two, docs, own_w, other_w, xs):
+    lax.fori_loop(0, out_ref.shape[0] // rows, narrow, 0)
+
+
+def mla_mix(spot, lifted, latents, back_one, ahead_one, back_two, ahead_two, docs, own_w, other_w, xs):
     spec = pl.BlockSpec(memory_space=pltpu.VMEM)
     hbm = pl.BlockSpec(memory_space=pltpu.HBM)
-    rows = q.shape[0]
+    rows = 2 * lifted.shape[1]
     return pl.pallas_call(
-        functools.partial(mla_kernel, xs=xs),
-        name="mla",
+        functools.partial(mla_mix_kernel, xs=xs),
+        name="mla_mix",
         out_shape=jax.ShapeDtypeStruct((rows, DN), BF),
-        in_specs=[pl.BlockSpec(memory_space=pltpu.SMEM), hbm, spec, hbm, hbm, hbm, hbm, spec, hbm, hbm],
+        in_specs=[pl.BlockSpec(memory_space=pltpu.SMEM), spec, spec, hbm, hbm, hbm, hbm, spec, hbm, hbm],
         out_specs=spec,
         scratch_shapes=[
-            pltpu.VMEM((rows, DN), BF),
             pltpu.VMEM((4 * HALF, DN), BF),
             pltpu.VMEM((8 * HALF, DN), BF),
             pltpu.VMEM((4 * HALF, DN), BF),
             pltpu.VMEM((4 * HALF, DN), BF),
-            pltpu.VMEM(own_w.shape, BF),
-            pltpu.VMEM(own_w.shape, BF),
-            pltpu.SemaphoreType.DMA((7,)),
-            pltpu.VMEM((rows, DN), F32),
+            pltpu.VMEM(own_w.shape[1:], BF),
+            pltpu.VMEM(own_w.shape[1:], BF),
+            pltpu.SemaphoreType.DMA((6,)),
             pltpu.VMEM((2, 256, 4 * DN), BF),
             pltpu.VMEM((2, 256, 4 * DN), BF),
             pltpu.VMEM((2, 256, 256), F32),
             pltpu.VMEM((2, rows // 2, 4 * DN), BF),
-            pltpu.VMEM((2, rows // 2, 4 * DN), BF),
             pltpu.VMEM((rows, DN), F32),
         ],
         compiler_params=pltpu.CompilerParams(vmem_limit_bytes=60 << 20),
-        cost_estimate=pl.CostEstimate(flops=1_500_000_000, bytes_accessed=7_000_000, transcendentals=600_000),
-    )(spot, q, latents, back_one, ahead_one, back_two, ahead_two, docs, own_w, other_w)
+        cost_estimate=pl.CostEstimate(flops=1_100_000_000, bytes_accessed=6_000_000, transcendentals=600_000),
+    )(spot, lifted, latents, back_one, ahead_one, back_two, ahead_two, docs, own_w, other_w)
 
 
 def from_behind(value, axis, steps):
@@ -646,16 +680,17 @@
     tiles = latents.reshape(2, HALF, 4, DN).transpose(0, 2, 1, 3).reshape(2, 4 * HALF, DN)
     ahead_one = shifted(jnp.concatenate([lift, lower, tiles[0], tiles[1]], axis=0), 1)
     back_one = shifted(jnp.concatenate([lift, lower, tiles[0]], axis=0), -1)
-    ahead_two = shifted(jnp.concatenate([lift, tiles[1]], axis=0), 2)
-    back_two = shifted(jnp.concatenate([lower, tiles[0]], axis=0), -2)
+    ahead_two = shifted(jnp.concatenate([lift, lower, tiles[1]], axis=0), 2)
     many = span * 32
     lift = jnp.stack([lift, ahead_one[:many], ahead_two[:many], back_one[:many]])
     lift = lift.reshape(XS, 2, span, 4, 4, DN).transpose(2, 3, 0, 1, 4, 5).reshape(XS * many, DN)
     lower = jnp.concatenate(
-        [lower, ahead_one[many : 2 * many], back_two[:many], back_one[many : 2 * many]], axis=0
-    )
-    lift = jnp.stack([lift, shifted(lift, 2 * XS)])
-    lower = jnp.stack([lower, shifted(lower, -2 * XS)])
+        [lower, ahead_one[many : 2 * many], ahead_two[many : 2 * many], back_one[many : 2 * many]], axis=0
+    )
+    both = jnp.stack([lift, lower])
+    moved = shifted(both, 2 * XS)
+    lift = jnp.stack([both[0], moved[0]])
+    lower = jnp.stack([both[1], moved[1]])
     lift = jnp.stack([lift, shifted(lift, XS)])
     lower = jnp.stack([lower, shifted(lower, -XS)])
     own_w = jnp.stack([lift, lower])
@@ -673,7 +708,7 @@
         docs,
     )
     xmat = kda_invert(lmat)
-    offs_first, offs_second, tmap, upd = kda_leave(xmat, rhs, leaving, closing)
+    offs_first, offs_second, tmap, upd = kda_leave(xmat, rhs, leaving, closing, back_one)
     near_first = from_behind(offs_first, "ctx", 1)
     near_second = from_behind(offs_second, "ctx", -1)
     local, squery = kda_local(att, upd, carried_q)
@@ -701,18 +736,9 @@
     gain_grad = total_grad / math.sqrt(seqs * groups * rows * ranks * heads)
 
     spot = jnp.stack([place, core]).astype(jnp.int32)
-    mla_rows = mla(
-        spot,
-        flat(latent_query_rows),
-        latents,
-        back_one,
-        ahead_one,
-        back_two,
-        ahead_two,
-        docs,
-        own_w,
-        other_w,
-        XS,
+    lifted = mla_lift(spot, flat(latent_query_rows), own_w, other_w, XS, ranks)
+    mla_rows = mla_mix(
+        spot, lifted, latents, back_one, ahead_one, near_first, ahead_two, docs, own_w, other_w, XS
     )
     mla_output = mla_rows.reshape(seqs, rows, heads, DN)
     return (kda_output, mla_output, gain_grad)

time: 197 us -> 211 us (1.071)
  waiting for transfers between devices: 52.9 us -> 62.6 us
  Pallas kernels: 40.9 us -> 44.8 us
    ppermute x9 -> x7, waiting for transfers between devices: 22 us -> 31.8 us  [shifted(): lax.ppermute(value, 'ctx', [((i + step) % ranks, i) for i in range(ranks)])]
    pallas_call x1 -> x2, Pallas kernels: 14.2 us -> 18 us  [the longest x1 11.7 us: mla_mix(): pl.pallas_call(functools.partial(mla_mix_kernel, xs=xs), name='mla_mix',...]
    ppermute x9 -> x7, starting transfers between devices: 47.8 us -> 44.4 us  [shifted(): lax.ppermute(value, 'ctx', [((i + step) % ranks, i) for i in range(ranks)])]
    unnamed x46 -> x48, local copies, waits for them, and re-layouts: 7.31 us -> 7.55 us
  transfers between devices with their start and end apart: 15 -> 13, of which waited for: 11 -> 9; matrix products, arithmetic and copies ran while one was open for 2% -> 1% of each run, Pallas kernels for 14% -> 13%
where the time goes in v4:
time: 211 us; the launch traced here: 210 us
  starting transfers between devices  66.6 us (32%)
  waiting for transfers between devices  62.6 us (30%)
  Pallas kernels  44.8 us (21%)
  blocking collectives  21.3 us (10%)
  local copies, waits for them, and re-layouts  10.1 us (5%)
  other arithmetic  3.4 us (2%)
    ppermute x7, starting transfers between devices, shifted(): lax.ppermute(value, 'ctx', [((i + step) % ranks, i) for i in range(ranks)])  44.4 us
    ppermute x7, waiting for transfers between devices, shifted(): lax.ppermute(value, 'ctx', [((i + step) % ranks, i) for i in range(ranks)])  31.8 us
    ppermute x4, waiting for transfers between devices, from_behind(): lax.ppermute(value, axis, [(source, source + steps) for source in range(l...  24.4 us
    all_to_all x1, blocking collectives, shards(): terms = lax.all_to_all(partial_grad, 'ctx', 0, 0, tiled=True)  21.3 us
    pallas_call x1, Pallas kernels, mla_mix(): pl.pallas_call(functools.partial(mla_mix_kernel, xs=xs), name='mla_mix',...  11.7 us
    all_to_all x1, starting transfers between devices, shards(): terms = lax.all_to_all(spread, 'dp', 0, 0, tiled=True)  10.5 us
    pallas_call x1, Pallas kernels, kda_pairs(): pl.pallas_call(kda_pairs_kernel, name='kda_pairs', out_shape=shapes, in_s...  8.82 us
    unnamed x48, local copies, waits for them, and re-layouts  7.55 us
  transfers between devices with their start and end apart: 13, of which 9 were waited for; matrix products, arithmetic and copies ran while one was open for 1% of the time, Pallas kernels for 13%

profile of v4, /device:TPU:1, one launch (start us, length us, event | category | flops | bytes accessed | tf_op | source)
XLA Modules:
  0.0 209.8 jit_solution(5373765988525457492)
XLA Ops:
  2.3 11.5 %collective-permute-start = (bf16[256,128]{1,0:T(8,128)(2,1)S(1)}, bf16[256,128]{1,0:T(8,128)(2,1)S(1)}, u32[]{:S(2)}, u32[]{:S(2)}) collective-permute-start(bf16[256,128]{1,0:T(8,128)(2,1)S(1)} %pad_maximum_fusion.6), channel_id=1, source_target_pairs={{16,0},{17,1},{18,2},{19,3},{20,4},{21,5},{22,6},{23,7},{24,8},{25... | collective-permute-start | bytes 196616 | tf_op jit(solution)/shard_map/ppermute | solution.py:675
  15.6 9.4 %collective-permute-start.6 = (bf16[1024,128]{1,0:T(8,128)(2,1)S(1)}, bf16[1024,128]{1,0:T(8,128)(2,1)S(1)}, u32[]{:S(2)}, u32[]{:S(2)}) collective-permute-start(bf16[1024,128]{1,0:T(8,128)(2,1)S(1)} %get-tuple-element.53), channel_id=1, source_target_pairs={{1,0},{2,1},{3,2},{4,3},{5,4},{6,5},{7,6},{8,7},{9,8},{10,9},{11,1... | collective-permute-start | bytes 786440 | tf_op jit(solution)/shard_map/ppermute | solution.py:675
  27.0 3.6 %collective-permute-start.7 = (bf16[768,128]{1,0:T(8,128)(2,1)S(1)}, bf16[768,128]{1,0:T(8,128)(2,1)S(1)}, u32[]{:S(2)}, u32[]{:S(2)}) collective-permute-start(bf16[768,128]{1,0:T(8,128)(2,1)S(1)} %get-tuple-element.54), channel_id=1, source_target_pairs={{2,0},{3,1},{4,2},{5,3},{6,4},{7,5},{8,6},{9,7},{10,8},{11,9},{12,... | collective-permute-start | bytes 589832 | tf_op jit(solution)/shard_map/ppermute | solution.py:675
  30.7 7.9 %collective-permute-done.7.ahead_two_hbm = bf16[768,128]{1,0:T(8,128)(2,1)S(1)} collective-permute-done((bf16[768,128]{1,0:T(8,128)(2,1)S(1)}, bf16[768,128]{1,0:T(8,128)(2,1)S(1)}, u32[]{:S(2)}, u32[]{:S(2)}) %collective-permute-start.7) | collective-permute-done | bytes 196640 | tf_op jit(solution)/shard_map/ppermute | solution.py:675
  41.5 14.3 %collective-permute-done.8 = bf16[2,1024,128]{2,1,0:T(8,128)(2,1)S(1)} collective-permute-done((bf16[2,1024,128]{2,1,0:T(8,128)(2,1)S(1)}, bf16[2,1024,128]{2,1,0:T(8,128)(2,1)S(1)}, u32[]{:S(2)}, u32[]{:S(2)}) %collective-permute-start.8) | collective-permute-done | bytes 524320 | tf_op jit(solution)/shard_map/ppermute | solution.py:675
  56.0 10.6 %collective-permute-start.10 = (bf16[2,1024,128]{2,1,0:T(8,128)(2,1)S(1)}, bf16[2,1024,128]{2,1,0:T(8,128)(2,1)S(1)}, u32[]{:S(2)}, u32[]{:S(2)}) collective-permute-start(bf16[2,1024,128]{2,1,0:T(8,128)(2,1)S(1)} %get-tuple-element.40), channel_id=1, source_target_pairs={{28,0},{29,1},{30,2},{31,3},{0,4},{1,5},{2,6},{3,7},{4,8},{5,9},{6... | collective-permute-start | bytes 1572872 | tf_op jit(solution)/shard_map/ppermute | solution.py:675
  66.7 4.9 %collective-permute-start.9 = (bf16[2,1024,128]{2,1,0:T(8,128)(2,1)S(1)}, bf16[2,1024,128]{2,1,0:T(8,128)(2,1)S(1)}, u32[]{:S(2)}, u32[]{:S(2)}) collective-permute-start(bf16[2,1024,128]{2,1,0:T(8,128)(2,1)S(1)} %get-tuple-element.36), channel_id=1, source_target_pairs={{4,0},{5,1},{6,2},{7,3},{8,4},{9,5},{10,6},{11,7},{12,8},{13,9},{1... | collective-permute-start | bytes 1572872 | tf_op jit(solution)/shard_map/ppermute | solution.py:675
  71.5 8.0 %collective-permute-done.10 = bf16[2,1024,128]{2,1,0:T(8,128)(2,1)S(1)} collective-permute-done((bf16[2,1024,128]{2,1,0:T(8,128)(2,1)S(1)}, bf16[2,1024,128]{2,1,0:T(8,128)(2,1)S(1)}, u32[]{:S(2)}, u32[]{:S(2)}) %collective-permute-start.10) | collective-permute-done | bytes 524320 | tf_op jit(solution)/shard_map/ppermute | solution.py:675
  82.2 5.0 %collective-permute-start.11 = (bf16[2,2,2,1024,128]{4,3,2,1,0:T(8,128)(2,1)}, bf16[2,2,2,1024,128]{4,3,2,1,0:T(8,128)(2,1)}, u32[]{:S(2)}, u32[]{:S(2)}) collective-permute-start(bf16[2,2,2,1024,128]{4,3,2,1,0:T(8,128)(2,1)} %pad_maximum_fusion.own_hbm), channel_id=1, source_target_pairs={{0,32},{32,0},{64,96},{96,64},{128,160},{160,128},{192,224},{224,1... | collective-permute-start | bytes 6291464 | tf_op jit(solution)/shard_map/ppermute | solution.py:697
  87.2 8.8 %kda_pairs.1 = (f32[32,64,64]{2,1,0:T(8,128)}, bf16[32,64,64]{2,1,0:T(8,128)(2,1)}, bf16[32,64,256]{2,1,0:T(8,128)(2,1)}, bf16[32,64,128]{2,1,0:T(8,128)(2,1)}, ...) custom-call(s32[1]{0:T(128)} %bitcast.place_ref, bf16[2048,128]{1,0:T(8,128)(2,1)} %bitcast.67, ...), custom_call_target="tpu_custom_call" | custom-call | flops 300000000 | bytes 12000000 | tf_op jit(solution)/shard_map/kda_pairs/pallas_call | solution.py:148
  97.4 5.0 %kda_invert.1.xmat = f32[32,64,64]{2,1,0:T(8,128)S(1)} custom-call(f32[32,64,64]{2,1,0:T(8,128)S(1)} %copy-done.5), custom_call_target="tpu_custom_call" | custom-call | flops 300000000 | bytes 12000000 | tf_op jit(solution)/shard_map/kda_invert/pallas_call | solution.py:227
  102.4 2.9 %kda_leave.1 = (bf16[2304,128]{1,0:T(8,128)(2,1)S(1)}, bf16[2048,128]{1,0:T(8,128)(2,1)S(1)}, bf16[32,128,128]{2,1,0:T(8,128)(2,1)S(1)}, bf16[32,64,256]{2,1,0:T(8,128)(2,1)S(1)}) custom-call(f32[32,64,64]{2,1,0:T(8,128)S(1)} %kda_invert.1.xmat, bf16[32,64,256]{2,1,0:T(8,128)(2,1)S(1)} %copy-done.2, bf16[32,64,128]{2,1,0:T(8,128)(2,1)S(1)} %copy-done.12, ...), custom_call_target="tpu_custom_call" | custom-call | flops 300000000 | bytes 8000000 | tf_op jit(solution)/shard_map/kda_leave/pallas_call | solution.py:277
  110.0 13.9 %collective-permute-done.3.in_second = bf16[2048,128]{1,0:T(8,128)(2,1)S(1)} collective-permute-done((bf16[2048,128]{1,0:T(8,128)(2,1)S(1)}, bf16[2048,128]{1,0:T(8,128)(2,1)S(1)}, u32[]{:S(2)}, u32[]{:S(2)}) %collective-permute-start.3) | collective-permute-done | bytes 524320 | tf_op jit(solution)/shard_map/ppermute | solution.py:635
  124.9 3.9 %kda_carry.1 = (bf16[2048,128]{1,0:T(8,128)(2,1)}, bf16[2048,128]{1,0:T(8,128)(2,1)}) custom-call(s32[1]{0:T(128)} %bitcast.place_ref, bf16[32,128,128]{2,1,0:T(8,128)(2,1)} %copy-done.4, bf16[2304,128]{1,0:T(8,128)(2,1)} %copy-done.7, bf16[2048,128]{1,0:T(8,128)(2,1)} %copy-done.10, bf16[2304,128]{1,0:T(8,128)(2,1)} %copy-done.15, bf16[2048,128]{1,0:T(8,128)(2,1)} %copy-done.18), custom_call_target="tpu_custom_call" | custom-call | flops 130000000 | bytes 5000000 | tf_op jit(solution)/shard_map/kda_carry/pallas_call | solution.py:337
  128.8 2.8 %collective-permute-start.4 = (bf16[2048,128]{1,0:T(8,128)(2,1)}, bf16[2048,128]{1,0:T(8,128)(2,1)S(1)}, u32[]{:S(2)}, u32[]{:S(2)}) collective-permute-start(bf16[2048,128]{1,0:T(8,128)(2,1)} %get-tuple-element.31.own_first), channel_id=1, source_target_pairs={{0,1},{1,2},{2,3},{3,4},{4,5},{5,6},{6,7},{7,8},{8,9},{9,10},{10,1... | collective-permute-start | bytes 1572872 | tf_op jit(solution)/shard_map/ppermute | solution.py:635
  132.9 3.5 %kda_local.1 = (f32[32,64,128]{2,1,0:T(8,128)}, bf16[32,64,128]{2,1,0:T(8,128)(2,1)}) custom-call(bf16[32,64,64]{2,1,0:T(8,128)(2,1)} %get-tuple-element.19.att, bf16[32,64,256]{2,1,0:T(8,128)(2,1)} %copy-done.3, bf16[32,64,128]{2,1,0:T(8,128)(2,1)} %get-tuple-element.25.carried_q), custom_call_target="tpu_custom_call" | custom-call | flops 70000000 | bytes 4000000 | tf_op jit(solution)/shard_map/kda_local/pallas_call | solution.py:305
  136.4 5.6 %collective-permute-done.4.in_first = bf16[2048,128]{1,0:T(8,128)(2,1)S(1)} collective-permute-done((bf16[2048,128]{1,0:T(8,128)(2,1)}, bf16[2048,128]{1,0:T(8,128)(2,1)S(1)}, u32[]{:S(2)}, u32[]{:S(2)}) %collective-permute-start.4) | collective-permute-done | bytes 524320 | tf_op jit(solution)/shard_map/ppermute | solution.py:635
  142.0 4.9 %collective-permute-done.5.in_second = bf16[2048,128]{1,0:T(8,128)(2,1)S(1)} collective-permute-done((bf16[2048,128]{1,0:T(8,128)(2,1)}, bf16[2048,128]{1,0:T(8,128)(2,1)S(1)}, u32[]{:S(2)}, u32[]{:S(2)}) %collective-permute-start.5) | collective-permute-done | bytes 524320 | tf_op jit(solution)/shard_map/ppermute | solution.py:635
  149.2 2.6 %kda_close.1 = (bf16[2048,128]{1,0:T(8,128)(2,1)}, f32[32,128]{1,0:T(8,128)S(1)}) custom-call(s32[1]{0:T(128)} %bitcast.place_ref, f32[32,64,128]{2,1,0:T(8,128)S(1)} %copy-done.6, bf16[32,64,128]{2,1,0:T(8,128)(2,1)S(1)} %copy-done.11, bf16[2048,128]{1,0:T(8,128)(2,1)S(1)} %copy-done.9, bf16[2048,128]{1,0:T(8,128)(2,1)S(1)} %collective-permute-done.4.in_first, ...), custom_call_target="tpu_custom_call" | custom-call | flops 70000000 | bytes 5000000 | tf_op jit(solution)/shard_map/kda_close/pallas_call | solution.py:393
  151.8 21.3 %all_to_all.15 = f32[32,1,128]{2,1,0:T(1,128)S(1)} all-to-all(f32[32,1,128]{2,1,0:T(1,128)S(1)} %bitcast.52), channel_id=1, replica_groups=mesh['dp'=16,'ctx'=32] {'ctx'}, dimensions={0} | all-to-all | bytes 32768 | tf_op jit(solution)/shard_map/all_to_all | solution.py:732
  173.8 10.5 %all-to-all-start.1 = ((f32[16,1,128]{2,1,0:T(1,128)}), f32[16,1,128]{2,1,0:T(1,128)S(1)}, u32[]{:S(2)}, u32[]{:S(2)}) async-start(f32[16,1,128]{2,1,0:T(1,128)} %broadcast_in_dim.3), calls=%async_computation.1 | async-start | bytes 16384 | tf_op jit(solution)/shard_map/all_to_all | solution.py:734
  184.9 6.3 %all-to-all-done.1 = f32[16,1,128]{2,1,0:T(1,128)S(1)} async-done(((f32[16,1,128]{2,1,0:T(1,128)}), f32[16,1,128]{2,1,0:T(1,128)S(1)}, u32[]{:S(2)}, u32[]{:S(2)}) %all-to-all-start.1) | async-done | bytes 8224 | tf_op jit(solution)/shard_map/all_to_all | solution.py:734
  191.8 6.2 %mla_lift.1.lifted = bf16[2,1024,512]{2,1,0:T(8,128)(2,1)} custom-call(s32[2]{0:T(128)} %pad_add_fusion.spot_ref, bf16[2048,128]{1,0:T(8,128)(2,1)} %bitcast.72, bf16[2,2,2,1024,128]{4,3,2,1,0:T(8,128)(2,1)} %pad_maximum_fusion.own_hbm, bf16[2,2,2,1024,128]{4,3,2,1,0:T(8,128)(2,1)} %collective-permute-done.11.other_hbm), custom_call_target="tpu_custom_call" | custom-call | flops 400000000 | bytes 5000000 | tf_op jit(solution)/shard_map/mla_lift/pallas_call | solution.py:461
  198.0 11.7 %mla_mix.1 = bf16[2048,128]{1,0:T(8,128)(2,1)} custom-call(s32[2]{0:T(128)} %pad_add_fusion.spot_ref, bf16[2,1024,512]{2,1,0:T(8,128)(2,1)} %mla_lift.1.lifted, bf16[128,512]{1,0:T(8,128)(2,1)} %bitcast.58, bf16[768,128]{1,0:T(8,128)(2,1)} %copy-done.1, bf16[1024,128]{1,0:T(8,128)(2,1)} %copy-done.16, bf16[2304,128]{1,0:T(8,128)(2,1)} %copy-done.15, ...), custom_call_target="tpu_custom_call" | custom-call | flops 1100000000 | bytes 6000000 | tf_op jit(solution)/shard_map/mla_mix/pallas_call | solution.py:607
  (82 shorter events, 23.4 us)
Async XLA Ops:
  2.3 13.2 %collective-permute-start = (bf16[256,128]{1,0:T(8,128)(2,1)S(1)}, bf16[256,128]{1,0:T(8,128)(2,1)S(1)}, u32[]{:S(2)}, u32[]{:S(2)}) collective-permute-start(bf16[256,128]{1,0:T(8,128)(2,1)S(1)} %pad_maximum_fusion.6), channel_id=1, source_target_pairs={{16,0},{17,1},{18,2},{19,3},{20,4},{21,5},{22,6},{23,7},{24,8},{25... | collective-permute-start | bytes 196616 | tf_op jit(solution)/shard_map/ppermute | solution.py:675
  15.6 15.0 %collective-permute-start.6 = (bf16[1024,128]{1,0:T(8,128)(2,1)S(1)}, bf16[1024,128]{1,0:T(8,128)(2,1)S(1)}, u32[]{:S(2)}, u32[]{:S(2)}) collective-permute-start(bf16[1024,128]{1,0:T(8,128)(2,1)S(1)} %get-tuple-element.53), channel_id=1, source_target_pairs={{1,0},{2,1},{3,2},{4,3},{5,4},{6,5},{7,6},{8,7},{9,8},{10,9},{11,1... | collective-permute-start | bytes 786440 | tf_op jit(solution)/shard_map/ppermute | solution.py:675
  25.1 13.5 %collective-permute-start.1 = (bf16[768,128]{1,0:T(8,128)(2,1)S(1)}, bf16[768,128]{1,0:T(8,128)(2,1)S(1)}, u32[]{:S(2)}, u32[]{:S(2)}) collective-permute-start(bf16[768,128]{1,0:T(8,128)(2,1)S(1)} %get-tuple-element.56), channel_id=1, source_target_pairs={{31,0},{0,1},{1,2},{2,3},{3,4},{4,5},{5,6},{6,7},{7,8},{8,9},{9,10... | collective-permute-start | bytes 589832 | tf_op jit(solution)/shard_map/ppermute | solution.py:675
  27.0 11.6 %collective-permute-start.7 = (bf16[768,128]{1,0:T(8,128)(2,1)S(1)}, bf16[768,128]{1,0:T(8,128)(2,1)S(1)}, u32[]{:S(2)}, u32[]{:S(2)}) collective-permute-start(bf16[768,128]{1,0:T(8,128)(2,1)S(1)} %get-tuple-element.54), channel_id=1, source_target_pairs={{2,0},{3,1},{4,2},{5,3},{6,4},{7,5},{8,6},{9,7},{10,8},{11,9},{12,... | collective-permute-start | bytes 589832 | tf_op jit(solution)/shard_map/ppermute | solution.py:675
  30.6 25.3 %copy-start.16 = (bf16[1024,128]{1,0:T(8,128)(2,1)}, bf16[1024,128]{1,0:T(8,128)(2,1)S(1)}, u32[]{:S(2)}) copy-start(bf16[1024,128]{1,0:T(8,128)(2,1)S(1)} %collective-permute-done.6.ahead_one_hbm) | copy-start | bytes 786436
  38.5 17.5 %copy-start.17 = (bf16[768,128]{1,0:T(8,128)(2,1)}, bf16[768,128]{1,0:T(8,128)(2,1)S(1)}, u32[]{:S(2)}) copy-start(bf16[768,128]{1,0:T(8,128)(2,1)S(1)} %collective-permute-done.7.ahead_two_hbm) | copy-start | bytes 589828
  38.6 63.8 %copy-start.1 = (bf16[768,128]{1,0:T(8,128)(2,1)}, bf16[768,128]{1,0:T(8,128)(2,1)S(1)}, u32[]{:S(2)}) copy-start(bf16[768,128]{1,0:T(8,128)(2,1)S(1)} %collective-permute-done.1.behind.back_one_hbm) | copy-start | bytes 589828
  39.0 16.9 %collective-permute-start.8 = (bf16[2,1024,128]{2,1,0:T(8,128)(2,1)S(1)}, bf16[2,1024,128]{2,1,0:T(8,128)(2,1)S(1)}, u32[]{:S(2)}, u32[]{:S(2)}) collective-permute-start(bf16[2,1024,128]{2,1,0:T(8,128)(2,1)S(1)} %pad_maximum_fusion.1), channel_id=1, source_target_pairs={{8,0},{9,1},{10,2},{11,3},{12,4},{13,5},{14,6},{15,7},{16,8},{17,9... | collective-permute-start | bytes 1572872 | tf_op jit(solution)/shard_map/ppermute | solution.py:675
  56.0 23.5 %collective-permute-start.10 = (bf16[2,1024,128]{2,1,0:T(8,128)(2,1)S(1)}, bf16[2,1024,128]{2,1,0:T(8,128)(2,1)S(1)}, u32[]{:S(2)}, u32[]{:S(2)}) collective-permute-start(bf16[2,1024,128]{2,1,0:T(8,128)(2,1)S(1)} %get-tuple-element.40), channel_id=1, source_target_pairs={{28,0},{29,1},{30,2},{31,3},{0,4},{1,5},{2,6},{3,7},{4,8},{5,9},{6... | collective-permute-start | bytes 1572872 | tf_op jit(solution)/shard_map/ppermute | solution.py:675
  66.7 13.9 %collective-permute-start.9 = (bf16[2,1024,128]{2,1,0:T(8,128)(2,1)S(1)}, bf16[2,1024,128]{2,1,0:T(8,128)(2,1)S(1)}, u32[]{:S(2)}, u32[]{:S(2)}) collective-permute-start(bf16[2,1024,128]{2,1,0:T(8,128)(2,1)S(1)} %get-tuple-element.36), channel_id=1, source_target_pairs={{4,0},{5,1},{6,2},{7,3},{8,4},{9,5},{10,6},{11,7},{12,8},{13,9},{1... | collective-permute-start | bytes 1572872 | tf_op jit(solution)/shard_map/ppermute | solution.py:675
  82.2 109.6 %collective-permute-start.11 = (bf16[2,2,2,1024,128]{4,3,2,1,0:T(8,128)(2,1)}, bf16[2,2,2,1024,128]{4,3,2,1,0:T(8,128)(2,1)}, u32[]{:S(2)}, u32[]{:S(2)}) collective-permute-start(bf16[2,2,2,1024,128]{4,3,2,1,0:T(8,128)(2,1)} %pad_maximum_fusion.own_hbm), channel_id=1, source_target_pairs={{0,32},{32,0},{64,96},{96,64},{128,160},{160,128},{192,224},{224,1... | collective-permute-start | bytes 6291464 | tf_op jit(solution)/shard_map/ppermute | solution.py:697
  96.0 6.4 %copy-start.2 = (bf16[32,64,256]{2,1,0:T(8,128)(2,1)S(1)}, bf16[32,64,256]{2,1,0:T(8,128)(2,1)}, u32[]{:S(2)}) copy-start(bf16[32,64,256]{2,1,0:T(8,128)(2,1)} %get-tuple-element.21.rhs) | copy-start | bytes 3145732
  97.4 5.1 %copy-start.12 = (bf16[32,64,128]{2,1,0:T(8,128)(2,1)S(1)}, bf16[32,64,128]{2,1,0:T(8,128)(2,1)}, u32[]{:S(2)}) copy-start(bf16[32,64,128]{2,1,0:T(8,128)(2,1)} %get-tuple-element.22.leaving) | copy-start | bytes 1572868
  97.4 5.1 %copy-start.13 = (f32[32,8,128]{2,1,0:T(8,128)S(1)}, f32[32,8,128]{2,1,0:T(8,128)}, u32[]{:S(2)}) copy-start(f32[32,8,128]{2,1,0:T(8,128)} %get-tuple-element.23.closing) | copy-start | bytes 393220
  107.3 16.5 %copy-start.7 = (bf16[2304,128]{1,0:T(8,128)(2,1)}, bf16[2304,128]{1,0:T(8,128)(2,1)S(1)}, u32[]{:S(2)}) copy-start(bf16[2304,128]{1,0:T(8,128)(2,1)S(1)} %get-tuple-element.29.offs_first) | copy-start | bytes 1769476
  107.3 16.5 %copy-start.10 = (bf16[2048,128]{1,0:T(8,128)(2,1)}, bf16[2048,128]{1,0:T(8,128)(2,1)S(1)}, u32[]{:S(2)}) copy-start(bf16[2048,128]{1,0:T(8,128)(2,1)S(1)} %get-tuple-element.30.offs_second) | copy-start | bytes 1572868
  107.4 16.5 %collective-permute-start.2 = (bf16[2304,128]{1,0:T(8,128)(2,1)S(1)}, bf16[2304,128]{1,0:T(8,128)(2,1)S(1)}, u32[]{:S(2)}, u32[]{:S(2)}) collective-permute-start(bf16[2304,128]{1,0:T(8,128)(2,1)S(1)} %get-tuple-element.29.offs_first), channel_id=1, source_target_pairs={{0,1},{1,2},{2,3},{3,4},{4,5},{5,6},{6,7},{7,8},{8,9},{9,10},{10,1... | collective-permute-start | bytes 1769480 | tf_op jit(solution)/shard_map/ppermute | solution.py:635
  108.7 15.2 %collective-permute-start.3 = (bf16[2048,128]{1,0:T(8,128)(2,1)S(1)}, bf16[2048,128]{1,0:T(8,128)(2,1)S(1)}, u32[]{:S(2)}, u32[]{:S(2)}) collective-permute-start(bf16[2048,128]{1,0:T(8,128)(2,1)S(1)} %get-tuple-element.30.offs_second), channel_id=1, source_target_pairs={{1,0},{2,1},{3,2},{4,3},{5,4},{6,5},{7,6},{8,7},{9,8},{10,9},{11,1... | collective-permute-start | bytes 1572872 | tf_op jit(solution)/shard_map/ppermute | solution.py:635
  124.9 22.0 %copy-start.8 = (bf16[1,128,16,128]{3,2,1,0:T(8,128)(2,1)S(1)}, bf16[1,128,16,128]{3,2,1,0:T(8,128)(2,1)}, u32[]{:S(2)}) copy-start(bf16[1,128,16,128]{3,2,1,0:T(8,128)(2,1)} %param.23) | copy-start | bytes 1572868
  124.9 22.0 %copy-start.14 = (f32[128]{0:T(128)S(1)}, f32[128]{0:T(128)}, u32[]{:S(2)}) copy-start(f32[128]{0:T(128)} %param.22) | copy-start | bytes 1540
  128.8 18.1 %copy-start.9 = (bf16[2048,128]{1,0:T(8,128)(2,1)S(1)}, bf16[2048,128]{1,0:T(8,128)(2,1)}, u32[]{:S(2)}) copy-start(bf16[2048,128]{1,0:T(8,128)(2,1)} %get-tuple-element.31.own_first) | copy-start | bytes 1572868
  128.8 13.2 %collective-permute-start.4 = (bf16[2048,128]{1,0:T(8,128)(2,1)}, bf16[2048,128]{1,0:T(8,128)(2,1)S(1)}, u32[]{:S(2)}, u32[]{:S(2)}) collective-permute-start(bf16[2048,128]{1,0:T(8,128)(2,1)} %get-tuple-element.31.own_first), channel_id=1, source_target_pairs={{0,1},{1,2},{2,3},{3,4},{4,5},{5,6},{6,7},{7,8},{8,9},{9,10},{10,1... | collective-permute-start | bytes 1572872 | tf_op jit(solution)/shard_map/ppermute | solution.py:635
  131.6 15.3 %collective-permute-start.5 = (bf16[2048,128]{1,0:T(8,128)(2,1)}, bf16[2048,128]{1,0:T(8,128)(2,1)S(1)}, u32[]{:S(2)}, u32[]{:S(2)}) collective-permute-start(bf16[2048,128]{1,0:T(8,128)(2,1)} %get-tuple-element.32), channel_id=1, source_target_pairs={{1,0},{2,1},{3,2},{4,3},{5,4},{6,5},{7,6},{8,7},{9,8},{10,9},{11,1... | collective-permute-start | bytes 1572872 | tf_op jit(solution)/shard_map/ppermute | solution.py:635
  173.8 17.5 %all-to-all-start.1 = ((f32[16,1,128]{2,1,0:T(1,128)}), f32[16,1,128]{2,1,0:T(1,128)S(1)}, u32[]{:S(2)}, u32[]{:S(2)}) async-start(f32[16,1,128]{2,1,0:T(1,128)} %broadcast_in_dim.3), calls=%async_computation.1 | async-start | bytes 16384 | tf_op jit(solution)/shard_map/all_to_all | solution.py:734
  (8 other events, 8.2 us)
